TPU v7x, 128 devices: a whole 4x4x4 slice. The times are simulated.
128 devices in a mesh: gx: 16 (over z, y), gy: 8 (over x, core).
Axes of the slice: x: 4, y: 4, z: 4, core: 2. Of those that a mesh axis runs over, the one named last changes fastest.
Arguments:
- features: bfloat16 [16, 8, 64, 2048], P('gx', 'gy'), may hold values from -6 to 6
- counts: int32 [16, 8], P('gx', 'gy'), may hold values from 1 to 4, as said below
- sub_rows: int32 [16, 8, 27, 2048], P('gx', 'gy'), may hold values from 0 to 2047, as said below
- sub_from: int32 [16, 8, 27, 2048], P('gx', 'gy'), may hold values from 0 to 9, as said below
- down_map: int32 [16, 8, 2, 2048], P('gx', 'gy'), may hold values from 0 to 1088, as said below
- w_sub: bfloat16 [27, 64, 64], replicated, may hold values from -0.15625 to 0.15625
- w_down: bfloat16 [8, 64, 64], replicated, may hold values from -0.75 to 0.75
- cotangent: bfloat16 [16, 8, 64, 512], P('gx', 'gy'), may hold values from -6 to 6
Outputs:
- coarse_out: bfloat16 [16, 8, 64, 512], P('gx', 'gy')
- grad_features: bfloat16 [16, 8, 64, 2048], P('gx', 'gy')
- grad_w_sub: float32 [27, 64, 64], replicated
- grad_w_down: float32 [8, 64, 64], replicated
Inputs may be any that keep to these rules, and one draw needn't show every extreme that they name: Active voxel blocks of a tile; the first 512 * counts rows of a tile are live, the others padded. `sub_from`: offset k stands for the step (k // 9 - 1, k // 3 % 3 - 1, k % 3 - 1). Value d < 9 names the tile d // 3 - 1 steps along gx and d % 3 - 1 along gy, which exists; d is 4 (the same tile) or 3 * (k // 9) + k // 3 % 3, and differs from 4 only for output rows below 512. 9 means no source. Padded rows have no source; a live row is its own source at offset 13. `sub_rows`: the source voxel's row in the tile named by sub_from: where that tile is the same one, a row of the same block of 512 rows as the output row; where it is another one, a row below 512; 0 where there is no source. `down_map`: row 0: below 512 a coarse row of the same tile, and then for the fine row r one of the coarse rows (r // 512) * 128 to (r // 512 + 1) * 128 - 1; 512 + d * 64 + j (d not 4, j below 64) coarse row j of the tile d // 3 - 1 steps along gx and d % 3 - 1 along gy, which exists, used only by fine rows below 512; 1088 exactly on padded rows. Row 1: the kernel offset of the stride-2 convolution, 0 on padded rows.
All inputs are finite; a program needn't handle non-finite values.
Results may differ from a plain program's by a relative error of at most 0.0052.
Values may be sent and summed in bfloat16 or wider, within the bound.
No kernel may reach another device: no remote copies, remote signals or barrier semaphores. Data moves between devices by JAX's collectives and lax.ppermute only.
A program may use at most 64 MiB of HBM per device.

v0:
```python
import jax
import jax.numpy as jnp
from jax import lax
from jax.sharding import PartitionSpec as P

VB = 512
ROWS = 2048
BND = 512
CROWS = 512
CB = 64


def shifted(block, axis, distance):
    devices = range(lax.axis_size(axis))
    route = [(i - distance, i) for i in devices if i - distance in devices]
    return lax.ppermute(block, axis, route)


def with_halo(cells, sides, width):
    for axis, dim in sides:
        count = lax.axis_size(axis)
        ends = count - 1
        head = lax.slice_in_dim(cells, 0, width, axis=dim)
        tail = lax.slice_in_dim(cells, cells.shape[dim] - width, cells.shape[dim], axis=dim)
        cells = jnp.concatenate(
            [
                lax.ppermute(tail, axis, [(i, (i + 1) % count) for i in range(ends)]),
                cells,
                lax.ppermute(head, axis, [((i + 1) % count, i) for i in range(ends)]),
            ],
            axis=dim,
        )
    return cells


def return_direct(slabs):
    total = slabs[:, 1, 1].astype(jnp.float32)
    for first in range(3):
        for second in range(3):
            if first == 1 and second == 1:
                continue
            piece = slabs[:, first, second]
            if first != 1:
                piece = shifted(piece, "gx", first - 1)
            if second != 1:
                piece = shifted(piece, "gy", second - 1)
            total = total + piece.astype(jnp.float32)
    return total


def shards(features, counts, sub_rows, sub_from, down_map, w_sub, w_down, cotangent):
    highest = lax.Precision.HIGHEST
    feat_tile = features[0, 0]
    grad_tile = cotangent[0, 0]
    chans = feat_tile.shape[0]
    coarse_blk = VB // 4
    border = jnp.concatenate([feat_tile[:, :BND], grad_tile[:, :CB]], axis=1)[:, None, None, :]
    extended = with_halo(border, (("gx", 1), ("gy", 2)), 1)
    extended = extended.reshape(chans, 9, BND + CB)
    offset_ids = jnp.arange(27, dtype=jnp.int32)
    direction_of = 3 * (offset_ids // 9) + offset_ids // 3 % 3
    dir_table = (direction_of[:, None] == jnp.arange(9, dtype=jnp.int32)[None, :]).astype(
        jnp.float32
    )
    halo_by_off = jnp.einsum(
        "cdi,kd->cki",
        extended[:, :, :BND],
        dir_table.astype(jnp.bfloat16),
        preferred_element_type=jnp.float32,
    ).astype(jnp.bfloat16)
    halo_grad = extended[:, :, BND:].reshape(chans, 9 * CB)
    w_sub_wide = w_sub.astype(jnp.float32)
    w_down_wide = w_down.astype(jnp.float32)
    live_total = counts[0, 0] * VB
    rows_map = sub_rows[0, 0]
    from_map = sub_from[0, 0]
    coarse_map = down_map[0, 0]
    kernel_ids = jnp.arange(8, dtype=jnp.int32)
    column_ids = jnp.arange(VB, dtype=jnp.int32)
    border_ids = jnp.arange(BND, dtype=jnp.int32)
    coarse_ids = jnp.arange(coarse_blk, dtype=jnp.int32)
    edge_ids = jnp.arange(9 * CB, dtype=jnp.int32)
    border_blocks = BND // VB

    def one_block(block, carry):
        coarse_acc, coarse_edge, feat_acc, halo_acc, grad_sub, grad_down = carry
        start = block * VB
        rows_blk = lax.dynamic_slice_in_dim(rows_map, start, VB, 1)
        from_blk = lax.dynamic_slice_in_dim(from_map, start, VB, 1)
        local_rel = jnp.where(from_blk == 4, rows_blk - start, -1)
        pick_local = (local_rel[:, None, :] == column_ids[None, :, None]).astype(jnp.bfloat16)
        remote_rel = jnp.where((from_blk != 4) & (from_blk != 9), rows_blk, -1)
        table_blk = lax.dynamic_slice_in_dim(feat_tile, start, VB, 1)
        mapping = lax.dynamic_slice_in_dim(coarse_map, start, VB, 1)
        target = mapping[0]
        local_t = jnp.where(target < CROWS, target - block * coarse_blk, -1)
        pick_coarse = (local_t[None, :] == coarse_ids[:, None]).astype(jnp.bfloat16)
        edge_t = target - CROWS
        on_border = block < border_blocks

        def pick_remote():
            return (remote_rel[:, None, :] == border_ids[None, :, None]).astype(jnp.bfloat16)

        def pick_edges():
            return (edge_t[None, :] == edge_ids[:, None]).astype(jnp.bfloat16)

        def remote_in():
            src = jnp.einsum(
                "cki,kis->cks", halo_by_off, pick_remote(), preferred_element_type=jnp.float32
            )
            upward = jnp.dot(halo_grad, pick_edges(), preferred_element_type=jnp.float32)
            return (src, upward)

        def remote_none():
            return (jnp.zeros((chans, 27, VB), jnp.float32), jnp.zeros((chans, VB), jnp.float32))

        src_remote, up_remote = lax.cond(on_border, remote_in, remote_none)
        source = (
            jnp.einsum("ci,kis->cks", table_blk, pick_local, preferred_element_type=jnp.float32)
            + src_remote
        ).astype(jnp.bfloat16)
        live_mask = (start + column_ids < live_total).astype(jnp.float32)
        pre_act = jnp.einsum("koc,cks->os", w_sub, source, preferred_element_type=jnp.float32)
        sigmoid_v = jax.nn.sigmoid(pre_act)
        hidden = (pre_act * sigmoid_v * live_mask).astype(jnp.bfloat16)
        chosen = (mapping[1][None, :] == kernel_ids[:, None])[:, None, :]
        picked_h = jnp.where(chosen, hidden[None], jnp.zeros((), jnp.bfloat16))
        summed_h = jnp.einsum(
            "kcs,qs->kcq", picked_h, pick_coarse, preferred_element_type=jnp.float32
        )
        coarse_part = jnp.einsum("koc,kcq->oq", w_down_wide, summed_h, precision=highest)
        old_coarse = lax.dynamic_slice_in_dim(coarse_acc, block * coarse_blk, coarse_blk, 1)
        coarse_acc = lax.dynamic_update_slice_in_dim(
            coarse_acc, old_coarse + coarse_part, block * coarse_blk, 1
        )
        grad_blk = lax.dynamic_slice_in_dim(grad_tile, block * coarse_blk, coarse_blk, 1)
        upstream = (
            jnp.dot(grad_blk, pick_coarse, preferred_element_type=jnp.float32) + up_remote
        ).astype(jnp.bfloat16)
        picked_g = jnp.where(chosen, upstream[None], jnp.zeros((), jnp.bfloat16))
        grad_hidden = jnp.einsum(
            "koc,kos->cs", w_down, picked_g, preferred_element_type=jnp.float32
        )
        grad_pre = (
            grad_hidden * sigmoid_v * (1.0 + pre_act * (1.0 - sigmoid_v)) * live_mask
        ).astype(jnp.bfloat16)
        grad_down = grad_down + jnp.einsum(
            "kos,cs->koc", picked_g, hidden, preferred_element_type=jnp.float32
        )
        grad_sub = grad_sub + jnp.einsum(
            "os,cks->koc", grad_pre, source, preferred_element_type=jnp.float32
        )
        gathered = jnp.einsum(
            "os,kis->koi", grad_pre, pick_local, preferred_element_type=jnp.float32
        )
        feat_part = jnp.einsum("koc,koi->ci", w_sub_wide, gathered, precision=highest)
        old_feat = lax.dynamic_slice_in_dim(feat_acc, start, VB, 1)
        feat_acc = lax.dynamic_update_slice_in_dim(feat_acc, old_feat + feat_part, start, 1)

        def remote_out():
            gathered_rem = jnp.einsum(
                "os,kis->koi", grad_pre, pick_remote(), preferred_element_type=jnp.float32
            )
            terms = jnp.einsum("koc,koi->kci", w_sub_wide, gathered_rem, precision=highest)
            halo_add = jnp.einsum("kci,kd->cdi", terms, dir_table, precision=highest)
            summed_e = jnp.einsum(
                "kcs,js->kcj", picked_h, pick_edges(), preferred_element_type=jnp.float32
            )
            edge_add = jnp.einsum("koc,kcj->oj", w_down_wide, summed_e, precision=highest)
            return (halo_add, edge_add)

        def remote_quiet():
            return (
                jnp.zeros((chans, 9, BND), jnp.float32),
                jnp.zeros((chans, 9 * CB), jnp.float32),
            )

        halo_add, edge_add = lax.cond(on_border, remote_out, remote_quiet)
        return (
            coarse_acc,
            coarse_edge + edge_add,
            feat_acc,
            halo_acc + halo_add,
            grad_sub,
            grad_down,
        )

    initial = (
        jnp.zeros((chans, CROWS), jnp.float32),
        jnp.zeros((chans, 9 * CB), jnp.float32),
        jnp.zeros((chans, ROWS), jnp.float32),
        jnp.zeros((chans, 9, BND), jnp.float32),
        jnp.zeros((27, chans, chans), jnp.float32),
        jnp.zeros((8, chans, chans), jnp.float32),
    )
    result = lax.fori_loop(0, ROWS // VB, one_block, initial)
    coarse_acc, coarse_edge, feat_acc, halo_acc, grad_sub, grad_down = result
    scale = float(ROWS * lax.axis_size("gx") * lax.axis_size("gy")) ** (-0.5)
    grad_w_sub, grad_w_down = lax.psum((grad_sub * scale, grad_down * scale), ("gx", "gy"))
    slabs = jnp.concatenate([halo_acc, coarse_edge.reshape(chans, 9, CB)], axis=2)
    slabs = slabs.reshape(chans, 3, 3, BND + CB).astype(jnp.bfloat16)
    incoming = return_direct(slabs)
    grad_local = feat_acc.at[:, :BND].add(incoming[:, :BND])
    live_rows = (jnp.arange(ROWS) < live_total).astype(jnp.float32)
    grad_features = (grad_local * live_rows).astype(jnp.bfloat16)
    coarse_out = coarse_acc.at[:, :CB].add(incoming[:, BND:]).astype(jnp.bfloat16)
    return (coarse_out[None, None], grad_features[None, None], grad_w_sub, grad_w_down)


def solution(mesh):
    return jax.shard_map(
        shards,
        mesh=mesh,
        in_specs=(
            P("gx", "gy", None, None),
            P("gx", "gy"),
            P("gx", "gy", None, None),
            P("gx", "gy", None, None),
            P("gx", "gy", None, None),
            P(),
            P(),
            P("gx", "gy", None, None),
        ),
        out_specs=(P("gx", "gy", None, None), P("gx", "gy", None, None), P(), P()),
        check_vma=False,
    )
```

profile of v0, /device:TPU:1, one launch (start us, length us, event | category | flops | bytes accessed | tf_op | source)
XLA Modules:
  0.0 417.9 jit_solution(14460559080024138564)
XLA Ops:
  8.8 4.0 collective-permute-start
  14.3 3.7 collective-permute-done.1
  18.1 5.1 %collective-permute-start.2 = (bf16[64,3,1,576]{3,0,2,1:T(8,128)(2,1)S(1)}, bf16[64,3,1,576]{3,0,2,1:T(8,128)(2,1)S(1)}, u32[]{:S(2)}, u32[]{:S(2)}) collective-permute-start(bf16[64,3,1,576]{3,0,2,1:T(8,128)(2,1)S(1)} %pad_maximum_fusion.1), channel_id=1, source_target_pairs={{0,1},{1,2},{2,3},{3,4},{4,5},{5,6},{6,7},{8,9},{9,10},{10,11},{11... | collective-permute-start | bytes 663560 | tf_op jit(solution)/shard_map/ppermute | solution.py:27
  38.7 177.0 %while.29 = (s32[]{:T(128)}, f32[64,512]{1,0:T(8,128)}, f32[64,576]{1,0:T(8,128)}, f32[64,2048]{1,0:T(8,128)}, f32[64,9,512]{2,1,0:T(8,128)}, /*index=5*/f32[27,...) while((s32[]{:T(128)}, f32[64,512]{1,0:T(8,128)}, ...), condition=%wide.region_5.6_spmd.clone.clone, body=%wide.region_0.5_spmd.clone.clone.sunk | while | flops 6097582592 | bytes 55294452 | solution.py:196
  65.5 7.2 %conditional.8 = (f32[64,27,512]{2,0,1:T(8,128)S(1)}, f32[64,512]{1,0:T(8,128)S(1)}) conditional(s32[]{:T(128)} %convert_element_type.208, () %tuple.105, (s32[27,512]{1,0:T(8,128)S(1)}, s32[512]{0:T(512)}, bf16[64,27,512]{2,0,1:T(8,128)(2,1)}, s32[512]{0:T(512)}, s32[576]{0:T(1024)}, /*index=5*/bf16[64,576]{1,0:T(8,128)(2,1)}) %tuple.106), branch_computations={%region_1.1_spmd, %region_2.2_spmd} | conditional | flops 951091200 | bytes 5574928 | solution.py:117
  65.5 5.9 %fusion.14 = f32[64,27,512]{2,0,1:T(8,128)S(1)} fusion(bf16[64,27,512]{2,0,1:T(8,128)(2,1)} %get-tuple-element.652, s32[27,512]{1,0:T(8,128)S(1)} %get-tuple-element.650, s32[512]{0:T(512)} %get-tuple-element.651), kind=kOutput, calls=%fused_computation.9 | convolution fusion | flops 913047552 | bytes 5365760 | tf_op jit(solution)/shard_map/while/body/eval_jaxpr/cond/branch_1_fun/cki,kis->cks/dot_general | solution.py:108
  72.7 6.7 %add_convert_fusion.2 = bf16[64,27,512]{2,0,1:T(8,128)(2,1)S(1)} fusion(f32[64,27,512]{2,0,1:T(8,128)S(1)} %get-tuple-element.1108, s32[27,512]{1,0:T(8,128)S(1)} %get-tuple-element.1109, bf16[64,2048]{1,0:T(8,128)(2,1)} %get-tuple-element.1183, s32[]{:T(128)S(6)} %select_n.159), kind=kOutput, calls=%fused_computation.38.clone.1 | convolution fusion | flops 914817024 | bytes 5429252 | tf_op jit(solution)/shard_map/while/body/eval_jaxpr/ci,kis->cks/dot_general | solution.py:119
  84.3 17.3 %conditional.9 = (f32[64,9,512]{2,1,0:T(8,128)S(1)}, f32[64,576]{1,0:T(8,128)S(1)}) conditional(s32[]{:T(128)} %convert_element_type.208, () %tuple.107, (s32[27,512]{1,0:T(8,128)S(1)}, s32[512]{0:T(512)}, bf16[64,512]{1,0:T(8,128)(2,1)S(1)}, f32[27,64,64]{1,2,0:T(8,128)S(1)}, f32[27,9]{0,1:T(8,128)S(1)}, /*index=5*/s32[512]{0:T(512)}, ...), branch_computations={%region_3.3_spmd, %region_4.4_spmd} | conditional | flops 2216853504 | bytes 19068124 | solution.py:178
  84.4 5.6 %fusion.24 = f32[27,512,64]{1,2,0:T(8,128)S(1)} fusion(s32[27,512]{1,0:T(8,128)S(1)} %get-tuple-element.656, s32[512]{0:T(512)} %get-tuple-element.657, bf16[64,512]{1,0:T(8,128)(2,1)S(1)} %get-tuple-element.658), kind=kOutput, calls=%fused_computation.15 | convolution fusion | flops 913047552 | bytes 3661824 | tf_op jit(solution)/shard_map/while/body/eval_jaxpr/cond/branch_1_fun/os,kis->koi/dot_general | solution.py:161
  90.0 3.3 convolution_bitcast_fusion
  93.3 6.1 %fusion.30 = f32[64,9,512]{2,1,0:T(8,128)S(1)} fusion(f32[27,64,512]{2,1,0:T(8,128)S(1)} %convolution_bitcast_fusion, f32[27,9]{0,1:T(8,128)S(1)} %get-tuple-element.660), kind=kOutput, calls=%fused_computation.22 | convolution fusion | flops 95551488 | bytes 4719564 | tf_op jit(solution)/shard_map/while/body/eval_jaxpr/cond/branch_1_fun/kci,kd->cdi/dot_general | solution.py:165
  103.6 5.2 %fusion.182 = f32[27,512,64]{1,2,0:T(8,128)S(1)} fusion(s32[27,512]{1,0:T(8,128)S(1)} %copy-done.8, bf16[64,512]{1,0:T(8,128)(2,1)S(1)} %fusion.180), kind=kOutput, calls=%fused_computation.32.clone.1 | convolution fusion | flops 913047552 | bytes 3659776 | tf_op jit(solution)/shard_map/while/body/eval_jaxpr/os,kis->koi/dot_general | solution.py:153
  108.8 4.1 fusion.183
  119.5 6.7 %add_convert_fusion.2 = bf16[64,27,512]{2,0,1:T(8,128)(2,1)S(1)} fusion(f32[64,27,512]{2,0,1:T(8,128)S(1)} %get-tuple-element.1108, s32[27,512]{1,0:T(8,128)S(1)} %get-tuple-element.1109, bf16[64,2048]{1,0:T(8,128)(2,1)} %get-tuple-element.1183, s32[]{:T(128)S(6)} %select_n.159), kind=kOutput, calls=%fused_computation.38.clone.1 | convolution fusion | flops 914817024 | bytes 5429252 | tf_op jit(solution)/shard_map/while/body/eval_jaxpr/ci,kis->cks/dot_general | solution.py:119
  132.6 3.5 select_add_fusion.5
  136.1 5.2 %fusion.182 = f32[27,512,64]{1,2,0:T(8,128)S(1)} fusion(s32[27,512]{1,0:T(8,128)S(1)} %copy-done.8, bf16[64,512]{1,0:T(8,128)(2,1)S(1)} %fusion.180), kind=kOutput, calls=%fused_computation.32.clone.1 | convolution fusion | flops 913047552 | bytes 3659776 | tf_op jit(solution)/shard_map/while/body/eval_jaxpr/os,kis->koi/dot_general | solution.py:153
  141.3 4.1 fusion.183
  152.0 6.7 %add_convert_fusion.2 = bf16[64,27,512]{2,0,1:T(8,128)(2,1)S(1)} fusion(f32[64,27,512]{2,0,1:T(8,128)S(1)} %get-tuple-element.1108, s32[27,512]{1,0:T(8,128)S(1)} %get-tuple-element.1109, bf16[64,2048]{1,0:T(8,128)(2,1)} %get-tuple-element.1183, s32[]{:T(128)S(6)} %select_n.159), kind=kOutput, calls=%fused_computation.38.clone.1 | convolution fusion | flops 914817024 | bytes 5429252 | tf_op jit(solution)/shard_map/while/body/eval_jaxpr/ci,kis->cks/dot_general | solution.py:119
  165.1 3.5 select_add_fusion.5
  168.6 5.2 %fusion.182 = f32[27,512,64]{1,2,0:T(8,128)S(1)} fusion(s32[27,512]{1,0:T(8,128)S(1)} %copy-done.8, bf16[64,512]{1,0:T(8,128)(2,1)S(1)} %fusion.180), kind=kOutput, calls=%fused_computation.32.clone.1 | convolution fusion | flops 913047552 | bytes 3659776 | tf_op jit(solution)/shard_map/while/body/eval_jaxpr/os,kis->koi/dot_general | solution.py:153
  173.8 4.1 fusion.183
  184.5 6.7 %add_convert_fusion.2 = bf16[64,27,512]{2,0,1:T(8,128)(2,1)S(1)} fusion(f32[64,27,512]{2,0,1:T(8,128)S(1)} %get-tuple-element.1108, s32[27,512]{1,0:T(8,128)S(1)} %get-tuple-element.1109, bf16[64,2048]{1,0:T(8,128)(2,1)} %get-tuple-element.1183, s32[]{:T(128)S(6)} %select_n.159), kind=kOutput, calls=%fused_computation.38.clone.1 | convolution fusion | flops 914817024 | bytes 5429252 | tf_op jit(solution)/shard_map/while/body/eval_jaxpr/ci,kis->cks/dot_general | solution.py:119
  197.6 3.5 select_add_fusion.5
  201.0 5.2 %fusion.182 = f32[27,512,64]{1,2,0:T(8,128)S(1)} fusion(s32[27,512]{1,0:T(8,128)S(1)} %copy-done.8, bf16[64,512]{1,0:T(8,128)(2,1)S(1)} %fusion.180), kind=kOutput, calls=%fused_computation.32.clone.1 | convolution fusion | flops 913047552 | bytes 3659776 | tf_op jit(solution)/shard_map/while/body/eval_jaxpr/os,kis->koi/dot_general | solution.py:153
  206.3 4.1 fusion.183
  219.0 4.0 collective-permute-start.11
  223.0 2.9 collective-permute-start.14
  228.9 4.2 %collective-permute-start.10 = (bf16[64,576]{1,0:T(8,128)(2,1)}, bf16[64,576]{1,0:T(8,128)(2,1)S(1)}, u32[]{:S(2)}, u32[]{:S(2)}) collective-permute-start(bf16[64,576]{1,0:T(8,128)(2,1)} %get-tuple-element.966), channel_id=1, source_target_pairs={{0,1},{1,2},{2,3},{3,4},{4,5},{5,6},{6,7},{8,9},{9,10},{10,11},{11... | collective-permute-start | bytes 221192 | tf_op jit(solution)/shard_map/ppermute | solution.py:16
  233.2 6.0 %collective-permute-start.13 = (bf16[64,576]{1,0:T(8,128)(2,1)S(1)}, bf16[64,576]{1,0:T(8,128)(2,1)S(1)}, u32[]{:S(2)}, u32[]{:S(2)}) collective-permute-start(bf16[64,576]{1,0:T(8,128)(2,1)S(1)} %get-tuple-element.969), channel_id=1, source_target_pairs={{0,8},{8,16},{16,24},{24,32},{32,40},{40,48},{48,56},{56,64},{64,7... | collective-permute-start | bytes 221192 | tf_op jit(solution)/shard_map/ppermute | solution.py:16
  245.3 3.6 collective-permute-start.15
  250.9 3.6 collective-permute-start.8
  259.3 147.6 %all-reduce.3.cloned.1.call-done = (f32[27,64,64]{2,1,0:T(8,128)}, f32[8,64,64]{2,1,0:T(8,128)}) async-done(((f32[27,64,64]{2,1,0:T(8,128)}, f32[8,64,64]{2,1,0:T(8,128)}), (f32[27,64,64]{2,1,0:T(8,128)}, f32[8,64,64]{2,1,0:T(8,128)})) %all-reduce.3.cloned.1.call-update) | async-done | bytes 573456 | tf_op jit(solution)/shard_map/psum | solution.py:199
  (267 shorter events, 97.5 us)
Async XLA Ops:
  7.2 399.8 %all-reduce.3.cloned.1.call-start = ((), (), s32[]{:S(2)}) async-start(), calls=%async_computation | async-start | bytes 2293760 | tf_op jit(solution)/shard_map/psum | solution.py:199
  8.8 5.5 %collective-permute-start = (bf16[64,1,1,576]{3,0,2,1:T(8,128)(2,1)S(1)}, bf16[64,1,1,576]{3,0,2,1:T(8,128)(2,1)S(1)}, u32[]{:S(2)}, u32[]{:S(2)}) collective-permute-start(bf16[64,1,1,576]{3,0,2,1:T(8,128)(2,1)S(1)} %maximum_bitcast_fusion), channel_id=1, source_target_pairs={{0,8},{8,16},{16,24},{24,32},{32,40},{40,48},{48,56},{56,64},{64,7... | collective-permute-start | bytes 221192 | tf_op jit(solution)/shard_map/ppermute | solution.py:27
  12.8 5.2 %collective-permute-start.1 = (bf16[64,1,1,576]{3,0,2,1:T(8,128)(2,1)S(1)}, bf16[64,1,1,576]{3,0,2,1:T(8,128)(2,1)S(1)}, u32[]{:S(2)}, u32[]{:S(2)}) collective-permute-start(bf16[64,1,1,576]{3,0,2,1:T(8,128)(2,1)S(1)} %maximum_bitcast_fusion), channel_id=1, source_target_pairs={{8,0},{16,8},{24,16},{32,24},{40,32},{48,40},{56,48},{64,56},{72,6... | collective-permute-start | bytes 221192 | tf_op jit(solution)/shard_map/ppermute | solution.py:29
  18.1 15.0 %collective-permute-start.2 = (bf16[64,3,1,576]{3,0,2,1:T(8,128)(2,1)S(1)}, bf16[64,3,1,576]{3,0,2,1:T(8,128)(2,1)S(1)}, u32[]{:S(2)}, u32[]{:S(2)}) collective-permute-start(bf16[64,3,1,576]{3,0,2,1:T(8,128)(2,1)S(1)} %pad_maximum_fusion.1), channel_id=1, source_target_pairs={{0,1},{1,2},{2,3},{3,4},{4,5},{5,6},{6,7},{8,9},{9,10},{10,11},{11... | collective-permute-start | bytes 663560 | tf_op jit(solution)/shard_map/ppermute | solution.py:27
  23.2 9.9 %collective-permute-start.3 = (bf16[64,3,1,576]{3,0,2,1:T(8,128)(2,1)S(1)}, bf16[64,3,1,576]{3,0,2,1:T(8,128)(2,1)S(1)}, u32[]{:S(2)}, u32[]{:S(2)}) collective-permute-start(bf16[64,3,1,576]{3,0,2,1:T(8,128)(2,1)S(1)} %pad_maximum_fusion.1), channel_id=1, source_target_pairs={{1,0},{2,1},{3,2},{4,3},{5,4},{6,5},{7,6},{9,8},{10,9},{11,10},{12... | collective-permute-start | bytes 663560 | tf_op jit(solution)/shard_map/ppermute | solution.py:29
  62.0 22.3 %copy-start.16 = (s32[27]{0:T(128)}, s32[27]{0:T(128)S(1)}, u32[]{:S(2)}) copy-start(s32[27]{0:T(128)S(1)} %get-tuple-element.1194) | copy-start | bytes 328 | tf_op jit(solution)/shard_map/while
  62.9 9.8 %copy-start.7 = (s32[27,512]{1,0:T(8,128)}, s32[27,512]{1,0:T(8,128)S(1)}, u32[]{:S(2)}) copy-start(s32[27,512]{1,0:T(8,128)S(1)} %get-tuple-element.1109) | copy-start | bytes 165892 | tf_op jit(solution)/shard_map/while
  72.7 6.7 %copy-start.12 = (bf16[27,64,64]{2,1,0:T(8,128)(2,1)S(1)}, bf16[27,64,64]{2,1,0:T(8,128)(2,1)}, u32[]{:S(2)}) copy-start(bf16[27,64,64]{2,1,0:T(8,128)(2,1)} %get-tuple-element.1188) | copy-start | bytes 663556 | tf_op jit(solution)/shard_map/while
  115.5 16.8 %copy-start.16 = (s32[27]{0:T(128)}, s32[27]{0:T(128)S(1)}, u32[]{:S(2)}) copy-start(s32[27]{0:T(128)S(1)} %get-tuple-element.1194) | copy-start | bytes 328 | tf_op jit(solution)/shard_map/while
  119.5 6.7 %copy-start.12 = (bf16[27,64,64]{2,1,0:T(8,128)(2,1)S(1)}, bf16[27,64,64]{2,1,0:T(8,128)(2,1)}, u32[]{:S(2)}) copy-start(bf16[27,64,64]{2,1,0:T(8,128)(2,1)} %get-tuple-element.1188) | copy-start | bytes 663556 | tf_op jit(solution)/shard_map/while
  141.3 6.7 %copy-start.11 = (s32[27,2048]{1,0:T(8,128)S(1)}, s32[27,2048]{1,0:T(8,128)}, u32[]{:S(2)}) copy-start(s32[27,2048]{1,0:T(8,128)} %copy-done.10) | copy-start | bytes 663556 | tf_op jit(solution)/shard_map/while
  141.3 6.7 %copy-start.17 = (s32[27]{0:T(128)S(1)}, s32[27]{0:T(128)}, u32[]{:S(2)}) copy-start(s32[27]{0:T(128)} %copy-done.16) | copy-start | bytes 328 | tf_op jit(solution)/shard_map/while
  148.0 16.8 %copy-start.16 = (s32[27]{0:T(128)}, s32[27]{0:T(128)S(1)}, u32[]{:S(2)}) copy-start(s32[27]{0:T(128)S(1)} %get-tuple-element.1194) | copy-start | bytes 328 | tf_op jit(solution)/shard_map/while
  152.0 6.7 %copy-start.12 = (bf16[27,64,64]{2,1,0:T(8,128)(2,1)S(1)}, bf16[27,64,64]{2,1,0:T(8,128)(2,1)}, u32[]{:S(2)}) copy-start(bf16[27,64,64]{2,1,0:T(8,128)(2,1)} %get-tuple-element.1188) | copy-start | bytes 663556 | tf_op jit(solution)/shard_map/while
  180.4 16.8 %copy-start.16 = (s32[27]{0:T(128)}, s32[27]{0:T(128)S(1)}, u32[]{:S(2)}) copy-start(s32[27]{0:T(128)S(1)} %get-tuple-element.1194) | copy-start | bytes 328 | tf_op jit(solution)/shard_map/while
  184.4 6.7 %copy-start.12 = (bf16[27,64,64]{2,1,0:T(8,128)(2,1)S(1)}, bf16[27,64,64]{2,1,0:T(8,128)(2,1)}, u32[]{:S(2)}) copy-start(bf16[27,64,64]{2,1,0:T(8,128)(2,1)} %get-tuple-element.1188) | copy-start | bytes 663556 | tf_op jit(solution)/shard_map/while
  215.7 10.2 %copy-start = (f32[27,64,64]{1,2,0:T(8,128)S(1)}, f32[27,64,64]{1,2,0:T(8,128)}, u32[]{:S(2)}) copy-start(f32[27,64,64]{1,2,0:T(8,128)} %get-tuple-element.712) | copy-start | bytes 1327108
  217.6 37.0 %copy-start.15 = (f32[8,64,64]{2,1,0:T(8,128)S(1)}, f32[8,64,64]{2,1,0:T(8,128)}, u32[]{:S(2)}) copy-start(f32[8,64,64]{2,1,0:T(8,128)} %get-tuple-element.713) | copy-start | bytes 393220
  219.0 37.1 %copy-start.1 = (f32[64,2048]{1,0:T(8,128)S(1)}, f32[64,2048]{1,0:T(8,128)}, u32[]{:S(2)}) copy-start(f32[64,2048]{1,0:T(8,128)} %get-tuple-element.711) | copy-start | bytes 1572868
  219.0 14.1 %collective-permute-start.11 = (bf16[64,576]{1,0:T(8,128)(2,1)}, bf16[64,576]{1,0:T(8,128)(2,1)}, u32[]{:S(2)}, u32[]{:S(2)}) collective-permute-start(bf16[64,576]{1,0:T(8,128)(2,1)} %get-tuple-element.967), channel_id=1, source_target_pairs={{0,8},{8,16},{16,24},{24,32},{32,40},{40,48},{48,56},{56,64},{64,7... | collective-permute-start | bytes 221192 | tf_op jit(solution)/shard_map/ppermute | solution.py:16
  223.0 16.2 %collective-permute-start.14 = (bf16[64,576]{1,0:T(8,128)(2,1)}, bf16[64,576]{1,0:T(8,128)(2,1)}, u32[]{:S(2)}, u32[]{:S(2)}) collective-permute-start(bf16[64,576]{1,0:T(8,128)(2,1)} %get-tuple-element.968), channel_id=1, source_target_pairs={{0,8},{8,16},{16,24},{24,32},{32,40},{40,48},{48,56},{56,64},{64,7... | collective-permute-start | bytes 221192 | tf_op jit(solution)/shard_map/ppermute | solution.py:16
  226.2 31.3 %copy-start.9 = (f32[64,512]{1,0:T(8,128)S(1)}, f32[64,512]{1,0:T(8,128)}, u32[]{:S(2)}) copy-start(f32[64,512]{1,0:T(8,128)} %get-tuple-element.708) | copy-start | bytes 393220
  226.2 15.2 %collective-permute-start.4 = (bf16[64,576]{1,0:T(8,128)(2,1)}, bf16[64,576]{1,0:T(8,128)(2,1)S(1)}, u32[]{:S(2)}, u32[]{:S(2)}) collective-permute-start(bf16[64,576]{1,0:T(8,128)(2,1)} %get-tuple-element.962), channel_id=1, source_target_pairs={{8,0},{16,8},{24,16},{32,24},{40,32},{48,40},{56,48},{64,56},{72,6... | collective-permute-start | bytes 221192 | tf_op jit(solution)/shard_map/ppermute | solution.py:16
  227.6 15.7 %collective-permute-start.7 = (bf16[64,576]{1,0:T(8,128)(2,1)}, bf16[64,576]{1,0:T(8,128)(2,1)S(1)}, u32[]{:S(2)}, u32[]{:S(2)}) collective-permute-start(bf16[64,576]{1,0:T(8,128)(2,1)} %get-tuple-element.964), channel_id=1, source_target_pairs={{8,0},{16,8},{24,16},{32,24},{40,32},{48,40},{56,48},{64,56},{72,6... | collective-permute-start | bytes 221192 | tf_op jit(solution)/shard_map/ppermute | solution.py:16
  228.9 16.4 %collective-permute-start.10 = (bf16[64,576]{1,0:T(8,128)(2,1)}, bf16[64,576]{1,0:T(8,128)(2,1)S(1)}, u32[]{:S(2)}, u32[]{:S(2)}) collective-permute-start(bf16[64,576]{1,0:T(8,128)(2,1)} %get-tuple-element.966), channel_id=1, source_target_pairs={{0,1},{1,2},{2,3},{3,4},{4,5},{5,6},{6,7},{8,9},{9,10},{10,11},{11... | collective-permute-start | bytes 221192 | tf_op jit(solution)/shard_map/ppermute | solution.py:16
  233.2 15.8 %collective-permute-start.13 = (bf16[64,576]{1,0:T(8,128)(2,1)S(1)}, bf16[64,576]{1,0:T(8,128)(2,1)S(1)}, u32[]{:S(2)}, u32[]{:S(2)}) collective-permute-start(bf16[64,576]{1,0:T(8,128)(2,1)S(1)} %get-tuple-element.969), channel_id=1, source_target_pairs={{0,8},{8,16},{16,24},{24,32},{32,40},{40,48},{48,56},{56,64},{64,7... | collective-permute-start | bytes 221192 | tf_op jit(solution)/shard_map/ppermute | solution.py:16
  239.2 11.7 %collective-permute-start.6 = (bf16[64,576]{1,0:T(8,128)(2,1)S(1)}, bf16[64,576]{1,0:T(8,128)(2,1)S(1)}, u32[]{:S(2)}, u32[]{:S(2)}) collective-permute-start(bf16[64,576]{1,0:T(8,128)(2,1)S(1)} %get-tuple-element.963), channel_id=1, source_target_pairs={{8,0},{16,8},{24,16},{32,24},{40,32},{48,40},{56,48},{64,56},{72,6... | collective-permute-start | bytes 221192 | tf_op jit(solution)/shard_map/ppermute | solution.py:16
  241.4 13.9 %collective-permute-start.9 = (bf16[64,576]{1,0:T(8,128)(2,1)S(1)}, bf16[64,576]{1,0:T(8,128)(2,1)S(1)}, u32[]{:S(2)}, u32[]{:S(2)}) collective-permute-start(bf16[64,576]{1,0:T(8,128)(2,1)S(1)} %get-tuple-element.965), channel_id=1, source_target_pairs={{1,0},{2,1},{3,2},{4,3},{5,4},{6,5},{7,6},{9,8},{10,9},{11,10},{12... | collective-permute-start | bytes 221192 | tf_op jit(solution)/shard_map/ppermute | solution.py:16
  243.4 12.0 %collective-permute-start.12 = (bf16[64,576]{1,0:T(8,128)(2,1)}, bf16[64,576]{1,0:T(8,128)(2,1)S(1)}, u32[]{:S(2)}, u32[]{:S(2)}) collective-permute-start(bf16[64,576]{1,0:T(8,128)(2,1)} %collective-permute-done.11), channel_id=1, source_target_pairs={{1,0},{2,1},{3,2},{4,3},{5,4},{6,5},{7,6},{9,8},{10,9},{11,10},{12... | collective-permute-start | bytes 221192 | tf_op jit(solution)/shard_map/ppermute | solution.py:16
  245.3 10.0 %collective-permute-start.15 = (bf16[64,576]{1,0:T(8,128)(2,1)}, bf16[64,576]{1,0:T(8,128)(2,1)S(1)}, u32[]{:S(2)}, u32[]{:S(2)}) collective-permute-start(bf16[64,576]{1,0:T(8,128)(2,1)} %collective-permute-done.14), channel_id=1, source_target_pairs={{0,1},{1,2},{2,3},{3,4},{4,5},{5,6},{6,7},{8,9},{9,10},{10,11},{11... | collective-permute-start | bytes 221192 | tf_op jit(solution)/shard_map/ppermute | solution.py:16
  249.0 6.4 %collective-permute-start.5 = (bf16[64,576]{1,0:T(8,128)(2,1)S(1)}, bf16[64,576]{1,0:T(8,128)(2,1)S(1)}, u32[]{:S(2)}, u32[]{:S(2)}) collective-permute-start(bf16[64,576]{1,0:T(8,128)(2,1)S(1)} %collective-permute-done.4), channel_id=1, source_target_pairs={{1,0},{2,1},{3,2},{4,3},{5,4},{6,5},{7,6},{9,8},{10,9},{11,10},{12... | collective-permute-start | bytes 221192 | tf_op jit(solution)/shard_map/ppermute | solution.py:16
  250.9 5.1 %collective-permute-start.8 = (bf16[64,576]{1,0:T(8,128)(2,1)S(1)}, bf16[64,576]{1,0:T(8,128)(2,1)S(1)}, u32[]{:S(2)}, u32[]{:S(2)}) collective-permute-start(bf16[64,576]{1,0:T(8,128)(2,1)S(1)} %collective-permute-done.7), channel_id=1, source_target_pairs={{0,1},{1,2},{2,3},{3,4},{4,5},{5,6},{6,7},{8,9},{9,10},{10,11},{11... | collective-permute-start | bytes 221192 | tf_op jit(solution)/shard_map/ppermute | solution.py:16
  (42 other events, 161.2 us)
Sparse Core Ops, SparseCore 0:
  255.4 151.4 all-reduce.2
where the time goes:
time: 423 us; the launch traced here: 418 us
  waiting for transfers between devices  152 us (36%)
  matrix products  121 us (29%)
  starting transfers between devices  46.5 us (11%)
  other arithmetic  31.7 us (7%)
  loops' own time  27.3 us (6%)
  local copies, waits for them, and re-layouts  23.5 us (6%)
  between operations  15.2 us (4%)
    psum x1, waiting for transfers between devices, shards(): lax.psum((grad_sub * scale, grad_down * scale), ('gx', 'gy'))  148 us
    ppermute x12, starting transfers between devices, shifted(): return lax.ppermute(block, axis, route)  34.1 us
    another operation x1, loops' own time, shards(): result = lax.fori_loop(0, ROWS // VB, one_block, initial)  27.1 us
    dot_general x4, matrix products, one_block(): jnp.einsum('ci,kis->cks', table_blk, pick_local, preferred_element_type=j...  26.7 us
    dot_general x4, matrix products, one_block(): jnp.einsum('os,kis->koi', grad_pre, pick_local, preferred_element_type=jn...  20.7 us
    dot_general x4, matrix products, one_block(): jnp.einsum('koc,koi->ci', w_sub_wide, gathered, precision=highest)  16.5 us
    add x4, other arithmetic, one_block(): halo_acc + halo_add  12.3 us
    unnamed x17, local copies, waits for them, and re-layouts  11.7 us
  transfers between devices with their start and end apart: 17, of which 4 were waited for; matrix products, arithmetic and copies ran while one was open for 3% of the time, Pallas kernels for 0%

commit v1 on v0

v1 whole, which is shorter than its diff:
```python
import functools
import jax
import jax.numpy as jnp
from jax import lax
from jax.experimental import pallas as pl
from jax.sharding import PartitionSpec as P
from jax.experimental.pallas import tpu as pltpu

VB = 512
ROWS = 2048
CROWS = 512
CB = 64
C = 64
K = 27
KC = K * C
L = 256
H = VB // L
CQ = 128
EDGE = 640
WIDE = VB + 2 * CB
HALF = (KC + 8 * C) // 2
PIECE = 16
BF = jnp.bfloat16
F32 = jnp.float32
DIRS = [3 * (k // 9) + k // 3 % 3 for k in range(K)]


def mm(a, b):
    return jnp.dot(a, b, preferred_element_type=F32)


def mm_nt(a, b):
    return lax.dot_general(a, b, (((1,), (1,)), ((), ())), preferred_element_type=F32)


def pick(cond):
    return jnp.where(cond, jnp.ones((), BF), jnp.zeros((), BF))


def block_work(remote, first, base, refs):
    (feat, rows, frm, dmap, grad, halo, w_cat, w_t, wd_cat, wd_t, hot, source, spread) = refs
    slots = 2 * H if remote else H
    row_v = rows[...]
    frm_v = frm[...]
    if remote:
        joint = jnp.where(frm_v == 4, row_v, jnp.where(frm_v == 9, -1, row_v + VB))
    else:
        joint = jnp.where(frm_v == 4, row_v - base, -1)
    high = joint >> (L.bit_length() - 1)
    low = (joint & (L - 1)).astype(F32).astype(BF)
    low_ids = lax.broadcasted_iota(jnp.int32, (L, VB), 0).astype(F32).astype(BF)
    local = jnp.concatenate([feat[:, i * L:(i + 1) * L] for i in range(H)], axis=0)
    for k in range(K):
        one_hot = pick(low[k:k + 1, :] == low_ids)
        hot[k] = one_hot
        parts = [mm(local, one_hot)]
        if remote and DIRS[k] != 4:
            slab = halo[DIRS[k] % 3][DIRS[k] // 3, :, 0:VB]
            slab = jnp.concatenate([slab[:, i * L:(i + 1) * L] for i in range(H)], axis=0)
            parts.append(mm(slab, one_hot))
        high_k = high[k:k + 1, :]
        got = jnp.zeros((C, VB), F32)
        for j, part in enumerate(parts):
            for i in range(H):
                got = jnp.where(high_k == j * H + i, part[i * C:(i + 1) * C, :], got)
        source[k * C:(k + 1) * C, :] = got.astype(BF)
    pre = mm(w_cat[...], source[...])
    sig = jax.nn.sigmoid(pre)
    hidden = (pre * sig).astype(BF)
    target = dmap[0:1, :]
    kind = dmap[1:2, :]
    coarse_rel = jnp.where(target < CROWS, target - base // 4, -1)
    pick_own = pick(coarse_rel == lax.broadcasted_iota(jnp.int32, (CQ, VB), 0))
    zero = jnp.zeros((), BF)
    kinds = [kind == i for i in range(8)]
    picked_h = jnp.concatenate([jnp.where(m, hidden, zero) for m in kinds], axis=0)
    contrib = mm(wd_cat[...], picked_h)
    c_hi = contrib.astype(BF)
    c_lo = (contrib - c_hi.astype(F32)).astype(BF)
    split = jnp.concatenate([c_hi, c_lo], axis=0)
    own = mm_nt(split, pick_own)
    coarse = own[:C] + own[C:]
    up = mm(grad[...], pick_own)
    edge = None
    if remote:
        edge_ids = lax.broadcasted_iota(jnp.int32, (EDGE, VB), 0)
        pick_edge = pick((target - CROWS) == edge_ids)
        edge_grad = jnp.concatenate([halo[d % 3][d // 3, :, VB:VB + CB] for d in range(9)] + [jnp.zeros((C, EDGE - 9 * CB), BF)], axis=1)
        edge_grad = jnp.where(lax.broadcasted_iota(jnp.int32, (C, EDGE), 1) < 9 * CB, edge_grad, zero)
        up = up + mm(edge_grad, pick_edge)
        both = mm_nt(split, pick_edge)
        edge = both[:C] + both[C:]
    up = up.astype(BF)
    picked_g = jnp.concatenate([jnp.where(m, up, zero) for m in kinds], axis=0)
    grad_hidden = mm(wd_t[...], picked_g)
    grad_down = mm_nt(picked_g, hidden)
    grad_pre = (grad_hidden * sig * (1.0 + pre * (1.0 - sig))).astype(BF)
    grad_sub = mm_nt(source[...], grad_pre)
    for k in range(K):
        high_k = high[k:k + 1, :]
        count = slots if (remote and DIRS[k] != 4) else H
        masked = jnp.concatenate([jnp.where(high_k == i, grad_pre, zero) for i in range(count)], axis=0)
        out = mm_nt(masked, hot[k]).astype(BF)
        for i in range(count):
            spread[k * C:(k + 1) * C, i * L:(i + 1) * L] = out[i * C:(i + 1) * C, :]
    gfeat = mm(w_t[...], spread[:, 0:VB])
    outward = []
    if remote:
        for d in range(9):
            ks = [k for k in range(K) if DIRS[k] == d]
            if d == 4:
                outward.append(jnp.zeros((C, VB), F32))
            else:
                a, b = ks[0] * C, (ks[-1] + 1) * C
                outward.append(mm(w_t[:, a:b], spread[a:b, VB:2 * VB]))
    return coarse, gfeat, grad_sub, grad_down, edge, outward


def local_kernel(counts, feat, rows, frm, dmap, grad, w_sub, w_down,
                 coarse_o, gfeat_o, gsub_o, gdown_o, w_cat, w_t, wd_cat, wd_t, hot, source, spread):
    i = pl.program_id(0)

    @pl.when(i == 0)
    def _():
        w_cat[...] = jnp.concatenate([w_sub[k] for k in range(K)], axis=1)
        w_t[...] = w_sub[...].reshape(KC, C).T
        wd_cat[...] = jnp.concatenate([w_down[k] for k in range(8)], axis=1)
        wd_t[...] = w_down[...].reshape(8 * C, C).T
        gsub_o[...] = jnp.zeros_like(gsub_o)
        gdown_o[...] = jnp.zeros_like(gdown_o)

    @pl.when(i + 1 < counts[0])
    def _():
        refs = (feat, rows, frm, dmap, grad, None, w_cat, w_t, wd_cat, wd_t, hot, source, spread)
        coarse, gfeat, gsub, gdown, _, _ = block_work(False, False, (i + 1) * VB, refs)
        coarse_o[...] = coarse.astype(BF)
        gfeat_o[...] = gfeat.astype(BF)
        gsub_o[...] += gsub
        gdown_o[...] += gdown

    @pl.when(i + 1 >= counts[0])
    def _():
        coarse_o[...] = jnp.zeros_like(coarse_o)
        gfeat_o[...] = jnp.zeros_like(gfeat_o)


def full(shape):
    return pl.BlockSpec(shape, lambda i: (0,) * len(shape))


def local_call(counts, feat, rows, frm, dmap, grad, w_sub, w_down):
    sd = jax.ShapeDtypeStruct
    return pl.pallas_call(
        local_kernel,
        grid=(3,),
        in_specs=[
            pl.BlockSpec(memory_space=pltpu.SMEM),
            pl.BlockSpec((C, VB), lambda i: (0, i + 1)),
            pl.BlockSpec((K, VB), lambda i: (0, i + 1)),
            pl.BlockSpec((K, VB), lambda i: (0, i + 1)),
            pl.BlockSpec((2, VB), lambda i: (0, i + 1)),
            pl.BlockSpec((C, CQ), lambda i: (0, i + 1)),
            full((K, C, C)),
            full((8, C, C)),
        ],
        out_specs=[
            pl.BlockSpec((C, CQ), lambda i: (0, i + 1)),
            pl.BlockSpec((C, VB), lambda i: (0, i + 1)),
            full((KC, C)),
            full((8 * C, C)),
            full((C, KC)),
            full((C, KC)),
            full((C, 8 * C)),
            full((C, 8 * C)),
        ],
        out_shape=[
            sd((C, CROWS), BF), sd((C, ROWS), BF), sd((KC, C), F32), sd((8 * C, C), F32),
            sd((C, KC), BF), sd((C, KC), BF), sd((C, 8 * C), BF), sd((C, 8 * C), BF),
        ],
        scratch_shapes=[
            pltpu.VMEM((K, L, VB), BF),
            pltpu.VMEM((KC, VB), BF),
            pltpu.VMEM((KC, VB), BF),
        ],
        compiler_params=pltpu.CompilerParams(vmem_limit_bytes=48 << 20),
        name="local_blocks",
    )(counts, feat, rows, frm, dmap, grad, w_sub, w_down)


def border_kernel(feat, rows, frm, dmap, grad, below, column, above, w_cat, w_t, wd_cat, wd_t, gsub, gdown,
                  coarse_o, gfeat_o, packed_o, mid_o, down_o, up_o, hot, source, spread):
    refs = (feat, rows, frm, dmap, grad, (below, column, above), w_cat, w_t, wd_cat, wd_t, hot, source, spread)
    coarse, gfeat, dsub, ddown, edge, outward = block_work(True, True, 0, refs)
    coarse_o[...] = coarse
    gfeat_o[...] = gfeat
    whole = jnp.concatenate([gsub[...] + dsub, gdown[...] + ddown], axis=0)
    packed_o[0:HALF, :] = jnp.concatenate([whole[:HALF], whole[HALF:]], axis=1).astype(BF)
    packed_o[HALF:, :] = jnp.zeros((packed_o.shape[0] - HALF, 2 * C), BF)
    for d in range(9):
        out = (down_o, mid_o, up_o)[d % 3]
        out[d // 3, :, 0:VB] = outward[d].astype(out.dtype)
        tail = jnp.concatenate([edge[:, d * CB:(d + 1) * CB], jnp.zeros((C, CB), F32)], axis=1)
        out[d // 3, :, VB:] = tail.astype(out.dtype)


def border_call(feat, rows, frm, dmap, grad, below, column, above, w_cat, w_t, wd_cat, wd_t, gsub, gdown):
    sd = jax.ShapeDtypeStruct
    count = lax.axis_size("gx") * lax.axis_size("gy")
    return pl.pallas_call(
        border_kernel,
        grid=(1,),
        in_specs=[
            pl.BlockSpec((C, VB), lambda i: (0, 0)),
            pl.BlockSpec((K, VB), lambda i: (0, 0)),
            pl.BlockSpec((K, VB), lambda i: (0, 0)),
            pl.BlockSpec((2, VB), lambda i: (0, 0)),
            pl.BlockSpec((C, CQ), lambda i: (0, 0)),
            full((3, C, WIDE)), full((3, C, WIDE)), full((3, C, WIDE)),
            full((C, KC)), full((C, KC)), full((C, 8 * C)), full((C, 8 * C)),
            full((KC, C)), full((8 * C, C)),
        ],
        out_specs=[
            full((C, CQ)), full((C, VB)), full((count * PIECE, 2 * C)),
            full((3, C, WIDE)), full((3, C, WIDE)), full((3, C, WIDE)),
        ],
        out_shape=[
            sd((C, CQ), F32), sd((C, VB), F32), sd((count * PIECE, 2 * C), BF),
            sd((3, C, WIDE), F32), sd((3, C, WIDE), BF), sd((3, C, WIDE), BF),
        ],
        scratch_shapes=[
            pltpu.VMEM((K, L, VB), BF),
            pltpu.VMEM((KC, VB), BF),
            pltpu.VMEM((KC, 2 * VB), BF),
        ],
        compiler_params=pltpu.CompilerParams(vmem_limit_bytes=48 << 20),
        name="border_block",
    )(feat, rows, frm, dmap, grad, below, column, above, w_cat, w_t, wd_cat, wd_t, gsub, gdown)


def finish_kernel(coarse_i, gfeat_i, coarse, gfeat, total, left, right, coarse_o, gfeat_o):
    inc = total[...] + left[...].astype(F32) + right[...].astype(F32)
    gfeat_o[...] = (gfeat[...] + inc[:, 0:VB]).astype(BF)
    coarse_o[:, 0:CB] = (coarse[:, 0:CB] + inc[:, VB:VB + CB]).astype(BF)
    coarse_o[:, CB:] = coarse[:, CB:].astype(BF)


def finish_call(coarse_all, gfeat_all, coarse, gfeat, total, left, right):
    sd = jax.ShapeDtypeStruct
    return pl.pallas_call(
        finish_kernel,
        grid=(1,),
        in_specs=[
            pl.BlockSpec(memory_space=pl.ANY),
            pl.BlockSpec(memory_space=pl.ANY),
            full((C, CQ)), full((C, VB)), full((C, WIDE)), full((C, WIDE)), full((C, WIDE)),
        ],
        out_specs=[pl.BlockSpec((C, CQ), lambda i: (0, 0)), pl.BlockSpec((C, VB), lambda i: (0, 0))],
        out_shape=[sd((C, CROWS), BF), sd((C, ROWS), BF)],
        input_output_aliases={0: 0, 1: 1},
        name="add_incoming",
    )(coarse_all, gfeat_all, coarse, gfeat, total, left, right)


def weights_kernel(scale, packed, gsub_o, gdown_o):
    whole = packed[...].astype(F32) * scale
    for k in range(K):
        r = k * C
        part = whole[r:r + C, 0:C] if r + C <= HALF else None
        if part is None:
            if r >= HALF:
                part = whole[r - HALF:r - HALF + C, C:2 * C]
            else:
                part = jnp.concatenate([whole[r:HALF, 0:C], whole[0:r + C - HALF, C:2 * C]], axis=0)
        gsub_o[k] = part.T
    for k in range(8):
        r = KC + k * C - HALF
        gdown_o[k] = whole[r:r + C, C:2 * C]


def weights_call(scale, packed):
    sd = jax.ShapeDtypeStruct
    return pl.pallas_call(
        functools.partial(weights_kernel, scale),
        grid=(1,),
        in_specs=[pl.BlockSpec((HALF, 2 * C), lambda i: (0, 0))],
        out_specs=[full((K, C, C)), full((8, C, C))],
        out_shape=[sd((K, C, C), F32), sd((8, C, C), F32)],
        name="unpack_weights",
    )(packed)


def ring(block, axis, step):
    n = lax.axis_size(axis)
    return lax.ppermute(block, axis, [(i, (i + step) % n) for i in range(n)])


def shards(features, counts, sub_rows, sub_from, down_map, w_sub, w_down, cotangent):
    feat = features[0, 0]
    grad = cotangent[0, 0]
    rows, frm, dmap = sub_rows[0, 0], sub_from[0, 0], down_map[0, 0]
    nx, ny = lax.axis_size("gx"), lax.axis_size("gy")
    count = nx * ny
    border = jnp.concatenate([feat[:, :VB], grad[:, :CB], jnp.zeros((C, CB), BF)], axis=1)
    column = jnp.stack([ring(border, "gx", 1), border, ring(border, "gx", -1)])
    below, above = ring(column, "gy", 1), ring(column, "gy", -1)
    coarse_all, gfeat_all, gsub, gdown, w_cat, w_t, wd_cat, wd_t = local_call(
        counts.reshape(1), feat, rows, frm, dmap, grad, w_sub, w_down)
    coarse, gfeat, packed, mid, down, up = border_call(
        feat, rows, frm, dmap, grad, below, column, above, w_cat, w_t, wd_cat, wd_t, gsub, gdown)
    from_up, from_down = ring(down, "gy", -1), ring(up, "gy", 1)
    total = mid + from_up.astype(F32) + from_down.astype(F32)
    from_right = ring(total[0].astype(BF), "gx", -1)
    from_left = ring(total[2].astype(BF), "gx", 1)
    pieces = lax.all_to_all(packed.reshape(count, -1, 2 * C), ("gx", "gy"), 0, 0, tiled=True)
    summed = jnp.sum(pieces.astype(F32), axis=0).astype(BF)
    spread = jnp.broadcast_to(summed[None], pieces.shape)
    gathered = lax.all_to_all(spread, ("gx", "gy"), 0, 0, tiled=True).reshape(-1, 2 * C)
    grad_w_sub, grad_w_down = weights_call(float(ROWS * count) ** -0.5, gathered)
    coarse_out, grad_features = finish_call(coarse_all, gfeat_all, coarse, gfeat, total[1], from_left, from_right)
    return coarse_out[None, None], grad_features[None, None], grad_w_sub, grad_w_down


def solution(mesh):
    tile = P("gx", "gy", None, None)
    return jax.shard_map(
        shards,
        mesh=mesh,
        in_specs=(tile, P("gx", "gy"), tile, tile, tile, P(), P(), tile),
        out_specs=(tile, tile, P(), P()),
        check_vma=False,
    )
```

time: 423 us -> 85.4 us (0.20); the launches traced: 418 us -> 85.4 us
  waiting for transfers between devices: 152 us -> 28.1 us
  matrix products: 121 us -> 0 us
  other arithmetic: 31.7 us -> 0.3 us
  loops' own time: 27.3 us -> 0 us
  local copies, waits for them, and re-layouts: 23.5 us -> 6.62 us
  between operations: 15.2 us -> 1.44 us
  Pallas kernels: 0 us -> 11.9 us
  starting transfers between devices: 46.5 us -> 37 us
    psum x1 -> x0, waiting for transfers between devices: 148 us -> none  [shards(): lax.psum((grad_sub * scale, grad_down * scale), ('gx', 'gy'))]
    dot_general x48 -> x0, matrix products: 121 us -> none  [the longest x4 26.7 us: one_block(): jnp.einsum('ci,kis->cks', table_blk, pick_local, preferred_element_type=j...]
    ppermute x16 -> x8, starting transfers between devices: 46.4 us -> 17.9 us  [ring(): return lax.ppermute(block, axis, [(i, (i + step) % n) for i in range(n)])]
    another operation x9 -> x0, loops' own time: 27.3 us -> none  [the longest x1 27.1 us: shards(): result = lax.fori_loop(0, ROWS // VB, one_block, initial)]
    all_to_all x0 -> x2, starting transfers between devices: none -> 19.1 us  [the longest x1 14.6 us: shards(): lax.all_to_all(packed.reshape(count, -1, 2 * C), ('gx', 'gy'), 0, 0, tile...]
    add x10 -> x0, other arithmetic: 12.6 us -> none  [the longest x4 12.3 us: one_block(): halo_acc + halo_add]
    all_to_all x0 -> x2, waiting for transfers between devices: none -> 12.2 us  [the longest x1 12.2 us: shards(): lax.all_to_all(packed.reshape(count, -1, 2 * C), ('gx', 'gy'), 0, 0, tile...]
    pallas_call x0 -> x4, Pallas kernels: none -> 11.9 us  [the longest x1 5.99 us: border_call(): pl.pallas_call(border_kernel, grid=(1,), in_specs=[pl.BlockSpec((C, VB),...]
  transfers between devices with their start and end apart: 17 -> 10, of which waited for: 4 -> 6; matrix products, arithmetic and copies ran while one was open for 3% -> 2% of each run, Pallas kernels for 0% -> 4%
where the time goes in v1:
time: 85.4 us
  starting transfers between devices  37 us (43%)
  waiting for transfers between devices  28.1 us (33%)
  Pallas kernels  11.9 us (14%)
  local copies, waits for them, and re-layouts  6.62 us (8%)
  between operations  1.44 us (2%)
    ppermute x8, starting transfers between devices, ring(): return lax.ppermute(block, axis, [(i, (i + step) % n) for i in range(n)])  17.9 us
    ppermute x8, waiting for transfers between devices, ring(): return lax.ppermute(block, axis, [(i, (i + step) % n) for i in range(n)])  16 us
    all_to_all x1, starting transfers between devices, shards(): lax.all_to_all(packed.reshape(count, -1, 2 * C), ('gx', 'gy'), 0, 0, tile...  14.6 us
    all_to_all x1, waiting for transfers between devices, shards(): lax.all_to_all(packed.reshape(count, -1, 2 * C), ('gx', 'gy'), 0, 0, tile...  12.2 us
    pallas_call x1, Pallas kernels, border_call(): pl.pallas_call(border_kernel, grid=(1,), in_specs=[pl.BlockSpec((C, VB),...  5.99 us
    all_to_all x1, starting transfers between devices, shards(): lax.all_to_all(spread, ('gx', 'gy'), 0, 0, tiled=True).reshape(-1, 2 * C)  4.56 us
    unnamed x25, local copies, waits for them, and re-layouts  3.42 us
    pallas_call x1, Pallas kernels, weights_call(): pl.pallas_call(functools.partial(weights_kernel, scale), grid=(1,), in_sp...  2.41 us
  transfers between devices with their start and end apart: 10, of which 6 were waited for; matrix products, arithmetic and copies ran while one was open for 2% of the time, Pallas kernels for 4%

profile of v1, /device:TPU:1, one launch (start us, length us, event | category | flops | bytes accessed | tf_op | source)
XLA Modules:
  0.0 85.4 jit_solution(18405707892084409677)
XLA Ops:
  0.6 0.7 slice.23
  1.4 0.8 slice.22
  2.2 0.1 pad.5.clone
  2.3 7.1 %collective-permute-start.1 = (bf16[64,640]{1,0:T(8,128)(2,1)S(1)}, bf16[64,640]{1,0:T(8,128)(2,1)S(1)}, u32[]{:S(2)}, u32[]{:S(2)}) collective-permute-start(bf16[64,640]{1,0:T(8,128)(2,1)S(1)} %maximum_maximum_fusion), channel_id=1, source_target_pairs={{0,120},{8,0},{16,8},{24,16},{32,24},{40,32},{48,40},{56,48},{64,5... | collective-permute-start | bytes 245768 | tf_op jit(solution)/shard_map/ppermute | solution.py:294
  10.1 0.8 collective-permute-done.1
  10.9 5.1 %collective-permute-done = bf16[64,640]{1,0:T(8,128)(2,1)S(1)} collective-permute-done((bf16[64,640]{1,0:T(8,128)(2,1)S(1)}, bf16[64,640]{1,0:T(8,128)(2,1)S(1)}, u32[]{:S(2)}, u32[]{:S(2)}) %collective-permute-start) | collective-permute-done | bytes 81952 | tf_op jit(solution)/shard_map/ppermute | solution.py:294
  16.1 0.0 copy-start
  16.1 2.1 %collective-permute-start.3 = (bf16[3,64,640]{2,1,0:T(8,128)(2,1)S(1)}, bf16[3,64,640]{2,1,0:T(8,128)(2,1)S(1)}, u32[]{:S(2)}, u32[]{:S(2)}) collective-permute-start(bf16[3,64,640]{2,1,0:T(8,128)(2,1)S(1)} %pad_maximum_fusion.column), channel_id=1, source_target_pairs={{0,7},{1,0},{2,1},{3,2},{4,3},{5,4},{6,5},{7,6},{8,15},{9,8},{10,9... | collective-permute-start | bytes 737288 | tf_op jit(solution)/shard_map/ppermute | solution.py:294
  18.2 1.1 %collective-permute-start.2 = (bf16[3,64,640]{2,1,0:T(8,128)(2,1)S(1)}, bf16[3,64,640]{2,1,0:T(8,128)(2,1)S(1)}, u32[]{:S(2)}, u32[]{:S(2)}) collective-permute-start(bf16[3,64,640]{2,1,0:T(8,128)(2,1)S(1)} %pad_maximum_fusion.column), channel_id=1, source_target_pairs={{0,1},{1,2},{2,3},{3,4},{4,5},{5,6},{6,7},{7,0},{8,9},{9,10},{10,1... | collective-permute-start | bytes 737288 | tf_op jit(solution)/shard_map/ppermute | solution.py:294
  19.4 0.1 copy_bitcast_fusion
  19.5 0.5 copy-done.5
  20.1 1.7 %local_blocks.1 = (bf16[64,512]{1,0:T(8,128)(2,1)}, bf16[64,2048]{1,0:T(8,128)(2,1)}, f32[1728,64]{1,0:T(8,128)S(1)}, f32[512,64]{1,0:T(8,128)S(1)}, bf16[64,172...) custom-call(s32[1]{0:T(128)} %bitcast.22.counts, ...), custom_call_target="tpu_custom_call" | custom-call | tf_op jit(solution)/shard_map/local_blocks/pallas_call | solution.py:153
  21.8 1.7 %collective-permute-done.3.above = bf16[3,64,640]{2,1,0:T(8,128)(2,1)S(1)} collective-permute-done((bf16[3,64,640]{2,1,0:T(8,128)(2,1)S(1)}, bf16[3,64,640]{2,1,0:T(8,128)(2,1)S(1)}, u32[]{:S(2)}, u32[]{:S(2)}) %collective-permute-start.3) | collective-permute-done | bytes 245792 | tf_op jit(solution)/shard_map/ppermute | solution.py:294
  23.5 6.0 %border_block.1 = (f32[64,128]{1,0:T(8,128)S(1)}, f32[64,512]{1,0:T(8,128)S(1)}, bf16[2048,128]{1,0:T(8,128)(2,1)}, f32[3,64,640]{2,1,0:T(8,128)S(1)}, bf16[3,64...) custom-call(bf16[64,2048]{1,0:T(8,128)(2,1)S(1)} %bitcast.25, s32[27,2048]{1,0:T(8,128)S(1)} %get-tuple-element.45.rows, ...), custom_call_target="tpu_custom_call" | custom-call | tf_op jit(solution)/shard_map/border_block/pallas_call | solution.py:209
  29.5 0.7 copy-done.3
  30.2 0.6 copy-done.6
  30.8 14.6 %all-to-all-start = ((bf16[128,16,128]{2,1,0:T(8,128)(2,1)}), bf16[128,16,128]{2,1,0:T(8,128)(2,1)S(1)}, u32[]{:S(2)}, u32[]{:S(2)}) async-start(bf16[128,16,128]{2,1,0:T(8,128)(2,1)} %bitcast.12), calls=%async_computation | async-start | bytes 1048576 | tf_op jit(solution)/shard_map/all_to_all | solution.py:314
  45.3 1.1 %collective-permute-start.4 = (bf16[3,64,640]{2,1,0:T(8,128)(2,1)S(1)}, bf16[3,64,640]{2,1,0:T(8,128)(2,1)S(1)}, u32[]{:S(2)}, u32[]{:S(2)}) collective-permute-start(bf16[3,64,640]{2,1,0:T(8,128)(2,1)S(1)} %get-tuple-element.33), channel_id=1, source_target_pairs={{0,7},{1,0},{2,1},{3,2},{4,3},{5,4},{6,5},{7,6},{8,15},{9,8},{10,9... | collective-permute-start | bytes 737288 | tf_op jit(solution)/shard_map/ppermute | solution.py:294
  46.4 0.7 collective-permute-start.5
  47.1 12.2 %all-to-all-done = bf16[128,16,128]{2,1,0:T(8,128)(2,1)S(1)} async-done(((bf16[128,16,128]{2,1,0:T(8,128)(2,1)}), bf16[128,16,128]{2,1,0:T(8,128)(2,1)S(1)}, u32[]{:S(2)}, u32[]{:S(2)}) %all-to-all-start) | async-done | bytes 524320 | tf_op jit(solution)/shard_map/all_to_all | solution.py:314
  59.3 0.1 reduce_sum.12
  59.4 0.9 %broadcast_in_dim.18 = bf16[128,16,128]{2,1,0:T(8,128)(2,1)} broadcast(bf16[16,128]{1,0:T(8,128)(2,1)S(1)} %reduce_sum.12), dimensions={1,2} | broadcast | bytes 528384 | tf_op jit(solution)/shard_map/broadcast_in_dim | solution.py:316
  60.3 4.6 %all-to-all-start.1 = ((bf16[128,16,128]{2,1,0:T(8,128)(2,1)}), bf16[128,16,128]{2,1,0:T(8,128)(2,1)S(1)}, u32[]{:S(2)}, u32[]{:S(2)}) async-start(bf16[128,16,128]{2,1,0:T(8,128)(2,1)} %broadcast_in_dim.18), calls=%async_computation.1 | async-start | bytes 1048576 | tf_op jit(solution)/shard_map/all_to_all | solution.py:317
  64.9 0.1 fusion
  65.0 5.8 %collective-permute-start.7 = (bf16[64,640]{1,0:T(8,128)(2,1)S(1)}, bf16[64,640]{1,0:T(8,128)(2,1)S(1)}, u32[]{:S(2)}, u32[]{:S(2)}) collective-permute-start(bf16[64,640]{1,0:T(8,128)(2,1)S(1)} %get-tuple-element.42), channel_id=1, source_target_pairs={{0,120},{8,0},{16,8},{24,16},{32,24},{40,32},{48,40},{56,48},{64,5... | collective-permute-start | bytes 245768 | tf_op jit(solution)/shard_map/ppermute | solution.py:294
  70.8 0.7 slice_bitcast_fusion.total
  71.4 2.3 %collective-permute-done.7.right = bf16[64,640]{1,0:T(8,128)(2,1)S(1)} collective-permute-done((bf16[64,640]{1,0:T(8,128)(2,1)S(1)}, bf16[64,640]{1,0:T(8,128)(2,1)S(1)}, u32[]{:S(2)}, u32[]{:S(2)}) %collective-permute-start.7) | collective-permute-done | bytes 81952 | tf_op jit(solution)/shard_map/ppermute | solution.py:294
  73.7 6.0 %collective-permute-done.6.left = bf16[64,640]{1,0:T(8,128)(2,1)S(1)} collective-permute-done((bf16[64,640]{1,0:T(8,128)(2,1)S(1)}, bf16[64,640]{1,0:T(8,128)(2,1)S(1)}, u32[]{:S(2)}, u32[]{:S(2)}) %collective-permute-start.6) | collective-permute-done | bytes 81952 | tf_op jit(solution)/shard_map/ppermute | solution.py:294
  79.7 0.6 copy-done.11
  80.4 1.8 %add_incoming.1 = (bf16[64,512]{1,0:T(8,128)(2,1)}, bf16[64,2048]{1,0:T(8,128)(2,1)}) custom-call(bf16[64,512]{1,0:T(8,128)(2,1)} %get-tuple-element.22.coarse_i, bf16[64,2048]{1,0:T(8,128)(2,1)} %get-tuple-element.23.gfeat_i, f32[64,128]{1,0:T(8,128)} %copy-done.6, f32[64,512]{1,0:T(8,128)} %copy-done.3, ...), custom_call_target="tpu_custom_call", output_to_operand_aliasing={{0}: (0, {}), {1}: (1, {})} | custom-call | tf_op jit(solution)/shard_map/add_incoming/pallas_call | solution.py:249
  82.1 0.8 copy-done.7
  82.9 2.4 %unpack_weights.1 = (f32[27,64,64]{2,1,0:T(8,128)}, f32[8,64,64]{2,1,0:T(8,128)}) custom-call(bf16[2048,128]{1,0:T(8,128)(2,1)} %bitcast.31), custom_call_target="tpu_custom_call" | custom-call | tf_op jit(solution)/shard_map/unpack_weights/pallas_call | solution.py:282
  (29 shorter events, 0.2 us)
Async XLA Ops:
  2.3 8.6 %collective-permute-start.1 = (bf16[64,640]{1,0:T(8,128)(2,1)S(1)}, bf16[64,640]{1,0:T(8,128)(2,1)S(1)}, u32[]{:S(2)}, u32[]{:S(2)}) collective-permute-start(bf16[64,640]{1,0:T(8,128)(2,1)S(1)} %maximum_maximum_fusion), channel_id=1, source_target_pairs={{0,120},{8,0},{16,8},{24,16},{32,24},{40,32},{48,40},{56,48},{64,5... | collective-permute-start | bytes 245768 | tf_op jit(solution)/shard_map/ppermute | solution.py:294
  9.4 6.6 %collective-permute-start = (bf16[64,640]{1,0:T(8,128)(2,1)S(1)}, bf16[64,640]{1,0:T(8,128)(2,1)S(1)}, u32[]{:S(2)}, u32[]{:S(2)}) collective-permute-start(bf16[64,640]{1,0:T(8,128)(2,1)S(1)} %maximum_maximum_fusion), channel_id=1, source_target_pairs={{0,8},{8,16},{16,24},{24,32},{32,40},{40,48},{48,56},{56,64},{64,7... | collective-permute-start | bytes 245768 | tf_op jit(solution)/shard_map/ppermute | solution.py:294
  16.0 3.3 %copy-start.8 = (s32[1,1,27,2048]{3,1,2,0:T(1,128)S(1)}, s32[1,1,27,2048]{3,1,2,0:T(1,128)}, u32[]{:S(2)}) copy-start(s32[1,1,27,2048]{3,1,2,0:T(1,128)} %param.11) | copy-start | bytes 663556
  16.0 3.3 %copy-start.9 = (s32[1,1,27,2048]{3,1,2,0:T(1,128)S(1)}, s32[1,1,27,2048]{3,1,2,0:T(1,128)}, u32[]{:S(2)}) copy-start(s32[1,1,27,2048]{3,1,2,0:T(1,128)} %param.10) | copy-start | bytes 663556
  16.1 3.4 %copy-start = (bf16[1,1,64,2048]{3,2,1,0:T(8,128)(2,1)S(1)}, bf16[1,1,64,2048]{3,2,1,0:T(8,128)(2,1)}, u32[]{:S(2)}) copy-start(bf16[1,1,64,2048]{3,2,1,0:T(8,128)(2,1)} %param.8) | copy-start | bytes 786436
  16.1 3.4 %copy-start.1 = (bf16[27,64,64]{2,1,0:T(8,128)(2,1)S(1)}, bf16[27,64,64]{2,1,0:T(8,128)(2,1)}, u32[]{:S(2)}) copy-start(bf16[27,64,64]{2,1,0:T(8,128)(2,1)} %w_sub.1) | copy-start | bytes 663556
  16.1 3.4 %copy-start.2 = (bf16[1,1,64,512]{3,2,1,0:T(8,128)(2,1)S(1)}, bf16[1,1,64,512]{3,2,1,0:T(8,128)(2,1)}, u32[]{:S(2)}) copy-start(bf16[1,1,64,512]{3,2,1,0:T(8,128)(2,1)} %param.15) | copy-start | bytes 196612
  16.1 3.4 %copy-start.4 = (bf16[8,64,64]{2,1,0:T(8,128)(2,1)S(1)}, bf16[8,64,64]{2,1,0:T(8,128)(2,1)}, u32[]{:S(2)}) copy-start(bf16[8,64,64]{2,1,0:T(8,128)(2,1)} %w_down.1) | copy-start | bytes 196612
  16.1 7.4 %collective-permute-start.3 = (bf16[3,64,640]{2,1,0:T(8,128)(2,1)S(1)}, bf16[3,64,640]{2,1,0:T(8,128)(2,1)S(1)}, u32[]{:S(2)}, u32[]{:S(2)}) collective-permute-start(bf16[3,64,640]{2,1,0:T(8,128)(2,1)S(1)} %pad_maximum_fusion.column), channel_id=1, source_target_pairs={{0,7},{1,0},{2,1},{3,2},{4,3},{5,4},{6,5},{7,6},{8,15},{9,8},{10,9... | collective-permute-start | bytes 737288 | tf_op jit(solution)/shard_map/ppermute | solution.py:294
  18.2 5.3 %collective-permute-start.2 = (bf16[3,64,640]{2,1,0:T(8,128)(2,1)S(1)}, bf16[3,64,640]{2,1,0:T(8,128)(2,1)S(1)}, u32[]{:S(2)}, u32[]{:S(2)}) collective-permute-start(bf16[3,64,640]{2,1,0:T(8,128)(2,1)S(1)} %pad_maximum_fusion.column), channel_id=1, source_target_pairs={{0,1},{1,2},{2,3},{3,4},{4,5},{5,6},{6,7},{7,0},{8,9},{9,10},{10,1... | collective-permute-start | bytes 737288 | tf_op jit(solution)/shard_map/ppermute | solution.py:294
  19.4 0.7 copy-start.5
  29.5 0.7 copy-start.3
  30.2 0.6 copy-start.6
  30.8 28.5 %all-to-all-start = ((bf16[128,16,128]{2,1,0:T(8,128)(2,1)}), bf16[128,16,128]{2,1,0:T(8,128)(2,1)S(1)}, u32[]{:S(2)}, u32[]{:S(2)}) async-start(bf16[128,16,128]{2,1,0:T(8,128)(2,1)} %bitcast.12), calls=%async_computation | async-start | bytes 1048576 | tf_op jit(solution)/shard_map/all_to_all | solution.py:314
  45.3 19.5 %collective-permute-start.4 = (bf16[3,64,640]{2,1,0:T(8,128)(2,1)S(1)}, bf16[3,64,640]{2,1,0:T(8,128)(2,1)S(1)}, u32[]{:S(2)}, u32[]{:S(2)}) collective-permute-start(bf16[3,64,640]{2,1,0:T(8,128)(2,1)S(1)} %get-tuple-element.33), channel_id=1, source_target_pairs={{0,7},{1,0},{2,1},{3,2},{4,3},{5,4},{6,5},{7,6},{8,15},{9,8},{10,9... | collective-permute-start | bytes 737288 | tf_op jit(solution)/shard_map/ppermute | solution.py:294
  46.4 18.4 %collective-permute-start.5 = (bf16[3,64,640]{2,1,0:T(8,128)(2,1)S(1)}, bf16[3,64,640]{2,1,0:T(8,128)(2,1)S(1)}, u32[]{:S(2)}, u32[]{:S(2)}) collective-permute-start(bf16[3,64,640]{2,1,0:T(8,128)(2,1)S(1)} %get-tuple-element.34), channel_id=1, source_target_pairs={{0,1},{1,2},{2,3},{3,4},{4,5},{5,6},{6,7},{7,0},{8,9},{9,10},{10,1... | collective-permute-start | bytes 737288 | tf_op jit(solution)/shard_map/ppermute | solution.py:294
  60.3 21.9 %all-to-all-start.1 = ((bf16[128,16,128]{2,1,0:T(8,128)(2,1)}), bf16[128,16,128]{2,1,0:T(8,128)(2,1)S(1)}, u32[]{:S(2)}, u32[]{:S(2)}) async-start(bf16[128,16,128]{2,1,0:T(8,128)(2,1)} %broadcast_in_dim.18), calls=%async_computation.1 | async-start | bytes 1048576 | tf_op jit(solution)/shard_map/all_to_all | solution.py:317
  65.0 8.7 %collective-permute-start.7 = (bf16[64,640]{1,0:T(8,128)(2,1)S(1)}, bf16[64,640]{1,0:T(8,128)(2,1)S(1)}, u32[]{:S(2)}, u32[]{:S(2)}) collective-permute-start(bf16[64,640]{1,0:T(8,128)(2,1)S(1)} %get-tuple-element.42), channel_id=1, source_target_pairs={{0,120},{8,0},{16,8},{24,16},{32,24},{40,32},{48,40},{56,48},{64,5... | collective-permute-start | bytes 245768 | tf_op jit(solution)/shard_map/ppermute | solution.py:294
  70.8 9.0 %collective-permute-start.6 = (bf16[64,640]{1,0:T(8,128)(2,1)S(1)}, bf16[64,640]{1,0:T(8,128)(2,1)S(1)}, u32[]{:S(2)}, u32[]{:S(2)}) collective-permute-start(bf16[64,640]{1,0:T(8,128)(2,1)S(1)} %get-tuple-element.43), channel_id=1, source_target_pairs={{0,8},{8,16},{16,24},{24,32},{32,40},{40,48},{48,56},{56,64},{64,7... | collective-permute-start | bytes 245768 | tf_op jit(solution)/shard_map/ppermute | solution.py:294
  73.7 6.1 %copy-start.10 = (bf16[64,640]{1,0:T(8,128)(2,1)}, bf16[64,640]{1,0:T(8,128)(2,1)S(1)}, u32[]{:S(2)}) copy-start(bf16[64,640]{1,0:T(8,128)(2,1)S(1)} %collective-permute-done.7.right) | copy-start | bytes 245764
  79.7 0.6 copy-start.11
  82.1 0.8 copy-start.7

commit v2 on v1

--- a/solution.py
+++ b/solution.py
@@ -19,7 +19,8 @@
 EDGE = 640
 WIDE = VB + 2 * CB
 HALF = (KC + 8 * C) // 2
-PIECE = 16
+PAIRS = 5
+PIECE = 2 * PAIRS
 BF = jnp.bfloat16
 F32 = jnp.float32
 DIRS = [3 * (k // 9) + k // 3 % 3 for k in range(K)]
@@ -37,7 +38,7 @@
     return jnp.where(cond, jnp.ones((), BF), jnp.zeros((), BF))
 
 
-def block_work(remote, first, base, refs):
+def block_work(remote, base, refs):
     (feat, rows, frm, dmap, grad, halo, w_cat, w_t, wd_cat, wd_t, hot, source, spread) = refs
     slots = 2 * H if remote else H
     row_v = rows[...]
@@ -116,81 +117,156 @@
     return coarse, gfeat, grad_sub, grad_down, edge, outward
 
 
-def local_kernel(counts, feat, rows, frm, dmap, grad, w_sub, w_down,
-                 coarse_o, gfeat_o, gsub_o, gdown_o, w_cat, w_t, wd_cat, wd_t, hot, source, spread):
-    i = pl.program_id(0)
-
-    @pl.when(i == 0)
+def prepare_weights(w_sub, w_down, w_cat, w_t, wd_cat, wd_t):
+    w_cat[...] = jnp.concatenate([w_sub[k] for k in range(K)], axis=1)
+    w_t[...] = w_sub[...].reshape(KC, C).T
+    wd_cat[...] = jnp.concatenate([w_down[k] for k in range(8)], axis=1)
+    wd_t[...] = w_down[...].reshape(8 * C, C).T
+
+
+def one_local(block, counts, feat, rows, frm, dmap, grad, weights, outs, scratch):
+    coarse_o, gfeat_o, gsub_o, gdown_o = outs
+
+    @pl.when(block < counts[0])
     def _():
-        w_cat[...] = jnp.concatenate([w_sub[k] for k in range(K)], axis=1)
-        w_t[...] = w_sub[...].reshape(KC, C).T
-        wd_cat[...] = jnp.concatenate([w_down[k] for k in range(8)], axis=1)
-        wd_t[...] = w_down[...].reshape(8 * C, C).T
-        gsub_o[...] = jnp.zeros_like(gsub_o)
-        gdown_o[...] = jnp.zeros_like(gdown_o)
-
-    @pl.when(i + 1 < counts[0])
-    def _():
-        refs = (feat, rows, frm, dmap, grad, None, w_cat, w_t, wd_cat, wd_t, hot, source, spread)
-        coarse, gfeat, gsub, gdown, _, _ = block_work(False, False, (i + 1) * VB, refs)
+        refs = (feat, rows, frm, dmap, grad, None) + weights + scratch
+        coarse, gfeat, gsub, gdown, _, _ = block_work(False, block * VB, refs)
         coarse_o[...] = coarse.astype(BF)
         gfeat_o[...] = gfeat.astype(BF)
         gsub_o[...] += gsub
         gdown_o[...] += gdown
 
-    @pl.when(i + 1 >= counts[0])
+    @pl.when(block >= counts[0])
     def _():
         coarse_o[...] = jnp.zeros_like(coarse_o)
         gfeat_o[...] = jnp.zeros_like(gfeat_o)
 
 
+def first_kernel(counts, feat, rows, frm, dmap, grad, w_sub, w_down,
+                 coarse_o, gfeat_o, gsub_o, gdown_o, w_cat, w_t, wd_cat, wd_t, hot, source, spread):
+    prepare_weights(w_sub, w_down, w_cat, w_t, wd_cat, wd_t)
+    gsub_o[...] = jnp.zeros_like(gsub_o)
+    gdown_o[...] = jnp.zeros_like(gdown_o)
+    one_local(1, counts, feat, rows, frm, dmap, grad, (w_cat, w_t, wd_cat, wd_t),
+              (coarse_o, gfeat_o, gsub_o, gdown_o), (hot, source, spread))
+
+
+def rest_kernel(counts, feat, rows, frm, dmap, grad, w_cat, w_t, wd_cat, wd_t, gsub, gdown, coarse_a, gfeat_a,
+                coarse_o, gfeat_o, gsub_o, gdown_o, hot, source, spread):
+    i = pl.program_id(0)
+
+    @pl.when(i == 0)
+    def _():
+        gsub_o[...] = gsub[...]
+        gdown_o[...] = gdown[...]
+
+    one_local(i + 2, counts, feat, rows, frm, dmap, grad, (w_cat, w_t, wd_cat, wd_t),
+              (coarse_o, gfeat_o, gsub_o, gdown_o), (hot, source, spread))
+
+
 def full(shape):
     return pl.BlockSpec(shape, lambda i: (0,) * len(shape))
 
 
-def local_call(counts, feat, rows, frm, dmap, grad, w_sub, w_down):
+def columns(shape, first):
+    return pl.BlockSpec(shape, lambda i: (0, i + first))
+
+
+def table_specs(first):
+    return [columns((C, VB), first), columns((K, VB), first), columns((K, VB), first),
+            columns((2, VB), first), columns((C, CQ), first)]
+
+
+def work_scratch(width):
+    return [pltpu.VMEM((K, L, VB), BF), pltpu.VMEM((KC, VB), BF), pltpu.VMEM((KC, width), BF)]
+
+
+WEIGHTS = [(C, KC), (C, KC), (C, 8 * C), (C, 8 * C)]
+LIMIT = pltpu.CompilerParams(vmem_limit_bytes=26 << 20)
+SMALL = pltpu.CompilerParams(vmem_limit_bytes=8 << 20)
+
+
+def first_call(counts, feat, rows, frm, dmap, grad, w_sub, w_down):
     sd = jax.ShapeDtypeStruct
     return pl.pallas_call(
-        local_kernel,
-        grid=(3,),
-        in_specs=[
-            pl.BlockSpec(memory_space=pltpu.SMEM),
-            pl.BlockSpec((C, VB), lambda i: (0, i + 1)),
-            pl.BlockSpec((K, VB), lambda i: (0, i + 1)),
-            pl.BlockSpec((K, VB), lambda i: (0, i + 1)),
-            pl.BlockSpec((2, VB), lambda i: (0, i + 1)),
-            pl.BlockSpec((C, CQ), lambda i: (0, i + 1)),
-            full((K, C, C)),
-            full((8, C, C)),
-        ],
-        out_specs=[
-            pl.BlockSpec((C, CQ), lambda i: (0, i + 1)),
-            pl.BlockSpec((C, VB), lambda i: (0, i + 1)),
-            full((KC, C)),
-            full((8 * C, C)),
-            full((C, KC)),
-            full((C, KC)),
-            full((C, 8 * C)),
-            full((C, 8 * C)),
-        ],
-        out_shape=[
-            sd((C, CROWS), BF), sd((C, ROWS), BF), sd((KC, C), F32), sd((8 * C, C), F32),
-            sd((C, KC), BF), sd((C, KC), BF), sd((C, 8 * C), BF), sd((C, 8 * C), BF),
-        ],
-        scratch_shapes=[
-            pltpu.VMEM((K, L, VB), BF),
-            pltpu.VMEM((KC, VB), BF),
-            pltpu.VMEM((KC, VB), BF),
-        ],
-        compiler_params=pltpu.CompilerParams(vmem_limit_bytes=48 << 20),
-        name="local_blocks",
+        first_kernel,
+        grid=(1,),
+        in_specs=[pl.BlockSpec(memory_space=pltpu.SMEM)] + table_specs(1) + [full((K, C, C)), full((8, C, C))],
+        out_specs=[columns((C, CQ), 1), columns((C, VB), 1), full((KC, C)), full((8 * C, C))]
+        + [full(w) for w in WEIGHTS],
+        out_shape=[sd((C, CROWS), BF), sd((C, ROWS), BF), sd((KC, C), F32), sd((8 * C, C), F32)]
+        + [sd(w, BF) for w in WEIGHTS],
+        scratch_shapes=work_scratch(VB),
+        compiler_params=LIMIT,
+        name="first_local_block",
     )(counts, feat, rows, frm, dmap, grad, w_sub, w_down)
+
+
+def rest_call(counts, feat, rows, frm, dmap, grad, weights, gsub, gdown, coarse_all, gfeat_all):
+    sd = jax.ShapeDtypeStruct
+    return pl.pallas_call(
+        rest_kernel,
+        grid=(2,),
+        in_specs=[pl.BlockSpec(memory_space=pltpu.SMEM)] + table_specs(2) + [full(w) for w in WEIGHTS]
+        + [full((KC, C)), full((8 * C, C)), pl.BlockSpec(memory_space=pl.ANY), pl.BlockSpec(memory_space=pl.ANY)],
+        out_specs=[columns((C, CQ), 2), columns((C, VB), 2), full((KC, C)), full((8 * C, C))],
+        out_shape=[sd((C, CROWS), BF), sd((C, ROWS), BF), sd((KC, C), F32), sd((8 * C, C), F32)],
+        scratch_shapes=work_scratch(VB),
+        input_output_aliases={12: 0, 13: 1},
+        compiler_params=LIMIT,
+        name="other_local_blocks",
+    )(counts, feat, rows, frm, dmap, grad, *weights, gsub, gdown, coarse_all, gfeat_all)
+
+
+def border_pack_kernel(feat, grad, out, sems):
+    a = pltpu.make_async_copy(feat.at[:, 0:VB], out.at[:, 0:VB], sems.at[0])
+    b = pltpu.make_async_copy(grad.at[:, 0:CQ], out.at[:, VB:], sems.at[1])
+    a.start()
+    b.start()
+    a.wait()
+    b.wait()
+
+
+def border_pack(feat, grad):
+    return pl.pallas_call(
+        border_pack_kernel,
+        in_specs=[pl.BlockSpec(memory_space=pltpu.HBM), pl.BlockSpec(memory_space=pltpu.HBM)],
+        out_specs=pl.BlockSpec(memory_space=pltpu.VMEM),
+        out_shape=jax.ShapeDtypeStruct((C, WIDE), BF),
+        scratch_shapes=[pltpu.SemaphoreType.DMA((2,))],
+        compiler_params=SMALL,
+        name="pack_border",
+    )(feat, grad)
+
+
+def sum_kernel(pieces, out):
+    rows = pieces.shape[0]
+    span = 4 * PIECE
+    total = jnp.sum(pieces[...].astype(F32).reshape(rows // span, span, 2 * C), axis=0)
+    mine = total[0:PIECE]
+    for i in range(1, 4):
+        mine = mine + total[i * PIECE:(i + 1) * PIECE]
+    tiled = jnp.concatenate([mine] * 8, axis=0).astype(BF)
+    for i in range(rows // (8 * PIECE)):
+        out[i * 8 * PIECE:(i + 1) * 8 * PIECE, :] = tiled
+
+
+def sum_call(pieces):
+    return pl.pallas_call(
+        sum_kernel,
+        grid=(1,),
+        in_specs=[full(pieces.shape)],
+        out_specs=full(pieces.shape),
+        out_shape=jax.ShapeDtypeStruct(pieces.shape, BF),
+        compiler_params=SMALL,
+        name="sum_pieces",
+    )(pieces)
 
 
 def border_kernel(feat, rows, frm, dmap, grad, below, column, above, w_cat, w_t, wd_cat, wd_t, gsub, gdown,
                   coarse_o, gfeat_o, packed_o, mid_o, down_o, up_o, hot, source, spread):
     refs = (feat, rows, frm, dmap, grad, (below, column, above), w_cat, w_t, wd_cat, wd_t, hot, source, spread)
-    coarse, gfeat, dsub, ddown, edge, outward = block_work(True, True, 0, refs)
+    coarse, gfeat, dsub, ddown, edge, outward = block_work(True, 0, refs)
     coarse_o[...] = coarse
     gfeat_o[...] = gfeat
     whole = jnp.concatenate([gsub[...] + dsub, gdown[...] + ddown], axis=0)
@@ -232,7 +308,7 @@
             pltpu.VMEM((KC, VB), BF),
             pltpu.VMEM((KC, 2 * VB), BF),
         ],
-        compiler_params=pltpu.CompilerParams(vmem_limit_bytes=48 << 20),
+        compiler_params=pltpu.CompilerParams(vmem_limit_bytes=26 << 20),
         name="border_block",
     )(feat, rows, frm, dmap, grad, below, column, above, w_cat, w_t, wd_cat, wd_t, gsub, gdown)
 
@@ -257,6 +333,7 @@
         out_specs=[pl.BlockSpec((C, CQ), lambda i: (0, 0)), pl.BlockSpec((C, VB), lambda i: (0, 0))],
         out_shape=[sd((C, CROWS), BF), sd((C, ROWS), BF)],
         input_output_aliases={0: 0, 1: 1},
+        compiler_params=SMALL,
         name="add_incoming",
     )(coarse_all, gfeat_all, coarse, gfeat, total, left, right)
 
@@ -285,6 +362,7 @@
         in_specs=[pl.BlockSpec((HALF, 2 * C), lambda i: (0, 0))],
         out_specs=[full((K, C, C)), full((8, C, C))],
         out_shape=[sd((K, C, C), F32), sd((8, C, C), F32)],
+        compiler_params=SMALL,
         name="unpack_weights",
     )(packed)
 
@@ -300,23 +378,28 @@
     rows, frm, dmap = sub_rows[0, 0], sub_from[0, 0], down_map[0, 0]
     nx, ny = lax.axis_size("gx"), lax.axis_size("gy")
     count = nx * ny
-    border = jnp.concatenate([feat[:, :VB], grad[:, :CB], jnp.zeros((C, CB), BF)], axis=1)
-    column = jnp.stack([ring(border, "gx", 1), border, ring(border, "gx", -1)])
+    border = border_pack(feat, grad)
+    from_before, from_after = ring(border, "gx", 1), ring(border, "gx", -1)
+    counts = counts.reshape(1)
+    coarse_all, gfeat_all, gsub, gdown, *weights = first_call(counts, feat, rows, frm, dmap, grad, w_sub, w_down)
+    from_before, from_after, gsub = lax.optimization_barrier((from_before, from_after, gsub))
+    column = jnp.stack([from_before, border, from_after])
     below, above = ring(column, "gy", 1), ring(column, "gy", -1)
-    coarse_all, gfeat_all, gsub, gdown, w_cat, w_t, wd_cat, wd_t = local_call(
-        counts.reshape(1), feat, rows, frm, dmap, grad, w_sub, w_down)
+    coarse_all, gfeat_all, gsub, gdown = rest_call(
+        counts, feat, rows, frm, dmap, grad, weights, gsub, gdown, coarse_all, gfeat_all)
     coarse, gfeat, packed, mid, down, up = border_call(
-        feat, rows, frm, dmap, grad, below, column, above, w_cat, w_t, wd_cat, wd_t, gsub, gdown)
+        feat, rows, frm, dmap, grad, below, column, above, *weights, gsub, gdown)
+    pieces = lax.all_to_all(packed.reshape(count, PAIRS, 2, 2 * C), ("gx", "gy"), 0, 0, tiled=True)
     from_up, from_down = ring(down, "gy", -1), ring(up, "gy", 1)
     total = mid + from_up.astype(F32) + from_down.astype(F32)
     from_right = ring(total[0].astype(BF), "gx", -1)
     from_left = ring(total[2].astype(BF), "gx", 1)
-    pieces = lax.all_to_all(packed.reshape(count, -1, 2 * C), ("gx", "gy"), 0, 0, tiled=True)
-    summed = jnp.sum(pieces.astype(F32), axis=0).astype(BF)
-    spread = jnp.broadcast_to(summed[None], pieces.shape)
-    gathered = lax.all_to_all(spread, ("gx", "gy"), 0, 0, tiled=True).reshape(-1, 2 * C)
+    pieces, from_right, from_left = lax.optimization_barrier((pieces, from_right, from_left))
+    shape = pieces.shape
+    spread = sum_call(pieces.reshape(count * PIECE, 2 * C))
+    gathered = lax.all_to_all(spread.reshape(shape), ("gx", "gy"), 0, 0, tiled=True).reshape(-1, 2 * C)
+    coarse_out, grad_features = finish_call(coarse_all, gfeat_all, coarse, gfeat, total[1], from_left, from_right)
     grad_w_sub, grad_w_down = weights_call(float(ROWS * count) ** -0.5, gathered)
-    coarse_out, grad_features = finish_call(coarse_all, gfeat_all, coarse, gfeat, total[1], from_left, from_right)
     return coarse_out[None, None], grad_features[None, None], grad_w_sub, grad_w_down
 
 

time: 85.4 us -> 74.6 us (0.87); the launches traced: 85.4 us -> 75.6 us
  waiting for transfers between devices: 28.1 us -> 23.9 us
  local copies, waits for them, and re-layouts: 6.62 us -> 2.94 us
  Pallas kernels: 11.9 us -> 11 us
    ppermute x8, waiting for transfers between devices: 16 us -> 6.93 us  [ring(): return lax.ppermute(block, axis, [(i, (i + step) % n) for i in range(n)])]
    all_to_all x2, waiting for transfers between devices: 12.2 us -> 17 us  [the longest x1 11.1 us: shards(): lax.all_to_all(spread.reshape(shape), ('gx', 'gy'), 0, 0, tiled=True)]
    slice x2 -> x0, local copies, waits for them, and re-layouts: 1.57 us -> none  [the longest x1 0.84 us: shards(): feat[:, :VB]]
    all_to_all x2, starting transfers between devices: 19.1 us -> 17.9 us  [the longest x1 12 us: shards(): lax.all_to_all(packed.reshape(count, PAIRS, 2, 2 * C), ('gx', 'gy'), 0, 0...]
    pallas_call x1 -> x4, Pallas kernels: 1.72 us -> 2.87 us  [the longest x1 1.17 us: first_call(): pl.pallas_call(first_kernel, grid=(1,), in_specs=[pl.BlockSpec(memory_spa...]
    pallas_call x1, Pallas kernels: 1.75 us -> 0.68 us  [finish_call(): pl.pallas_call(finish_kernel, grid=(1,), in_specs=[pl.BlockSpec(memory_sp...]
    pallas_call x1, Pallas kernels: 2.41 us -> 1.46 us  [weights_call(): pl.pallas_call(functools.partial(weights_kernel, scale), grid=(1,), in_sp...]
    broadcast_in_dim x2 -> x0, local copies, waits for them, and re-layouts: 0.87 us -> none  [the longest x1 0.86 us: shards(): spread = jnp.broadcast_to(summed[None], pieces.shape)]
  transfers between devices with their start and end apart: 10 -> 10, of which waited for: 6 -> 4; matrix products, arithmetic and copies ran while one was open for 2% -> 2% of each run, Pallas kernels for 4% -> 4%
where the time goes in v2:
time: 74.6 us; the launch traced here: 75.6 us
  starting transfers between devices  36.3 us (49%)
  waiting for transfers between devices  23.9 us (32%)
  Pallas kernels  11 us (15%)
  local copies, waits for them, and re-layouts  2.94 us (4%)
  between operations  1.45 us (2%)
    ppermute x8, starting transfers between devices, ring(): return lax.ppermute(block, axis, [(i, (i + step) % n) for i in range(n)])  18.4 us
    all_to_all x1, starting transfers between devices, shards(): lax.all_to_all(packed.reshape(count, PAIRS, 2, 2 * C), ('gx', 'gy'), 0, 0...  12 us
    all_to_all x1, waiting for transfers between devices, shards(): lax.all_to_all(spread.reshape(shape), ('gx', 'gy'), 0, 0, tiled=True)  11.1 us
    ppermute x8, waiting for transfers between devices, ring(): return lax.ppermute(block, axis, [(i, (i + step) % n) for i in range(n)])  6.93 us
    pallas_call x1, Pallas kernels, border_call(): pl.pallas_call(border_kernel, grid=(1,), in_specs=[pl.BlockSpec((C, VB),...  5.99 us
    all_to_all x1, waiting for transfers between devices, shards(): lax.all_to_all(packed.reshape(count, PAIRS, 2, 2 * C), ('gx', 'gy'), 0, 0...  5.9 us
    all_to_all x1, starting transfers between devices, shards(): lax.all_to_all(spread.reshape(shape), ('gx', 'gy'), 0, 0, tiled=True)  5.85 us
    unnamed x17, local copies, waits for them, and re-layouts  2.91 us
  transfers between devices with their start and end apart: 10, of which 4 were waited for; matrix products, arithmetic and copies ran while one was open for 2% of the time, Pallas kernels for 4%

profile of v2, /device:TPU:1, one launch (start us, length us, event | category | flops | bytes accessed | tf_op | source)
XLA Modules:
  0.0 75.6 jit_solution(6596266069022954940)
XLA Ops:
  0.6 0.0 copy-start
  0.6 0.9 %copy-done = bf16[1,1,64,2048]{3,2,1,0:T(8,128)(2,1)S(1)} copy-done((bf16[1,1,64,2048]{3,2,1,0:T(8,128)(2,1)S(1)}, bf16[1,1,64,2048]{3,2,1,0:T(8,128)(2,1)}, u32[]{:S(2)}) %copy-start) | copy-done | bytes 262168
  1.6 0.8 %copy-done.2 = bf16[1,1,64,512]{3,2,1,0:T(8,128)(2,1)S(1)} copy-done((bf16[1,1,64,512]{3,2,1,0:T(8,128)(2,1)S(1)}, bf16[1,1,64,512]{3,2,1,0:T(8,128)(2,1)}, u32[]{:S(2)}) %copy-start.2) | copy-done | bytes 65560
  2.5 0.0 copy-start.1
  2.5 0.0 copy-start.3
  2.5 0.0 copy-start.4
  2.5 0.0 copy-start.6
  2.5 7.1 %collective-permute-start.1 = (bf16[64,640]{1,0:T(8,128)(2,1)S(1)}, bf16[64,640]{1,0:T(8,128)(2,1)S(1)}, u32[]{:S(2)}, u32[]{:S(2)}) collective-permute-start(bf16[64,640]{1,0:T(8,128)(2,1)S(1)} %pack_border.1), channel_id=1, source_target_pairs={{0,120},{8,0},{16,8},{24,16},{32,24},{40,32},{48,40},{56,48},{64,5... | collective-permute-start | bytes 245768 | tf_op jit(solution)/shard_map/ppermute | solution.py:372
  9.6 0.0 collective-permute-start
  9.6 1.1 %copy_bitcast_fusion = (s32[27,2048]{1,0:T(8,128)S(1)}, s32[27,2048]{1,0:T(8,128)S(1)}) fusion(s32[1,1,27,2048]{3,1,2,0:T(1,128)S(1)} %copy-done.7, s32[1,1,27,2048]{3,1,2,0:T(1,128)} %param.10), kind=kLoop, calls=%fused_computation.1 | loop fusion | bytes 884736
  11.4 1.2 %first_local_block.1 = (bf16[64,512]{1,0:T(8,128)(2,1)}, bf16[64,2048]{1,0:T(8,128)(2,1)}, f32[1728,64]{1,0:T(8,128)S(1)}, f32[512,64]{1,0:T(8,128)S(1)}, bf16[6...) custom-call(s32[1]{0:T(128)} %bitcast.23.counts, ...), custom_call_target="tpu_custom_call" | custom-call | tf_op jit(solution)/shard_map/first_local_block/pallas_call | solution.py:191
  12.6 0.0 collective-permute-done.1
  12.6 3.6 %collective-permute-done = bf16[64,640]{1,0:T(8,128)(2,1)S(1)} collective-permute-done((bf16[64,640]{1,0:T(8,128)(2,1)S(1)}, bf16[64,640]{1,0:T(8,128)(2,1)S(1)}, u32[]{:S(2)}, u32[]{:S(2)}) %collective-permute-start) | collective-permute-done | bytes 81952 | tf_op jit(solution)/shard_map/ppermute | solution.py:372
  16.3 2.1 %collective-permute-start.3 = (bf16[3,64,640]{2,1,0:T(8,128)(2,1)S(1)}, bf16[3,64,640]{2,1,0:T(8,128)(2,1)S(1)}, u32[]{:S(2)}, u32[]{:S(2)}) collective-permute-start(bf16[3,64,640]{2,1,0:T(8,128)(2,1)S(1)} %pad_maximum_fusion.column), channel_id=1, source_target_pairs={{0,7},{1,0},{2,1},{3,2},{4,3},{5,4},{6,5},{7,6},{8,15},{9,8},{10,9... | collective-permute-start | bytes 737288 | tf_op jit(solution)/shard_map/ppermute | solution.py:372
  18.4 1.1 %collective-permute-start.2 = (bf16[3,64,640]{2,1,0:T(8,128)(2,1)S(1)}, bf16[3,64,640]{2,1,0:T(8,128)(2,1)S(1)}, u32[]{:S(2)}, u32[]{:S(2)}) collective-permute-start(bf16[3,64,640]{2,1,0:T(8,128)(2,1)S(1)} %pad_maximum_fusion.column), channel_id=1, source_target_pairs={{0,1},{1,2},{2,3},{3,4},{4,5},{5,6},{6,7},{7,0},{8,9},{9,10},{10,1... | collective-permute-start | bytes 737288 | tf_op jit(solution)/shard_map/ppermute | solution.py:372
  19.5 0.9 %other_local_blocks.1 = (bf16[64,512]{1,0:T(8,128)(2,1)}, bf16[64,2048]{1,0:T(8,128)(2,1)}, f32[1728,64]{1,0:T(8,128)S(1)}, f32[512,64]{1,0:T(8,128)S(1)}) custom-call(s32[1]{0:T(128)} %bitcast.24.counts, bf16[64,2048]{1,0:T(8,128)(2,1)S(1)} %bitcast.27, s32[27,2048]{1,0:T(8,128)S(1)} %get-tuple-element.65.rows, ...), custom_call_target="tpu_custom_call", output_to_operand_aliasing={{0}: (12, {}), {1}: (13, {})} | custom-call | tf_op jit(solution)/shard_map/other_local_blocks/pallas_call | solution.py:207
  20.4 3.3 %collective-permute-done.3.above = bf16[3,64,640]{2,1,0:T(8,128)(2,1)S(1)} collective-permute-done((bf16[3,64,640]{2,1,0:T(8,128)(2,1)S(1)}, bf16[3,64,640]{2,1,0:T(8,128)(2,1)S(1)}, u32[]{:S(2)}, u32[]{:S(2)}) %collective-permute-start.3) | collective-permute-done | bytes 245792 | tf_op jit(solution)/shard_map/ppermute | solution.py:372
  23.7 6.0 %border_block.1 = (f32[64,128]{1,0:T(8,128)S(1)}, f32[64,512]{1,0:T(8,128)S(1)}, bf16[1280,128]{1,0:T(8,128)(2,1)}, f32[3,64,640]{2,1,0:T(8,128)S(1)}, bf16[3,64...) custom-call(bf16[64,2048]{1,0:T(8,128)(2,1)S(1)} %bitcast.28, s32[27,2048]{1,0:T(8,128)S(1)} %get-tuple-element.65.rows, ...), custom_call_target="tpu_custom_call" | custom-call | tf_op jit(solution)/shard_map/border_block/pallas_call | solution.py:285
  29.7 2.3 %collective-permute-start.4 = (bf16[3,64,640]{2,1,0:T(8,128)(2,1)S(1)}, bf16[3,64,640]{2,1,0:T(8,128)(2,1)S(1)}, u32[]{:S(2)}, u32[]{:S(2)}) collective-permute-start(bf16[3,64,640]{2,1,0:T(8,128)(2,1)S(1)} %get-tuple-element.50), channel_id=1, source_target_pairs={{0,7},{1,0},{2,1},{3,2},{4,3},{5,4},{6,5},{7,6},{8,15},{9,8},{10,9... | collective-permute-start | bytes 737288 | tf_op jit(solution)/shard_map/ppermute | solution.py:372
  32.0 12.0 %all-to-all-start = ((bf16[128,5,2,128]{3,2,1,0:T(2,128)(2,1)}), bf16[128,5,2,128]{3,2,1,0:T(2,128)(2,1)S(1)}, u32[]{:S(2)}, u32[]{:S(2)}) async-start(bf16[128,5,2,128]{3,2,1,0:T(2,128)(2,1)} %bitcast.8), calls=%async_computation | async-start | bytes 655360 | tf_op jit(solution)/shard_map/all_to_all | solution.py:392
  44.0 0.0 collective-permute-done.4
  44.0 0.0 collective-permute-done.5
  44.0 0.1 fusion
  44.2 1.5 %collective-permute-start.7 = (bf16[64,640]{1,0:T(8,128)(2,1)S(1)}, bf16[64,640]{1,0:T(8,128)(2,1)S(1)}, u32[]{:S(2)}, u32[]{:S(2)}) collective-permute-start(bf16[64,640]{1,0:T(8,128)(2,1)S(1)} %get-tuple-element.62), channel_id=1, source_target_pairs={{0,8},{8,16},{16,24},{24,32},{32,40},{40,48},{48,56},{56,64},{64,7... | collective-permute-start | bytes 245768 | tf_op jit(solution)/shard_map/ppermute | solution.py:372
  45.6 4.3 %collective-permute-start.6 = (bf16[64,640]{1,0:T(8,128)(2,1)S(1)}, bf16[64,640]{1,0:T(8,128)(2,1)S(1)}, u32[]{:S(2)}, u32[]{:S(2)}) collective-permute-start(bf16[64,640]{1,0:T(8,128)(2,1)S(1)} %get-tuple-element.63), channel_id=1, source_target_pairs={{0,120},{8,0},{16,8},{24,16},{32,24},{40,32},{48,40},{56,48},{64,5... | collective-permute-start | bytes 245768 | tf_op jit(solution)/shard_map/ppermute | solution.py:372
  49.9 5.9 %all-to-all-done = bf16[128,5,2,128]{3,2,1,0:T(2,128)(2,1)S(1)} async-done(((bf16[128,5,2,128]{3,2,1,0:T(2,128)(2,1)}), bf16[128,5,2,128]{3,2,1,0:T(2,128)(2,1)S(1)}, u32[]{:S(2)}, u32[]{:S(2)}) %all-to-all-start) | async-done | bytes 327712 | tf_op jit(solution)/shard_map/all_to_all | solution.py:392
  55.8 0.0 collective-permute-done.7.left
  55.8 0.8 %sum_pieces.1 = bf16[1280,128]{1,0:T(8,128)(2,1)} custom-call(bf16[1280,128]{1,0:T(8,128)(2,1)S(1)} %bitcast.29), custom_call_target="tpu_custom_call" | custom-call | tf_op jit(solution)/shard_map/sum_pieces/pallas_call | solution.py:255
  56.6 5.8 %all-to-all-start.1 = ((bf16[128,5,2,128]{3,2,1,0:T(2,128)(2,1)}), bf16[128,5,2,128]{3,2,1,0:T(2,128)(2,1)S(1)}, u32[]{:S(2)}, u32[]{:S(2)}) async-start(bf16[128,5,2,128]{3,2,1,0:T(2,128)(2,1)} %bitcast.14), calls=%async_computation.1 | async-start | bytes 655360 | tf_op jit(solution)/shard_map/all_to_all | solution.py:400
  62.5 0.7 add_incoming.1
  63.1 11.1 %all-to-all-done.1 = bf16[128,5,2,128]{3,2,1,0:T(2,128)(2,1)S(1)} async-done(((bf16[128,5,2,128]{3,2,1,0:T(2,128)(2,1)}), bf16[128,5,2,128]{3,2,1,0:T(2,128)(2,1)S(1)}, u32[]{:S(2)}, u32[]{:S(2)}) %all-to-all-start.1) | async-done | bytes 327712 | tf_op jit(solution)/shard_map/all_to_all | solution.py:400
  74.2 1.5 %unpack_weights.1 = (f32[27,64,64]{2,1,0:T(8,128)}, f32[8,64,64]{2,1,0:T(8,128)}) custom-call(bf16[1280,128]{1,0:T(8,128)(2,1)S(1)} %bitcast.30), custom_call_target="tpu_custom_call" | custom-call | tf_op jit(solution)/shard_map/unpack_weights/pallas_call | solution.py:359
  (16 shorter events, 0.1 us)
Async XLA Ops:
  0.6 1.0 %copy-start = (bf16[1,1,64,2048]{3,2,1,0:T(8,128)(2,1)S(1)}, bf16[1,1,64,2048]{3,2,1,0:T(8,128)(2,1)}, u32[]{:S(2)}) copy-start(bf16[1,1,64,2048]{3,2,1,0:T(8,128)(2,1)} %param.8) | copy-start | bytes 786436
  1.6 0.8 %copy-start.2 = (bf16[1,1,64,512]{3,2,1,0:T(8,128)(2,1)S(1)}, bf16[1,1,64,512]{3,2,1,0:T(8,128)(2,1)}, u32[]{:S(2)}) copy-start(bf16[1,1,64,512]{3,2,1,0:T(8,128)(2,1)} %param.15) | copy-start | bytes 196612
  2.4 7.2 %copy-start.7 = (s32[1,1,27,2048]{3,1,2,0:T(1,128)S(1)}, s32[1,1,27,2048]{3,1,2,0:T(1,128)}, u32[]{:S(2)}) copy-start(s32[1,1,27,2048]{3,1,2,0:T(1,128)} %param.11) | copy-start | bytes 663556
  2.5 8.9 %copy-start.1 = (bf16[1,1,64,2048]{3,2,1,0:T(8,128)(2,1)S(1)}, bf16[1,1,64,2048]{3,2,1,0:T(8,128)(2,1)}, u32[]{:S(2)}) copy-start(bf16[1,1,64,2048]{3,2,1,0:T(8,128)(2,1)} %param.8) | copy-start | bytes 786436
  2.5 8.9 %copy-start.3 = (bf16[1,1,64,512]{3,2,1,0:T(8,128)(2,1)S(1)}, bf16[1,1,64,512]{3,2,1,0:T(8,128)(2,1)}, u32[]{:S(2)}) copy-start(bf16[1,1,64,512]{3,2,1,0:T(8,128)(2,1)} %param.15) | copy-start | bytes 196612
  2.5 8.9 %copy-start.4 = (bf16[27,64,64]{2,1,0:T(8,128)(2,1)S(1)}, bf16[27,64,64]{2,1,0:T(8,128)(2,1)}, u32[]{:S(2)}) copy-start(bf16[27,64,64]{2,1,0:T(8,128)(2,1)} %w_sub.1) | copy-start | bytes 663556
  2.5 8.9 %copy-start.6 = (bf16[8,64,64]{2,1,0:T(8,128)(2,1)S(1)}, bf16[8,64,64]{2,1,0:T(8,128)(2,1)}, u32[]{:S(2)}) copy-start(bf16[8,64,64]{2,1,0:T(8,128)(2,1)} %w_down.1) | copy-start | bytes 196612
  2.5 10.1 %collective-permute-start.1 = (bf16[64,640]{1,0:T(8,128)(2,1)S(1)}, bf16[64,640]{1,0:T(8,128)(2,1)S(1)}, u32[]{:S(2)}, u32[]{:S(2)}) collective-permute-start(bf16[64,640]{1,0:T(8,128)(2,1)S(1)} %pack_border.1), channel_id=1, source_target_pairs={{0,120},{8,0},{16,8},{24,16},{32,24},{40,32},{48,40},{56,48},{64,5... | collective-permute-start | bytes 245768 | tf_op jit(solution)/shard_map/ppermute | solution.py:372
  9.6 6.6 %collective-permute-start = (bf16[64,640]{1,0:T(8,128)(2,1)S(1)}, bf16[64,640]{1,0:T(8,128)(2,1)S(1)}, u32[]{:S(2)}, u32[]{:S(2)}) collective-permute-start(bf16[64,640]{1,0:T(8,128)(2,1)S(1)} %pack_border.1), channel_id=1, source_target_pairs={{0,8},{8,16},{16,24},{24,32},{32,40},{40,48},{48,56},{56,64},{64,7... | collective-permute-start | bytes 245768 | tf_op jit(solution)/shard_map/ppermute | solution.py:372
  9.6 1.8 %copy-start.5 = (s32[1,1,2,2048]{3,2,1,0:T(2,128)S(1)}, s32[1,1,2,2048]{3,2,1,0:T(2,128)}, u32[]{:S(2)}) copy-start(s32[1,1,2,2048]{3,2,1,0:T(2,128)} %param.12) | copy-start | bytes 49156
  16.3 7.4 %collective-permute-start.3 = (bf16[3,64,640]{2,1,0:T(8,128)(2,1)S(1)}, bf16[3,64,640]{2,1,0:T(8,128)(2,1)S(1)}, u32[]{:S(2)}, u32[]{:S(2)}) collective-permute-start(bf16[3,64,640]{2,1,0:T(8,128)(2,1)S(1)} %pad_maximum_fusion.column), channel_id=1, source_target_pairs={{0,7},{1,0},{2,1},{3,2},{4,3},{5,4},{6,5},{7,6},{8,15},{9,8},{10,9... | collective-permute-start | bytes 737288 | tf_op jit(solution)/shard_map/ppermute | solution.py:372
  18.4 5.3 %collective-permute-start.2 = (bf16[3,64,640]{2,1,0:T(8,128)(2,1)S(1)}, bf16[3,64,640]{2,1,0:T(8,128)(2,1)S(1)}, u32[]{:S(2)}, u32[]{:S(2)}) collective-permute-start(bf16[3,64,640]{2,1,0:T(8,128)(2,1)S(1)} %pad_maximum_fusion.column), channel_id=1, source_target_pairs={{0,1},{1,2},{2,3},{3,4},{4,5},{5,6},{6,7},{7,0},{8,9},{9,10},{10,1... | collective-permute-start | bytes 737288 | tf_op jit(solution)/shard_map/ppermute | solution.py:372
  29.7 14.4 %collective-permute-start.4 = (bf16[3,64,640]{2,1,0:T(8,128)(2,1)S(1)}, bf16[3,64,640]{2,1,0:T(8,128)(2,1)S(1)}, u32[]{:S(2)}, u32[]{:S(2)}) collective-permute-start(bf16[3,64,640]{2,1,0:T(8,128)(2,1)S(1)} %get-tuple-element.50), channel_id=1, source_target_pairs={{0,7},{1,0},{2,1},{3,2},{4,3},{5,4},{6,5},{7,6},{8,15},{9,8},{10,9... | collective-permute-start | bytes 737288 | tf_op jit(solution)/shard_map/ppermute | solution.py:372
  32.0 12.0 %collective-permute-start.5 = (bf16[3,64,640]{2,1,0:T(8,128)(2,1)S(1)}, bf16[3,64,640]{2,1,0:T(8,128)(2,1)S(1)}, u32[]{:S(2)}, u32[]{:S(2)}) collective-permute-start(bf16[3,64,640]{2,1,0:T(8,128)(2,1)S(1)} %get-tuple-element.51), channel_id=1, source_target_pairs={{0,1},{1,2},{2,3},{3,4},{4,5},{5,6},{6,7},{7,0},{8,9},{9,10},{10,1... | collective-permute-start | bytes 737288 | tf_op jit(solution)/shard_map/ppermute | solution.py:372
  32.0 23.8 %all-to-all-start = ((bf16[128,5,2,128]{3,2,1,0:T(2,128)(2,1)}), bf16[128,5,2,128]{3,2,1,0:T(2,128)(2,1)S(1)}, u32[]{:S(2)}, u32[]{:S(2)}) async-start(bf16[128,5,2,128]{3,2,1,0:T(2,128)(2,1)} %bitcast.8), calls=%async_computation | async-start | bytes 655360 | tf_op jit(solution)/shard_map/all_to_all | solution.py:392
  44.2 11.6 %collective-permute-start.7 = (bf16[64,640]{1,0:T(8,128)(2,1)S(1)}, bf16[64,640]{1,0:T(8,128)(2,1)S(1)}, u32[]{:S(2)}, u32[]{:S(2)}) collective-permute-start(bf16[64,640]{1,0:T(8,128)(2,1)S(1)} %get-tuple-element.62), channel_id=1, source_target_pairs={{0,8},{8,16},{16,24},{24,32},{32,40},{40,48},{48,56},{56,64},{64,7... | collective-permute-start | bytes 245768 | tf_op jit(solution)/shard_map/ppermute | solution.py:372
  45.6 10.2 %collective-permute-start.6 = (bf16[64,640]{1,0:T(8,128)(2,1)S(1)}, bf16[64,640]{1,0:T(8,128)(2,1)S(1)}, u32[]{:S(2)}, u32[]{:S(2)}) collective-permute-start(bf16[64,640]{1,0:T(8,128)(2,1)S(1)} %get-tuple-element.63), channel_id=1, source_target_pairs={{0,120},{8,0},{16,8},{24,16},{32,24},{40,32},{48,40},{56,48},{64,5... | collective-permute-start | bytes 245768 | tf_op jit(solution)/shard_map/ppermute | solution.py:372
  56.6 17.6 %all-to-all-start.1 = ((bf16[128,5,2,128]{3,2,1,0:T(2,128)(2,1)}), bf16[128,5,2,128]{3,2,1,0:T(2,128)(2,1)S(1)}, u32[]{:S(2)}, u32[]{:S(2)}) async-start(bf16[128,5,2,128]{3,2,1,0:T(2,128)(2,1)} %bitcast.14), calls=%async_computation.1 | async-start | bytes 655360 | tf_op jit(solution)/shard_map/all_to_all | solution.py:400

commit v3 on v2

v3 whole, which is shorter than its diff:
```python
import functools
import jax
import jax.numpy as jnp
from jax import lax
from jax.experimental import pallas as pl
from jax.sharding import PartitionSpec as P
from jax.experimental.pallas import tpu as pltpu

VB = 512
ROWS = 2048
CROWS = 512
CB = 64
C = 64
K = 27
KC = K * C
L = 256
H = VB // L
CQ = 128
EDGE = 640
WIDE = VB + 2 * CB
SUB_ROWS = (K + 1) // 2 * C
USED = SUB_ROWS + 4 * C
PAIRS = 5
PIECE = 2 * PAIRS
BF = jnp.bfloat16
F32 = jnp.float32
DIRS = [3 * (k // 9) + k // 3 % 3 for k in range(K)]


def mm(a, b):
    return jnp.dot(a, b, preferred_element_type=F32)


def mm_nt(a, b):
    return lax.dot_general(a, b, (((1,), (1,)), ((), ())), preferred_element_type=F32)


def pick(cond):
    return jnp.where(cond, jnp.ones((), BF), jnp.zeros((), BF))


def table(remote, base, rows, frm):
    row_v = rows[:, 0, :]
    frm_v = frm[:, 0, :]
    if remote:
        joint = jnp.where(frm_v == 4, row_v, jnp.where(frm_v == 9, -1, row_v + VB))
    else:
        joint = jnp.where(frm_v == 4, row_v - base, -1)
    high = joint >> (L.bit_length() - 1)
    low = jnp.where(joint < 0, -1, joint & (L - 1)).astype(F32)
    return high, low


def forward_work(remote, base, feat, rows, frm, dmap, grad, halo, w_cat, wd_cat, wd_t, source):
    high, low = table(remote, base, rows, frm)
    low = low.astype(BF)
    low_ids = lax.broadcasted_iota(jnp.int32, (L, VB), 0).astype(F32).astype(BF)
    local = jnp.concatenate([feat[:, i * L:(i + 1) * L] for i in range(H)], axis=0)
    for k in range(K):
        one_hot = pick(low[k:k + 1, :] == low_ids)
        parts = [mm(local, one_hot)]
        if remote and DIRS[k] != 4:
            slab = halo[DIRS[k] % 3][DIRS[k] // 3, :, 0:VB]
            slab = jnp.concatenate([slab[:, i * L:(i + 1) * L] for i in range(H)], axis=0)
            parts.append(mm(slab, one_hot))
        high_k = high[k:k + 1, :]
        pieces = [part[i * C:(i + 1) * C, :] for part in parts for i in range(H)]
        got = pieces[0]
        for i in range(1, len(pieces)):
            got = jnp.where(high_k == i, pieces[i], got)
        source[k * C:(k + 1) * C, :] = got.astype(BF)
    pre = mm(w_cat[...], source[...])
    sig = jax.nn.sigmoid(pre)
    hidden = (pre * sig).astype(BF)
    target = dmap[0:1, :]
    kind = dmap[1:2, :]
    coarse_rel = jnp.where(target < CROWS, target - base // 4, -1)
    pick_own = pick(coarse_rel == lax.broadcasted_iota(jnp.int32, (CQ, VB), 0))
    zero = jnp.zeros((), BF)
    kinds = [kind == i for i in range(8)]
    up = mm(grad[...], pick_own)
    if remote:
        edge_grad = [halo[d % 3][d // 3, :, VB:VB + CB] for d in range(9)] + [jnp.zeros((C, EDGE - 9 * CB), BF)]
        up = up + mm(jnp.concatenate(edge_grad, axis=1), pick_edges(target))
    up = up.astype(BF)
    picked_g = jnp.concatenate([jnp.where(m, up, zero) for m in kinds], axis=0)
    grad_hidden = mm(wd_t[...], picked_g)
    grad_pre = (grad_hidden * sig * (1.0 + pre * (1.0 - sig))).astype(BF)
    grad_sub = mm_nt(grad_pre, source[...])
    grad_down = mm_nt(picked_g, hidden)
    picked_h = jnp.concatenate([jnp.where(m, hidden, zero) for m in kinds], axis=0)
    contrib = mm(wd_cat[...], picked_h)
    c_hi = contrib.astype(BF)
    c_lo = (contrib - c_hi.astype(F32)).astype(BF)
    split = jnp.concatenate([c_hi, c_lo], axis=0)
    own = mm_nt(split, pick_own)
    return own[:C] + own[C:], grad_pre, grad_sub, grad_down, split


def pick_edges(target):
    return pick((target - CROWS) == lax.broadcasted_iota(jnp.int32, (EDGE, VB), 0))


def scatter_work(remote, base, rows, frm, grad_pre, w_t, spread):
    high, low = table(remote, base, rows, frm)
    low_t = jnp.concatenate([low, jnp.zeros((32 - K, VB), F32)], axis=0).T.astype(BF)
    lane_ids = lax.broadcasted_iota(jnp.int32, (VB, L), 1).astype(F32).astype(BF)
    zero = jnp.zeros((), BF)
    for k in range(K):
        high_k = high[k:k + 1, :]
        count = 2 * H if (remote and DIRS[k] != 4) else H
        masked = jnp.concatenate([jnp.where(high_k == i, grad_pre, zero) for i in range(count)], axis=0)
        out = mm(masked, pick(low_t[:, k:k + 1] == lane_ids)).astype(BF)
        for i in range(count):
            spread[k * C:(k + 1) * C, i * L:(i + 1) * L] = out[i * C:(i + 1) * C, :]
    return mm(w_t[...], spread[:, 0:VB])


def prepare_weights(w_sub, w_down, w_cat, w_t, wd_cat, wd_t):
    w_cat[...] = jnp.concatenate([w_sub[k] for k in range(K)], axis=1)
    w_t[...] = w_sub[...].reshape(KC, C).T
    wd_cat[...] = jnp.concatenate([w_down[k] for k in range(8)], axis=1)
    wd_t[...] = w_down[...].reshape(8 * C, C).T


def one_local(block, counts, feat, rows, frm, dmap, grad, w_cat, wd_cat, wd_t, outs, source):
    coarse_o, gpre_o, gsub_o, gdown_o = outs

    @pl.when(block < counts[0])
    def _():
        coarse, gpre, gsub, gdown, _ = forward_work(
            False, block * VB, feat, rows, frm, dmap, grad, None, w_cat, wd_cat, wd_t, source)
        coarse_o[...] = coarse.astype(BF)
        gpre_o[...] = gpre
        gsub_o[...] += gsub
        gdown_o[...] += gdown

    @pl.when(block >= counts[0])
    def _():
        coarse_o[...] = jnp.zeros_like(coarse_o)


def first_kernel(counts, feat, rows, frm, dmap, grad, w_sub, w_down,
                 coarse_o, gpre_o, gsub_o, gdown_o, w_cat, w_t, wd_cat, wd_t, source):
    prepare_weights(w_sub, w_down, w_cat, w_t, wd_cat, wd_t)
    gsub_o[...] = jnp.zeros_like(gsub_o)
    gdown_o[...] = jnp.zeros_like(gdown_o)
    one_local(1, counts, feat, rows, frm, dmap, grad, w_cat, wd_cat, wd_t,
              (coarse_o, gpre_o, gsub_o, gdown_o), source)


def rest_kernel(counts, feat, rows, frm, dmap, grad, w_cat, wd_cat, wd_t, gsub, gdown, coarse_a, gpre_a,
                coarse_o, gpre_o, gsub_o, gdown_o, source):
    i = pl.program_id(0)

    @pl.when(i == 0)
    def _():
        gsub_o[...] = gsub[...]
        gdown_o[...] = gdown[...]

    one_local(i + 2, counts, feat, rows, frm, dmap, grad, w_cat, wd_cat, wd_t,
              (coarse_o, gpre_o, gsub_o, gdown_o), source)


def local_scatter_kernel(counts, rows, frm, gpre, w_t, gfeat_o, spread):
    block = pl.program_id(0) + 1

    @pl.when(block < counts[0])
    def _():
        gfeat_o[...] = scatter_work(False, block * VB, rows, frm, gpre[...], w_t, spread).astype(BF)

    @pl.when(block >= counts[0])
    def _():
        gfeat_o[...] = jnp.zeros_like(gfeat_o)


def full(shape):
    return pl.BlockSpec(shape, lambda i: (0,) * len(shape))


def columns(shape, first):
    return pl.BlockSpec(shape, lambda i: (0, i + first))


def index_columns(first):
    return pl.BlockSpec((K, 1, VB), lambda i: (0, 0, i + first))


def table_specs(first):
    return [columns((C, VB), first), index_columns(first), index_columns(first),
            columns((2, VB), first), columns((C, CQ), first)]


LIMIT = pltpu.CompilerParams(vmem_limit_bytes=20 << 20)
SMALL = pltpu.CompilerParams(vmem_limit_bytes=8 << 20)
SOURCE = pltpu.VMEM((KC, VB), BF)


def sd(shape, dtype):
    return jax.ShapeDtypeStruct(shape, dtype)


def first_call(counts, feat, rows, frm, dmap, grad, w_sub, w_down):
    weights = [(C, KC), (C, KC), (C, 8 * C), (C, 8 * C)]
    return pl.pallas_call(
        first_kernel,
        grid=(1,),
        in_specs=[pl.BlockSpec(memory_space=pltpu.SMEM)] + table_specs(1) + [full((K, C, C)), full((8, C, C))],
        out_specs=[columns((C, CQ), 1), columns((C, VB), 1), full((C, KC)), full((8 * C, C))]
        + [full(w) for w in weights],
        out_shape=[sd((C, CROWS), BF), sd((C, ROWS), BF), sd((C, KC), F32), sd((8 * C, C), F32)]
        + [sd(w, BF) for w in weights],
        scratch_shapes=[SOURCE],
        compiler_params=LIMIT,
        name="first_local_block",
    )(counts, feat, rows, frm, dmap, grad, w_sub, w_down)


def rest_call(counts, feat, rows, frm, dmap, grad, w_cat, wd_cat, wd_t, gsub, gdown, coarse_all, gpre_all):
    return pl.pallas_call(
        rest_kernel,
        grid=(2,),
        in_specs=[pl.BlockSpec(memory_space=pltpu.SMEM)] + table_specs(2)
        + [full((C, KC)), full((C, 8 * C)), full((C, 8 * C)), full((C, KC)), full((8 * C, C)),
           pl.BlockSpec(memory_space=pl.ANY), pl.BlockSpec(memory_space=pl.ANY)],
        out_specs=[columns((C, CQ), 2), columns((C, VB), 2), full((C, KC)), full((8 * C, C))],
        out_shape=[sd((C, CROWS), BF), sd((C, ROWS), BF), sd((C, KC), F32), sd((8 * C, C), F32)],
        scratch_shapes=[SOURCE],
        input_output_aliases={11: 0, 12: 1},
        compiler_params=LIMIT,
        name="other_local_blocks",
    )(counts, feat, rows, frm, dmap, grad, w_cat, wd_cat, wd_t, gsub, gdown, coarse_all, gpre_all)


def local_scatter_call(counts, rows, frm, gpre_all, w_t):
    return pl.pallas_call(
        local_scatter_kernel,
        grid=(3,),
        in_specs=[pl.BlockSpec(memory_space=pltpu.SMEM), index_columns(1), index_columns(1),
                  columns((C, VB), 1), full((C, KC))],
        out_specs=columns((C, VB), 1),
        out_shape=sd((C, ROWS), BF),
        scratch_shapes=[SOURCE],
        compiler_params=LIMIT,
        name="local_scatter_blocks",
    )(counts, rows, frm, gpre_all, w_t)


def border_pack_kernel(feat, grad, out, sems):
    a = pltpu.make_async_copy(feat.at[:, 0:VB], out.at[:, 0:VB], sems.at[0])
    b = pltpu.make_async_copy(grad.at[:, 0:CQ], out.at[:, VB:], sems.at[1])
    a.start()
    b.start()
    a.wait()
    b.wait()


def border_pack(feat, grad):
    return pl.pallas_call(
        border_pack_kernel,
        in_specs=[pl.BlockSpec(memory_space=pltpu.HBM), pl.BlockSpec(memory_space=pltpu.HBM)],
        out_specs=pl.BlockSpec(memory_space=pltpu.VMEM),
        out_shape=jax.ShapeDtypeStruct((C, WIDE), BF),
        scratch_shapes=[pltpu.SemaphoreType.DMA((2,))],
        compiler_params=SMALL,
        name="pack_border",
    )(pltpu.with_memory_space_constraint(feat, pltpu.HBM), pltpu.with_memory_space_constraint(grad, pltpu.HBM))


def sum_kernel(pieces, out):
    rows = pieces.shape[0]
    span = 4 * PIECE
    total = jnp.sum(pieces[...].astype(F32).reshape(rows // span, span, 2 * C), axis=0)
    mine = total[0:PIECE]
    for i in range(1, 4):
        mine = mine + total[i * PIECE:(i + 1) * PIECE]
    tiled = jnp.concatenate([mine] * 8, axis=0).astype(BF)
    for i in range(rows // (8 * PIECE)):
        out[i * 8 * PIECE:(i + 1) * 8 * PIECE, :] = tiled


def sum_call(pieces):
    return pl.pallas_call(
        sum_kernel,
        grid=(1,),
        in_specs=[full(pieces.shape)],
        out_specs=full(pieces.shape),
        out_shape=jax.ShapeDtypeStruct(pieces.shape, BF),
        compiler_params=SMALL,
        name="sum_pieces",
    )(pieces)


def border_kernel(feat, rows, frm, dmap, grad, below, column, above, w_cat, wd_cat, wd_t, gsub, gdown,
                  coarse_o, packed_o, gpre_o, split_o, source):
    coarse, gpre, dsub, ddown, split = forward_work(
        True, 0, feat, rows, frm, dmap, grad, (below, column, above), w_cat, wd_cat, wd_t, source)
    coarse_o[...] = coarse
    gpre_o[...] = gpre
    split_o[...] = split
    total = gsub[...] + dsub
    for t in range(K // 2):
        packed_o[t * C:(t + 1) * C, :] = total[:, t * 2 * C:(t + 1) * 2 * C].astype(BF)
    last = jnp.concatenate([total[:, KC - C:], jnp.zeros((C, C), F32)], axis=1)
    packed_o[K // 2 * C:SUB_ROWS, :] = last.astype(BF)
    down = gdown[...] + ddown
    packed_o[SUB_ROWS:USED, :] = jnp.concatenate([down[:4 * C], down[4 * C:]], axis=1).astype(BF)
    packed_o[USED:, :] = jnp.zeros((packed_o.shape[0] - USED, 2 * C), BF)


def border_call(count, feat, rows, frm, dmap, grad, below, column, above, w_cat, wd_cat, wd_t, gsub, gdown):
    slab = full((3, C, WIDE))
    return pl.pallas_call(
        border_kernel,
        grid=(1,),
        in_specs=table_specs(0) + [slab, slab, slab, full((C, KC)), full((C, 8 * C)), full((C, 8 * C)),
                                   full((C, KC)), full((8 * C, C))],
        out_specs=[full((C, CQ)), full((count * PIECE, 2 * C)), full((C, VB)), full((2 * C, VB))],
        out_shape=[sd((C, CQ), F32), sd((count * PIECE, 2 * C), BF), sd((C, VB), BF), sd((2 * C, VB), BF)],
        scratch_shapes=[SOURCE],
        compiler_params=LIMIT,
        name="border_block",
    )(feat, rows, frm, dmap, grad, below, column, above, w_cat, wd_cat, wd_t, gsub, gdown)


def border_scatter_kernel(rows, frm, dmap, gpre, split, w_t, gfeat_o, mid_o, down_o, up_o, spread):
    gfeat_o[...] = scatter_work(True, 0, rows, frm, gpre[...], w_t, spread)
    both = mm_nt(split[...], pick_edges(dmap[0:1, :]))
    edge = both[:C] + both[C:]
    for d in range(9):
        out = (down_o, mid_o, up_o)[d % 3]
        ks = [k for k in range(K) if DIRS[k] == d]
        a, b = ks[0] * C, (ks[-1] + 1) * C
        outward = jnp.zeros((C, VB), F32) if d == 4 else mm(w_t[:, a:b], spread[a:b, VB:2 * VB])
        out[d // 3, :, 0:VB] = outward.astype(out.dtype)
        tail = jnp.concatenate([edge[:, d * CB:(d + 1) * CB], jnp.zeros((C, CB), F32)], axis=1)
        out[d // 3, :, VB:] = tail.astype(out.dtype)


def border_scatter_call(rows, frm, dmap, gpre, split, w_t):
    slab = (3, C, WIDE)
    return pl.pallas_call(
        border_scatter_kernel,
        grid=(1,),
        in_specs=[index_columns(0), index_columns(0), columns((2, VB), 0), full((C, VB)), full((2 * C, VB)),
                  full((C, KC))],
        out_specs=[full((C, VB)), full(slab), full(slab), full(slab)],
        out_shape=[sd((C, VB), F32), sd(slab, F32), sd(slab, BF), sd(slab, BF)],
        scratch_shapes=[pltpu.VMEM((KC, 2 * VB), BF)],
        compiler_params=LIMIT,
        name="border_scatter_block",
    )(rows, frm, dmap, gpre, split, w_t)


def finish_kernel(coarse_i, gfeat_i, coarse, gfeat, total, left, right, coarse_o, gfeat_o):
    inc = total[...] + left[...].astype(F32) + right[...].astype(F32)
    gfeat_o[...] = (gfeat[...] + inc[:, 0:VB]).astype(BF)
    coarse_o[:, 0:CB] = (coarse[:, 0:CB] + inc[:, VB:VB + CB]).astype(BF)
    coarse_o[:, CB:] = coarse[:, CB:].astype(BF)


def finish_call(coarse_all, gfeat_all, coarse, gfeat, total, left, right):
    return pl.pallas_call(
        finish_kernel,
        grid=(1,),
        in_specs=[
            pl.BlockSpec(memory_space=pl.ANY),
            pl.BlockSpec(memory_space=pl.ANY),
            full((C, CQ)), full((C, VB)), full((C, WIDE)), full((C, WIDE)), full((C, WIDE)),
        ],
        out_specs=[pl.BlockSpec((C, CQ), lambda i: (0, 0)), pl.BlockSpec((C, VB), lambda i: (0, 0))],
        out_shape=[sd((C, CROWS), BF), sd((C, ROWS), BF)],
        input_output_aliases={0: 0, 1: 1},
        compiler_params=SMALL,
        name="add_incoming",
    )(coarse_all, gfeat_all, coarse, gfeat, total, left, right)


def weights_kernel(scale, packed, gsub_o, gdown_o):
    for k in range(K):
        r, c = k // 2 * C, k % 2 * C
        gsub_o[k] = packed[r:r + C, c:c + C].astype(F32) * scale
    for k in range(8):
        r, c = SUB_ROWS + k % 4 * C, k // 4 * C
        gdown_o[k] = packed[r:r + C, c:c + C].astype(F32) * scale


def weights_call(scale, packed):
    return pl.pallas_call(
        functools.partial(weights_kernel, scale),
        grid=(1,),
        in_specs=[full(packed.shape)],
        out_specs=[full((K, C, C)), full((8, C, C))],
        out_shape=[sd((K, C, C), F32), sd((8, C, C), F32)],
        compiler_params=SMALL,
        name="unpack_weights",
    )(packed)


def shifted(block, axis, step):
    n = lax.axis_size(axis)
    return lax.ppermute(block, axis, [(i, i + step) for i in range(n) if 0 <= i + step < n])


def shards(features, counts, sub_rows, sub_from, down_map, w_sub, w_down, cotangent):
    feat = features[0, 0]
    grad = cotangent[0, 0]
    rows, frm, dmap = sub_rows.reshape(K, 1, ROWS), sub_from.reshape(K, 1, ROWS), down_map[0, 0]
    nx, ny = lax.axis_size("gx"), lax.axis_size("gy")
    count = nx * ny
    border = border_pack(feat, grad)
    from_before, from_after = shifted(border, "gx", 1), shifted(border, "gx", -1)
    counts = counts.reshape(1)
    coarse_all, gpre_all, gsub, gdown, w_cat, w_t, wd_cat, wd_t = first_call(
        counts, feat, rows, frm, dmap, grad, w_sub, w_down)
    from_before, from_after, gsub = lax.optimization_barrier((from_before, from_after, gsub))
    column = jnp.stack([from_before, border, from_after])
    below, above = shifted(column, "gy", 1), shifted(column, "gy", -1)
    coarse_all, gpre_all, gsub, gdown = rest_call(
        counts, feat, rows, frm, dmap, grad, w_cat, wd_cat, wd_t, gsub, gdown, coarse_all, gpre_all)
    coarse, packed, gpre, split = border_call(
        count, feat, rows, frm, dmap, grad, below, column, above, w_cat, wd_cat, wd_t, gsub, gdown)
    pieces = lax.all_to_all(packed.reshape(count, PAIRS, 2, 2 * C), ("gx", "gy"), 0, 0, tiled=True)
    gfeat, mid, down, up = border_scatter_call(rows, frm, dmap, gpre, split, w_t)
    from_up, from_down = shifted(down, "gy", -1), shifted(up, "gy", 1)
    pieces, from_up, from_down = lax.optimization_barrier((pieces, from_up, from_down))
    total = mid + from_up.astype(F32) + from_down.astype(F32)
    from_right = shifted(total[0].astype(BF), "gx", -1)
    from_left = shifted(total[2].astype(BF), "gx", 1)
    shape = pieces.shape
    spread = sum_call(pieces.reshape(count * PIECE, 2 * C))
    spread, gpre_all = lax.optimization_barrier((spread, gpre_all))
    gathered = lax.all_to_all(spread.reshape(shape), ("gx", "gy"), 0, 0, tiled=True).reshape(-1, 2 * C)
    gfeat_all = local_scatter_call(counts, rows, frm, gpre_all, w_t)
    coarse_out, grad_features = finish_call(coarse_all, gfeat_all, coarse, gfeat, total[1], from_left, from_right)
    grad_w_sub, grad_w_down = weights_call(float(ROWS * count) ** -0.5, gathered)
    return coarse_out[None, None], grad_features[None, None], grad_w_sub, grad_w_down


def solution(mesh):
    tile = P("gx", "gy", None, None)
    return jax.shard_map(
        shards,
        mesh=mesh,
        in_specs=(tile, P("gx", "gy"), tile, tile, tile, P(), P(), tile),
        out_specs=(tile, tile, P(), P()),
        check_vma=False,
    )
```

time: 74.6 us -> 80.1 us (1.074)
  the two profiles are of different devices: /device:TPU:1 before, /device:TPU:32 now
where the time goes in v3:
time: 80.1 us; the launch traced here: 78.5 us
  starting transfers between devices  43.3 us (54%)
  Pallas kernels  26.1 us (33%)
  local copies, waits for them, and re-layouts  3.84 us (5%)
  waiting for transfers between devices  3.74 us (5%)
  between operations  1.49 us (2%)
    ppermute x8, starting transfers between devices, shifted(): lax.ppermute(block, axis, [(i, i + step) for i in range(n) if 0 <= i + st...  21.5 us
    all_to_all x1, starting transfers between devices, shards(): lax.all_to_all(spread.reshape(shape), ('gx', 'gy'), 0, 0, tiled=True)  11.6 us
    all_to_all x1, starting transfers between devices, shards(): lax.all_to_all(packed.reshape(count, PAIRS, 2, 2 * C), ('gx', 'gy'), 0, 0...  10.2 us
    pallas_call x1, Pallas kernels, local_scatter_call(): pl.pallas_call(local_scatter_kernel, grid=(3,), in_specs=[pl.BlockSpec(me...  6.29 us
    pallas_call x1, Pallas kernels, rest_call(): pl.pallas_call(rest_kernel, grid=(2,), in_specs=[pl.BlockSpec(memory_spac...  5.78 us
    pallas_call x1, Pallas kernels, border_call(): pl.pallas_call(border_kernel, grid=(1,), in_specs=table_specs(0) + [slab,...  4.08 us
    unnamed x16, local copies, waits for them, and re-layouts  3.81 us
    pallas_call x1, Pallas kernels, first_call(): pl.pallas_call(first_kernel, grid=(1,), in_specs=[pl.BlockSpec(memory_spa...  3.4 us
  transfers between devices with their start and end apart: 10, of which 3 were waited for; matrix products, arithmetic and copies ran while one was open for 0% of the time, Pallas kernels for 24%

profile of v3, /device:TPU:32, one launch (start us, length us, event | category | flops | bytes accessed | tf_op | source)
XLA Modules:
  0.0 78.5 jit_solution(13328817503243573500)
XLA Ops:
  0.7 0.9 %pack_border.1 = bf16[64,640]{1,0:T(8,128)(2,1)S(1)} custom-call(bf16[64,2048]{1,0:T(8,128)(2,1)} %bitcast.34, bf16[64,512]{1,0:T(8,128)(2,1)} %bitcast.40), custom_call_target="tpu_custom_call" | custom-call | tf_op jit(solution)/shard_map/pack_border/pallas_call | solution.py:259
  1.6 4.5 %collective-permute-start.1 = (bf16[64,640]{1,0:T(8,128)(2,1)S(1)}, bf16[64,640]{1,0:T(8,128)(2,1)S(1)}, u32[]{:S(2)}, u32[]{:S(2)}) collective-permute-start(bf16[64,640]{1,0:T(8,128)(2,1)S(1)} %pack_border.1), channel_id=1, source_target_pairs={{8,0},{16,8},{24,16},{32,24},{40,32},{48,40},{56,48},{64,56},{72,6... | collective-permute-start | bytes 245768 | tf_op jit(solution)/shard_map/ppermute | solution.py:402
  6.0 1.9 %collective-permute-start = (bf16[64,640]{1,0:T(8,128)(2,1)S(1)}, bf16[64,640]{1,0:T(8,128)(2,1)S(1)}, u32[]{:S(2)}, u32[]{:S(2)}) collective-permute-start(bf16[64,640]{1,0:T(8,128)(2,1)S(1)} %pack_border.1), channel_id=1, source_target_pairs={{0,8},{8,16},{16,24},{24,32},{32,40},{40,48},{48,56},{56,64},{64,7... | collective-permute-start | bytes 245768 | tf_op jit(solution)/shard_map/ppermute | solution.py:402
  8.7 0.0 copy-start.1
  8.7 0.9 %copy-done.1 = s32[1,1,27,2048]{3,1,2,0:T(1,128)S(1)} copy-done((s32[1,1,27,2048]{3,1,2,0:T(1,128)S(1)}, s32[1,1,27,2048]{3,1,2,0:T(1,128)}, u32[]{:S(2)}) %copy-start.1) | copy-done | bytes 221208
  9.6 0.9 %copy-done.3 = bf16[1,1,64,2048]{3,2,1,0:T(8,128)(2,1)S(1)} copy-done((bf16[1,1,64,2048]{3,2,1,0:T(8,128)(2,1)S(1)}, bf16[1,1,64,2048]{3,2,1,0:T(8,128)(2,1)}, u32[]{:S(2)}) %copy-start.3) | copy-done | bytes 262168
  10.5 1.0 %copy-done.5 = bf16[27,64,64]{2,1,0:T(8,128)(2,1)S(1)} copy-done((bf16[27,64,64]{2,1,0:T(8,128)(2,1)S(1)}, bf16[27,64,64]{2,1,0:T(8,128)(2,1)}, u32[]{:S(2)}) %copy-start.5) | copy-done | bytes 221208
  11.6 0.9 %copy-done.7 = bf16[8,64,64]{2,1,0:T(8,128)(2,1)S(1)} copy-done((bf16[8,64,64]{2,1,0:T(8,128)(2,1)S(1)}, bf16[8,64,64]{2,1,0:T(8,128)(2,1)}, u32[]{:S(2)}) %copy-start.7) | copy-done | bytes 65560
  12.5 3.4 %first_local_block.1 = (bf16[64,512]{1,0:T(8,128)(2,1)}, bf16[64,2048]{1,0:T(8,128)(2,1)S(1)}, f32[64,1728]{1,0:T(8,128)S(1)}, f32[512,64]{1,0:T(8,128)S(1)}, bf...) custom-call(s32[1]{0:T(128)} %bitcast.21.counts, ...), custom_call_target="tpu_custom_call" | custom-call | tf_op jit(solution)/shard_map/first_local_block/pallas_call | solution.py:205
  15.9 0.0 collective-permute-done.1
  15.9 0.0 collective-permute-done
  15.9 1.3 %collective-permute-start.3 = (bf16[3,64,640]{2,1,0:T(8,128)(2,1)S(1)}, bf16[3,64,640]{2,1,0:T(8,128)(2,1)S(1)}, u32[]{:S(2)}, u32[]{:S(2)}) collective-permute-start(bf16[3,64,640]{2,1,0:T(8,128)(2,1)S(1)} %pad_maximum_fusion.column), channel_id=1, source_target_pairs={{1,0},{2,1},{3,2},{4,3},{5,4},{6,5},{7,6},{9,8},{10,9},{11,10},{12... | collective-permute-start | bytes 737288 | tf_op jit(solution)/shard_map/ppermute | solution.py:402
  17.2 3.0 %collective-permute-start.2 = (bf16[3,64,640]{2,1,0:T(8,128)(2,1)S(1)}, bf16[3,64,640]{2,1,0:T(8,128)(2,1)S(1)}, u32[]{:S(2)}, u32[]{:S(2)}) collective-permute-start(bf16[3,64,640]{2,1,0:T(8,128)(2,1)S(1)} %pad_maximum_fusion.column), channel_id=1, source_target_pairs={{0,1},{1,2},{2,3},{3,4},{4,5},{5,6},{6,7},{8,9},{9,10},{10,11},{11... | collective-permute-start | bytes 737288 | tf_op jit(solution)/shard_map/ppermute | solution.py:402
  20.3 5.8 %other_local_blocks.1 = (bf16[64,512]{1,0:T(8,128)(2,1)}, bf16[64,2048]{1,0:T(8,128)(2,1)S(1)}, f32[64,1728]{1,0:T(8,128)S(1)}, f32[512,64]{1,0:T(8,128)S(1)}) custom-call(s32[1]{0:T(128)} %bitcast.22.counts, bf16[64,2048]{1,0:T(8,128)(2,1)S(1)} %bitcast.36, s32[27,1,2048]{2,1,0:T(1,128)S(1)} %bitcast.25, ...), custom_call_target="tpu_custom_call", output_to_operand_aliasing={{0}: (11, {}), {1}: (12, {})} | custom-call | tf_op jit(solution)/shard_map/other_local_blocks/pallas_call | solution.py:220
  26.0 0.0 collective-permute-done.3.above
  26.1 4.1 %border_block.1 = (f32[64,128]{1,0:T(8,128)S(1)}, bf16[1280,128]{1,0:T(8,128)(2,1)}, bf16[64,512]{1,0:T(8,128)(2,1)S(1)}, bf16[128,512]{1,0:T(8,128)(2,1)S(1)}) custom-call(bf16[64,2048]{1,0:T(8,128)(2,1)S(1)} %bitcast.37, s32[27,1,2048]{2,1,0:T(1,128)S(1)} %bitcast.26, s32[27,1,2048]{2,1,0:T(1,128)S(1)} %bitcast.31, s32[2,2048]{1,0:T(2,128)S(1)} %bitcast.47, ...), custom_call_target="tpu_custom_call" | custom-call | tf_op jit(solution)/shard_map/border_block/pallas_call | solution.py:313
  30.1 10.2 %all-to-all-start = ((bf16[128,5,2,128]{3,2,1,0:T(2,128)(2,1)}), bf16[128,5,2,128]{3,2,1,0:T(2,128)(2,1)S(1)}, u32[]{:S(2)}, u32[]{:S(2)}) async-start(bf16[128,5,2,128]{3,2,1,0:T(2,128)(2,1)} %bitcast.9), calls=%async_computation | async-start | bytes 655360 | tf_op jit(solution)/shard_map/all_to_all | solution.py:423
  40.3 3.0 %border_scatter_block.1 = (f32[64,512]{1,0:T(8,128)S(1)}, f32[3,64,640]{2,1,0:T(8,128)S(1)}, bf16[3,64,640]{2,1,0:T(8,128)(2,1)S(1)}, bf16[3,64,640]{2,1,0:T(8,128)(2,1)S(1)}) custom-call(s32[27,1,2048]{2,1,0:T(1,128)S(1)} %bitcast.27, s32[27,1,2048]{2,1,0:T(1,128)S(1)} %bitcast.32, s32[2,2048]{1,0:T(2,128)S(1)} %bitcast.48, ...), custom_call_target="tpu_custom_call" | custom-call | tf_op jit(solution)/shard_map/border_scatter_block/pallas_call | solution.py:342
  43.3 1.3 %collective-permute-start.4 = (bf16[3,64,640]{2,1,0:T(8,128)(2,1)S(1)}, bf16[3,64,640]{2,1,0:T(8,128)(2,1)S(1)}, u32[]{:S(2)}, u32[]{:S(2)}) collective-permute-start(bf16[3,64,640]{2,1,0:T(8,128)(2,1)S(1)} %get-tuple-element.53), channel_id=1, source_target_pairs={{1,0},{2,1},{3,2},{4,3},{5,4},{6,5},{7,6},{9,8},{10,9},{11,10},{12... | collective-permute-start | bytes 737288 | tf_op jit(solution)/shard_map/ppermute | solution.py:402
  44.6 3.0 %collective-permute-start.5 = (bf16[3,64,640]{2,1,0:T(8,128)(2,1)S(1)}, bf16[3,64,640]{2,1,0:T(8,128)(2,1)S(1)}, u32[]{:S(2)}, u32[]{:S(2)}) collective-permute-start(bf16[3,64,640]{2,1,0:T(8,128)(2,1)S(1)} %get-tuple-element.54), channel_id=1, source_target_pairs={{0,1},{1,2},{2,3},{3,4},{4,5},{5,6},{6,7},{8,9},{9,10},{10,11},{11... | collective-permute-start | bytes 737288 | tf_op jit(solution)/shard_map/ppermute | solution.py:402
  47.6 0.0 collective-permute-done.4
  47.7 1.1 %collective-permute-done.5 = bf16[3,64,640]{2,1,0:T(8,128)(2,1)S(1)} collective-permute-done((bf16[3,64,640]{2,1,0:T(8,128)(2,1)S(1)}, bf16[3,64,640]{2,1,0:T(8,128)(2,1)S(1)}, u32[]{:S(2)}, u32[]{:S(2)}) %collective-permute-start.5) | collective-permute-done | bytes 245792 | tf_op jit(solution)/shard_map/ppermute | solution.py:402
  48.7 2.4 %all-to-all-done = bf16[128,5,2,128]{3,2,1,0:T(2,128)(2,1)S(1)} async-done(((bf16[128,5,2,128]{3,2,1,0:T(2,128)(2,1)}), bf16[128,5,2,128]{3,2,1,0:T(2,128)(2,1)S(1)}, u32[]{:S(2)}, u32[]{:S(2)}) %all-to-all-start) | async-done | bytes 327712 | tf_op jit(solution)/shard_map/all_to_all | solution.py:423
  51.2 0.8 %sum_pieces.1 = bf16[1280,128]{1,0:T(8,128)(2,1)} custom-call(bf16[1280,128]{1,0:T(8,128)(2,1)S(1)} %bitcast.39), custom_call_target="tpu_custom_call" | custom-call | tf_op jit(solution)/shard_map/sum_pieces/pallas_call | solution.py:283
  52.0 11.6 %all-to-all-start.1 = ((bf16[128,5,2,128]{3,2,1,0:T(2,128)(2,1)}), bf16[128,5,2,128]{3,2,1,0:T(2,128)(2,1)S(1)}, u32[]{:S(2)}, u32[]{:S(2)}) async-start(bf16[128,5,2,128]{3,2,1,0:T(2,128)(2,1)} %bitcast.16), calls=%async_computation.1 | async-start | bytes 655360 | tf_op jit(solution)/shard_map/all_to_all | solution.py:433
  63.6 0.1 fusion
  63.7 4.5 %collective-permute-start.7 = (bf16[64,640]{1,0:T(8,128)(2,1)S(1)}, bf16[64,640]{1,0:T(8,128)(2,1)S(1)}, u32[]{:S(2)}, u32[]{:S(2)}) collective-permute-start(bf16[64,640]{1,0:T(8,128)(2,1)S(1)} %get-tuple-element.70), channel_id=1, source_target_pairs={{8,0},{16,8},{24,16},{32,24},{40,32},{48,40},{56,48},{64,56},{72,6... | collective-permute-start | bytes 245768 | tf_op jit(solution)/shard_map/ppermute | solution.py:402
  68.2 1.9 %collective-permute-start.6 = (bf16[64,640]{1,0:T(8,128)(2,1)S(1)}, bf16[64,640]{1,0:T(8,128)(2,1)S(1)}, u32[]{:S(2)}, u32[]{:S(2)}) collective-permute-start(bf16[64,640]{1,0:T(8,128)(2,1)S(1)} %get-tuple-element.71), channel_id=1, source_target_pairs={{0,8},{8,16},{16,24},{24,32},{32,40},{40,48},{48,56},{56,64},{64,7... | collective-permute-start | bytes 245768 | tf_op jit(solution)/shard_map/ppermute | solution.py:402
  70.2 6.3 %local_scatter_blocks.1.gfeat_i = bf16[64,2048]{1,0:T(8,128)(2,1)} custom-call(s32[1]{0:T(128)} %bitcast.23.counts, s32[27,1,2048]{2,1,0:T(1,128)S(1)} %bitcast.28, s32[27,1,2048]{2,1,0:T(1,128)S(1)} %bitcast.33, bf16[64,2048]{1,0:T(8,128)(2,1)S(1)} %get-tuple-element.57.gpre, bf16[64,1728]{1,0:T(8,128)(2,1)S(1)} %get-tuple-element.52.w_t), custom_call_target="tpu_custom_call" | custom-call | tf_op jit(solution)/shard_map/local_scatter_blocks/pallas_call | solution.py:236
  76.5 0.2 collective-permute-done.6.left
  76.7 0.7 add_incoming.1
  77.4 1.2 %unpack_weights.1 = (f32[27,64,64]{2,1,0:T(8,128)}, f32[8,64,64]{2,1,0:T(8,128)}) custom-call(bf16[1280,128]{1,0:T(8,128)(2,1)S(1)} %bitcast.38), custom_call_target="tpu_custom_call" | custom-call | tf_op jit(solution)/shard_map/unpack_weights/pallas_call | solution.py:389
  (17 shorter events, 0.1 us)
Async XLA Ops:
  0.6 8.0 %copy-start = (s32[1,1,27,2048]{3,1,2,0:T(1,128)S(1)}, s32[1,1,27,2048]{3,1,2,0:T(1,128)}, u32[]{:S(2)}) copy-start(s32[1,1,27,2048]{3,1,2,0:T(1,128)} %param.10) | copy-start | bytes 663556
  0.6 8.0 %copy-start.4 = (bf16[1,1,64,512]{3,2,1,0:T(8,128)(2,1)S(1)}, bf16[1,1,64,512]{3,2,1,0:T(8,128)(2,1)}, u32[]{:S(2)}) copy-start(bf16[1,1,64,512]{3,2,1,0:T(8,128)(2,1)} %param.15) | copy-start | bytes 196612
  0.7 8.0 %copy-start.6 = (s32[1,1,2,2048]{3,2,1,0:T(2,128)S(1)}, s32[1,1,2,2048]{3,2,1,0:T(2,128)}, u32[]{:S(2)}) copy-start(s32[1,1,2,2048]{3,2,1,0:T(2,128)} %param.12) | copy-start | bytes 49156
  1.6 14.3 %collective-permute-start.1 = (bf16[64,640]{1,0:T(8,128)(2,1)S(1)}, bf16[64,640]{1,0:T(8,128)(2,1)S(1)}, u32[]{:S(2)}, u32[]{:S(2)}) collective-permute-start(bf16[64,640]{1,0:T(8,128)(2,1)S(1)} %pack_border.1), channel_id=1, source_target_pairs={{8,0},{16,8},{24,16},{32,24},{40,32},{48,40},{56,48},{64,56},{72,6... | collective-permute-start | bytes 245768 | tf_op jit(solution)/shard_map/ppermute | solution.py:402
  6.0 9.8 %collective-permute-start = (bf16[64,640]{1,0:T(8,128)(2,1)S(1)}, bf16[64,640]{1,0:T(8,128)(2,1)S(1)}, u32[]{:S(2)}, u32[]{:S(2)}) collective-permute-start(bf16[64,640]{1,0:T(8,128)(2,1)S(1)} %pack_border.1), channel_id=1, source_target_pairs={{0,8},{8,16},{16,24},{24,32},{32,40},{40,48},{48,56},{56,64},{64,7... | collective-permute-start | bytes 245768 | tf_op jit(solution)/shard_map/ppermute | solution.py:402
  8.7 0.9 %copy-start.1 = (s32[1,1,27,2048]{3,1,2,0:T(1,128)S(1)}, s32[1,1,27,2048]{3,1,2,0:T(1,128)}, u32[]{:S(2)}) copy-start(s32[1,1,27,2048]{3,1,2,0:T(1,128)} %param.11) | copy-start | bytes 663556
  9.6 0.9 %copy-start.3 = (bf16[1,1,64,2048]{3,2,1,0:T(8,128)(2,1)S(1)}, bf16[1,1,64,2048]{3,2,1,0:T(8,128)(2,1)}, u32[]{:S(2)}) copy-start(bf16[1,1,64,2048]{3,2,1,0:T(8,128)(2,1)} %param.8) | copy-start | bytes 786436
  10.5 1.0 %copy-start.5 = (bf16[27,64,64]{2,1,0:T(8,128)(2,1)S(1)}, bf16[27,64,64]{2,1,0:T(8,128)(2,1)}, u32[]{:S(2)}) copy-start(bf16[27,64,64]{2,1,0:T(8,128)(2,1)} %w_sub.1) | copy-start | bytes 663556
  11.6 0.9 %copy-start.7 = (bf16[8,64,64]{2,1,0:T(8,128)(2,1)S(1)}, bf16[8,64,64]{2,1,0:T(8,128)(2,1)}, u32[]{:S(2)}) copy-start(bf16[8,64,64]{2,1,0:T(8,128)(2,1)} %w_down.1) | copy-start | bytes 196612
  15.9 10.1 %collective-permute-start.3 = (bf16[3,64,640]{2,1,0:T(8,128)(2,1)S(1)}, bf16[3,64,640]{2,1,0:T(8,128)(2,1)S(1)}, u32[]{:S(2)}, u32[]{:S(2)}) collective-permute-start(bf16[3,64,640]{2,1,0:T(8,128)(2,1)S(1)} %pad_maximum_fusion.column), channel_id=1, source_target_pairs={{1,0},{2,1},{3,2},{4,3},{5,4},{6,5},{7,6},{9,8},{10,9},{11,10},{12... | collective-permute-start | bytes 737288 | tf_op jit(solution)/shard_map/ppermute | solution.py:402
  17.2 8.8 %collective-permute-start.2 = (bf16[3,64,640]{2,1,0:T(8,128)(2,1)S(1)}, bf16[3,64,640]{2,1,0:T(8,128)(2,1)S(1)}, u32[]{:S(2)}, u32[]{:S(2)}) collective-permute-start(bf16[3,64,640]{2,1,0:T(8,128)(2,1)S(1)} %pad_maximum_fusion.column), channel_id=1, source_target_pairs={{0,1},{1,2},{2,3},{3,4},{4,5},{5,6},{6,7},{8,9},{9,10},{10,11},{11... | collective-permute-start | bytes 737288 | tf_op jit(solution)/shard_map/ppermute | solution.py:402
  30.1 10.2 %copy-start.2 = (s32[1,1,27,2048]{3,1,2,0:T(1,128)S(1)}, s32[1,1,27,2048]{3,1,2,0:T(1,128)}, u32[]{:S(2)}) copy-start(s32[1,1,27,2048]{3,1,2,0:T(1,128)} %param.11) | copy-start | bytes 663556
  30.1 21.0 %all-to-all-start = ((bf16[128,5,2,128]{3,2,1,0:T(2,128)(2,1)}), bf16[128,5,2,128]{3,2,1,0:T(2,128)(2,1)S(1)}, u32[]{:S(2)}, u32[]{:S(2)}) async-start(bf16[128,5,2,128]{3,2,1,0:T(2,128)(2,1)} %bitcast.9), calls=%async_computation | async-start | bytes 655360 | tf_op jit(solution)/shard_map/all_to_all | solution.py:423
  43.3 4.4 %collective-permute-start.4 = (bf16[3,64,640]{2,1,0:T(8,128)(2,1)S(1)}, bf16[3,64,640]{2,1,0:T(8,128)(2,1)S(1)}, u32[]{:S(2)}, u32[]{:S(2)}) collective-permute-start(bf16[3,64,640]{2,1,0:T(8,128)(2,1)S(1)} %get-tuple-element.53), channel_id=1, source_target_pairs={{1,0},{2,1},{3,2},{4,3},{5,4},{6,5},{7,6},{9,8},{10,9},{11,10},{12... | collective-permute-start | bytes 737288 | tf_op jit(solution)/shard_map/ppermute | solution.py:402
  44.6 4.2 %collective-permute-start.5 = (bf16[3,64,640]{2,1,0:T(8,128)(2,1)S(1)}, bf16[3,64,640]{2,1,0:T(8,128)(2,1)S(1)}, u32[]{:S(2)}, u32[]{:S(2)}) collective-permute-start(bf16[3,64,640]{2,1,0:T(8,128)(2,1)S(1)} %get-tuple-element.54), channel_id=1, source_target_pairs={{0,1},{1,2},{2,3},{3,4},{4,5},{5,6},{6,7},{8,9},{9,10},{10,11},{11... | collective-permute-start | bytes 737288 | tf_op jit(solution)/shard_map/ppermute | solution.py:402
  52.0 25.4 %all-to-all-start.1 = ((bf16[128,5,2,128]{3,2,1,0:T(2,128)(2,1)}), bf16[128,5,2,128]{3,2,1,0:T(2,128)(2,1)S(1)}, u32[]{:S(2)}, u32[]{:S(2)}) async-start(bf16[128,5,2,128]{3,2,1,0:T(2,128)(2,1)} %bitcast.16), calls=%async_computation.1 | async-start | bytes 655360 | tf_op jit(solution)/shard_map/all_to_all | solution.py:433
  63.7 12.8 %collective-permute-start.7 = (bf16[64,640]{1,0:T(8,128)(2,1)S(1)}, bf16[64,640]{1,0:T(8,128)(2,1)S(1)}, u32[]{:S(2)}, u32[]{:S(2)}) collective-permute-start(bf16[64,640]{1,0:T(8,128)(2,1)S(1)} %get-tuple-element.70), channel_id=1, source_target_pairs={{8,0},{16,8},{24,16},{32,24},{40,32},{48,40},{56,48},{64,56},{72,6... | collective-permute-start | bytes 245768 | tf_op jit(solution)/shard_map/ppermute | solution.py:402
  68.2 8.4 %collective-permute-start.6 = (bf16[64,640]{1,0:T(8,128)(2,1)S(1)}, bf16[64,640]{1,0:T(8,128)(2,1)S(1)}, u32[]{:S(2)}, u32[]{:S(2)}) collective-permute-start(bf16[64,640]{1,0:T(8,128)(2,1)S(1)} %get-tuple-element.71), channel_id=1, source_target_pairs={{0,8},{8,16},{16,24},{24,32},{32,40},{40,48},{48,56},{56,64},{64,7... | collective-permute-start | bytes 245768 | tf_op jit(solution)/shard_map/ppermute | solution.py:402

commit v4 on v3

--- a/solution.py
+++ b/solution.py
@@ -291,8 +291,11 @@
     )(pieces)
 
 
-def border_kernel(feat, rows, frm, dmap, grad, below, column, above, w_cat, wd_cat, wd_t, gsub, gdown,
-                  coarse_o, packed_o, gpre_o, split_o, source):
+def border_kernel(side, feat, rows, frm, dmap, grad, near, column, far, w_cat, wd_cat, wd_t, gsub, gdown,
+                  coarse_o, packed_o, gpre_o, split_o, source, below, above):
+    even = side[0] == 1
+    below[...] = jnp.where(even, far[...], near[...])
+    above[...] = jnp.where(even, near[...], far[...])
     coarse, gpre, dsub, ddown, split = forward_work(
         True, 0, feat, rows, frm, dmap, grad, (below, column, above), w_cat, wd_cat, wd_t, source)
     coarse_o[...] = coarse
@@ -308,48 +311,54 @@
     packed_o[USED:, :] = jnp.zeros((packed_o.shape[0] - USED, 2 * C), BF)
 
 
-def border_call(count, feat, rows, frm, dmap, grad, below, column, above, w_cat, wd_cat, wd_t, gsub, gdown):
+def border_call(count, side, feat, rows, frm, dmap, grad, near, column, far, w_cat, wd_cat, wd_t, gsub, gdown):
     slab = full((3, C, WIDE))
     return pl.pallas_call(
         border_kernel,
         grid=(1,),
-        in_specs=table_specs(0) + [slab, slab, slab, full((C, KC)), full((C, 8 * C)), full((C, 8 * C)),
+        in_specs=[pl.BlockSpec(memory_space=pltpu.SMEM)] + table_specs(0) + [slab, slab, slab, full((C, KC)), full((C, 8 * C)), full((C, 8 * C)),
                                    full((C, KC)), full((8 * C, C))],
         out_specs=[full((C, CQ)), full((count * PIECE, 2 * C)), full((C, VB)), full((2 * C, VB))],
         out_shape=[sd((C, CQ), F32), sd((count * PIECE, 2 * C), BF), sd((C, VB), BF), sd((2 * C, VB), BF)],
-        scratch_shapes=[SOURCE],
+        scratch_shapes=[SOURCE, pltpu.VMEM((3, C, WIDE), BF), pltpu.VMEM((3, C, WIDE), BF)],
         compiler_params=LIMIT,
         name="border_block",
-    )(feat, rows, frm, dmap, grad, below, column, above, w_cat, wd_cat, wd_t, gsub, gdown)
-
-
-def border_scatter_kernel(rows, frm, dmap, gpre, split, w_t, gfeat_o, mid_o, down_o, up_o, spread):
+    )(side, feat, rows, frm, dmap, grad, near, column, far, w_cat, wd_cat, wd_t, gsub, gdown)
+
+
+def border_scatter_kernel(side, rows, frm, dmap, gpre, split, w_t, gfeat_o, mid_o, near_o, far_o, spread):
     gfeat_o[...] = scatter_work(True, 0, rows, frm, gpre[...], w_t, spread)
     both = mm_nt(split[...], pick_edges(dmap[0:1, :]))
     edge = both[:C] + both[C:]
-    for d in range(9):
-        out = (down_o, mid_o, up_o)[d % 3]
-        ks = [k for k in range(K) if DIRS[k] == d]
-        a, b = ks[0] * C, (ks[-1] + 1) * C
+    even = side[0] == 1
+
+    def slab(d):
+        a = 9 * (d // 3) + 3 * (d % 3)
+        a, b = a * C, (a + 3) * C
         outward = jnp.zeros((C, VB), F32) if d == 4 else mm(w_t[:, a:b], spread[a:b, VB:2 * VB])
-        out[d // 3, :, 0:VB] = outward.astype(out.dtype)
-        tail = jnp.concatenate([edge[:, d * CB:(d + 1) * CB], jnp.zeros((C, CB), F32)], axis=1)
-        out[d // 3, :, VB:] = tail.astype(out.dtype)
-
-
-def border_scatter_call(rows, frm, dmap, gpre, split, w_t):
+        return jnp.concatenate([outward, edge[:, d * CB:(d + 1) * CB], jnp.zeros((C, CB), F32)], axis=1)
+
+    for x in range(3):
+        down, up = slab(3 * x).astype(BF), slab(3 * x + 2).astype(BF)
+        mid_o[x] = slab(3 * x + 1)
+        near_o[x] = jnp.where(even, up, down)
+        far_o[x] = jnp.where(even, down, up)
+
+
+def border_scatter_call(side, rows, frm, dmap, gpre, split, w_t):
     slab = (3, C, WIDE)
     return pl.pallas_call(
         border_scatter_kernel,
         grid=(1,),
-        in_specs=[index_columns(0), index_columns(0), columns((2, VB), 0), full((C, VB)), full((2 * C, VB)),
+        in_specs=[pl.BlockSpec(memory_space=pltpu.SMEM), index_columns(0), index_columns(0), columns((2, VB), 0),
+                  full((C, VB)), full((2 * C, VB)),
                   full((C, KC))],
         out_specs=[full((C, VB)), full(slab), full(slab), full(slab)],
         out_shape=[sd((C, VB), F32), sd(slab, F32), sd(slab, BF), sd(slab, BF)],
         scratch_shapes=[pltpu.VMEM((KC, 2 * VB), BF)],
         compiler_params=LIMIT,
         name="border_scatter_block",
-    )(rows, frm, dmap, gpre, split, w_t)
+    )(side, rows, frm, dmap, gpre, split, w_t)
 
 
 def finish_kernel(coarse_i, gfeat_i, coarse, gfeat, total, left, right, coarse_o, gfeat_o):
@@ -397,9 +406,10 @@
     )(packed)
 
 
-def shifted(block, axis, step):
+def swapped(block, axis, first):
     n = lax.axis_size(axis)
-    return lax.ppermute(block, axis, [(i, i + step) for i in range(n) if 0 <= i + step < n])
+    pairs = [(i, i + 1) for i in range(0 if first else 1, n - 1, 2)]
+    return lax.ppermute(block, axis, pairs + [(b, a) for a, b in pairs])
 
 
 def shards(features, counts, sub_rows, sub_from, down_map, w_sub, w_down, cotangent):
@@ -409,30 +419,32 @@
     nx, ny = lax.axis_size("gx"), lax.axis_size("gy")
     count = nx * ny
     border = border_pack(feat, grad)
-    from_before, from_after = shifted(border, "gx", 1), shifted(border, "gx", -1)
+    even_x, even_y = lax.axis_index("gx") % 2 == 0, lax.axis_index("gy") % 2 == 0
+    side = even_y.astype(jnp.int32).reshape(1)
+    near, far = swapped(border, "gx", True), swapped(border, "gx", False)
     counts = counts.reshape(1)
     coarse_all, gpre_all, gsub, gdown, w_cat, w_t, wd_cat, wd_t = first_call(
-        counts, feat, rows, frm, dmap, grad, w_sub, w_down)
-    from_before, from_after, gsub = lax.optimization_barrier((from_before, from_after, gsub))
-    column = jnp.stack([from_before, border, from_after])
-    below, above = shifted(column, "gy", 1), shifted(column, "gy", -1)
+        counts, *[pltpu.with_memory_space_constraint(a, pltpu.HBM) for a in (feat, rows, frm, dmap, grad, w_sub, w_down)])
+    near, far, gsub = lax.optimization_barrier((near, far, gsub))
+    column = jnp.stack([jnp.where(even_x, far, near), border, jnp.where(even_x, near, far)])
+    near, far = swapped(column, "gy", True), swapped(column, "gy", False)
     coarse_all, gpre_all, gsub, gdown = rest_call(
         counts, feat, rows, frm, dmap, grad, w_cat, wd_cat, wd_t, gsub, gdown, coarse_all, gpre_all)
     coarse, packed, gpre, split = border_call(
-        count, feat, rows, frm, dmap, grad, below, column, above, w_cat, wd_cat, wd_t, gsub, gdown)
+        count, side, feat, rows, frm, dmap, grad, near, column, far, w_cat, wd_cat, wd_t, gsub, gdown)
     pieces = lax.all_to_all(packed.reshape(count, PAIRS, 2, 2 * C), ("gx", "gy"), 0, 0, tiled=True)
-    gfeat, mid, down, up = border_scatter_call(rows, frm, dmap, gpre, split, w_t)
-    from_up, from_down = shifted(down, "gy", -1), shifted(up, "gy", 1)
-    pieces, from_up, from_down = lax.optimization_barrier((pieces, from_up, from_down))
-    total = mid + from_up.astype(F32) + from_down.astype(F32)
-    from_right = shifted(total[0].astype(BF), "gx", -1)
-    from_left = shifted(total[2].astype(BF), "gx", 1)
+    gfeat, mid, out_near, out_far = border_scatter_call(side, rows, frm, dmap, gpre, split, w_t)
+    near, far = swapped(out_near, "gy", True), swapped(out_far, "gy", False)
+    pieces, near, far = lax.optimization_barrier((pieces, near, far))
+    total = mid + near.astype(F32) + far.astype(F32)
+    near = swapped(jnp.where(even_x, total[2], total[0]).astype(BF), "gx", True)
+    far = swapped(jnp.where(even_x, total[0], total[2]).astype(BF), "gx", False)
     shape = pieces.shape
     spread = sum_call(pieces.reshape(count * PIECE, 2 * C))
     spread, gpre_all = lax.optimization_barrier((spread, gpre_all))
     gathered = lax.all_to_all(spread.reshape(shape), ("gx", "gy"), 0, 0, tiled=True).reshape(-1, 2 * C)
     gfeat_all = local_scatter_call(counts, rows, frm, gpre_all, w_t)
-    coarse_out, grad_features = finish_call(coarse_all, gfeat_all, coarse, gfeat, total[1], from_left, from_right)
+    coarse_out, grad_features = finish_call(coarse_all, gfeat_all, coarse, gfeat, total[1], near, far)
     grad_w_sub, grad_w_down = weights_call(float(ROWS * count) ** -0.5, gathered)
     return coarse_out[None, None], grad_features[None, None], grad_w_sub, grad_w_down
 

time: 80.1 us -> 69.6 us (0.87)
  the two profiles are of different devices: /device:TPU:32 before, /device:TPU:1 now
where the time goes in v4:
time: 69.6 us; the launch traced here: 68.9 us
  starting transfers between devices  39.3 us (56%)
  Pallas kernels  14.8 us (21%)
  waiting for transfers between devices  12.4 us (18%)
  between operations  1.49 us (2%)
  local copies, waits for them, and re-layouts  0.7 us (1%)
    ppermute x8, starting transfers between devices, swapped(): return lax.ppermute(block, axis, pairs + [(b, a) for a, b in pairs])  18.4 us
    all_to_all x1, starting transfers between devices, shards(): lax.all_to_all(packed.reshape(count, PAIRS, 2, 2 * C), ('gx', 'gy'), 0, 0...  12.3 us
    ppermute x8, waiting for transfers between devices, swapped(): return lax.ppermute(block, axis, pairs + [(b, a) for a, b in pairs])  9.8 us
    all_to_all x1, starting transfers between devices, shards(): lax.all_to_all(spread.reshape(shape), ('gx', 'gy'), 0, 0, tiled=True)  8.58 us
    pallas_call x1, Pallas kernels, border_call(): pl.pallas_call(border_kernel, grid=(1,), in_specs=[pl.BlockSpec(memory_sp...  4.08 us
    pallas_call x1, Pallas kernels, border_scatter_call(): pl.pallas_call(border_scatter_kernel, grid=(1,), in_specs=[pl.BlockSpec(m...  2.98 us
    all_to_all x1, waiting for transfers between devices, shards(): lax.all_to_all(spread.reshape(shape), ('gx', 'gy'), 0, 0, tiled=True)  2.59 us
    pallas_call x1, Pallas kernels, first_call(): pl.pallas_call(first_kernel, grid=(1,), in_specs=[pl.BlockSpec(memory_spa...  2.05 us
  transfers between devices with their start and end apart: 10, of which 4 were waited for; matrix products, arithmetic and copies ran while one was open for 0% of the time, Pallas kernels for 11%

profile of v4, /device:TPU:1, one launch (start us, length us, event | category | flops | bytes accessed | tf_op | source)
XLA Modules:
  0.0 68.9 jit_solution(15707735479677370256)
XLA Ops:
  0.6 0.9 %pack_border.1 = bf16[64,640]{1,0:T(8,128)(2,1)S(1)} custom-call(bf16[64,2048]{1,0:T(8,128)(2,1)} %bitcast.37, bf16[64,512]{1,0:T(8,128)(2,1)} %bitcast.43), custom_call_target="tpu_custom_call" | custom-call | tf_op jit(solution)/shard_map/pack_border/pallas_call | solution.py:259
  1.5 0.7 collective-permute-start.1
  2.2 4.7 %collective-permute-start = (bf16[64,640]{1,0:T(8,128)(2,1)S(1)}, bf16[64,640]{1,0:T(8,128)(2,1)S(1)}, u32[]{:S(2)}, u32[]{:S(2)}) collective-permute-start(bf16[64,640]{1,0:T(8,128)(2,1)S(1)} %pack_border.1), channel_id=1, source_target_pairs={{0,8},{16,24},{32,40},{48,56},{64,72},{80,88},{96,104},{112,120},{... | collective-permute-start | bytes 245768 | tf_op jit(solution)/shard_map/ppermute | solution.py:412
  7.6 2.1 %first_local_block.1 = (bf16[64,512]{1,0:T(8,128)(2,1)}, bf16[64,2048]{1,0:T(8,128)(2,1)S(1)}, f32[64,1728]{1,0:T(8,128)S(1)}, f32[512,64]{1,0:T(8,128)S(1)}, bf...) custom-call(s32[1]{0:T(128)} %bitcast.24.counts, ...), custom_call_target="tpu_custom_call" | custom-call | tf_op jit(solution)/shard_map/first_local_block/pallas_call | solution.py:205
  9.6 0.0 copy-start.2
  9.7 0.0 copy-start
  9.7 0.0 copy-start.1
  9.7 0.0 copy-start.3
  9.8 4.4 %collective-permute-start.3 = (bf16[3,64,640]{2,1,0:T(8,128)(2,1)S(1)}, bf16[3,64,640]{2,1,0:T(8,128)(2,1)S(1)}, u32[]{:S(2)}, u32[]{:S(2)}) collective-permute-start(bf16[3,64,640]{2,1,0:T(8,128)(2,1)S(1)} %pad_maximum_fusion.column), channel_id=1, source_target_pairs={{1,2},{3,4},{5,6},{2,1},{4,3},{6,5},{9,10},{11,12},{13,14},{10,9},... | collective-permute-start | bytes 737288 | tf_op jit(solution)/shard_map/ppermute | solution.py:412
  14.1 0.1 collective-permute-start.2
  14.2 0.0 copy-start.4
  14.3 0.7 copy-done.4
  15.0 0.8 %other_local_blocks.1 = (bf16[64,512]{1,0:T(8,128)(2,1)}, bf16[64,2048]{1,0:T(8,128)(2,1)S(1)}, f32[64,1728]{1,0:T(8,128)S(1)}, f32[512,64]{1,0:T(8,128)S(1)}) custom-call(s32[1]{0:T(128)} %bitcast.25.counts, bf16[64,2048]{1,0:T(8,128)(2,1)S(1)} %bitcast.39, s32[27,1,2048]{2,1,0:T(1,128)S(1)} %bitcast.28, ...), custom_call_target="tpu_custom_call", output_to_operand_aliasing={{0}: (11, {}), {1}: (12, {})} | custom-call | tf_op jit(solution)/shard_map/other_local_blocks/pallas_call | solution.py:220
  15.8 2.2 %collective-permute-done.3.far = bf16[3,64,640]{2,1,0:T(8,128)(2,1)S(1)} collective-permute-done((bf16[3,64,640]{2,1,0:T(8,128)(2,1)S(1)}, bf16[3,64,640]{2,1,0:T(8,128)(2,1)S(1)}, u32[]{:S(2)}, u32[]{:S(2)}) %collective-permute-start.3) | collective-permute-done | bytes 245792 | tf_op jit(solution)/shard_map/ppermute | solution.py:412
  18.0 4.1 %border_block.1 = (f32[64,128]{1,0:T(8,128)S(1)}, bf16[1280,128]{1,0:T(8,128)(2,1)}, bf16[64,512]{1,0:T(8,128)(2,1)S(1)}, bf16[128,512]{1,0:T(8,128)(2,1)S(1)}) custom-call(s32[1]{0:T(128)} %bitcast.6.side, bf16[64,2048]{1,0:T(8,128)(2,1)S(1)} %bitcast.40, s32[27,1,2048]{2,1,0:T(1,128)S(1)} %bitcast.29, s32[27,1,2048]{2,1,0:T(1,128)S(1)} %bitcast.34, ...), custom_call_target="tpu_custom_call" | custom-call | tf_op jit(solution)/shard_map/border_block/pallas_call | solution.py:316
  22.1 12.3 %all-to-all-start = ((bf16[128,5,2,128]{3,2,1,0:T(2,128)(2,1)}), bf16[128,5,2,128]{3,2,1,0:T(2,128)(2,1)S(1)}, u32[]{:S(2)}, u32[]{:S(2)}) async-start(bf16[128,5,2,128]{3,2,1,0:T(2,128)(2,1)} %bitcast.10), calls=%async_computation | async-start | bytes 655360 | tf_op jit(solution)/shard_map/all_to_all | solution.py:435
  34.4 3.0 %border_scatter_block.1 = (f32[64,512]{1,0:T(8,128)S(1)}, f32[3,64,640]{2,1,0:T(8,128)S(1)}, bf16[3,64,640]{2,1,0:T(8,128)(2,1)S(1)}, bf16[3,64,640]{2,1,0:T(8,128)(2,1)S(1)}) custom-call(s32[1]{0:T(128)} %bitcast.6.side, s32[27,1,2048]{2,1,0:T(1,128)S(1)} %bitcast.30, s32[27,1,2048]{2,1,0:T(1,128)S(1)} %bitcast.35, s32[2,2048]{1,0:T(2,128)S(1)} %bitcast.51, ...), custom_call_target="tpu_custom_call" | custom-call | tf_op jit(solution)/shard_map/border_scatter_block/pallas_call | solution.py:350
  37.4 1.3 %collective-permute-start.4 = (bf16[3,64,640]{2,1,0:T(8,128)(2,1)S(1)}, bf16[3,64,640]{2,1,0:T(8,128)(2,1)S(1)}, u32[]{:S(2)}, u32[]{:S(2)}) collective-permute-start(bf16[3,64,640]{2,1,0:T(8,128)(2,1)S(1)} %get-tuple-element.53), channel_id=1, source_target_pairs={{0,1},{2,3},{4,5},{6,7},{1,0},{3,2},{5,4},{7,6},{8,9},{10,11},{12,... | collective-permute-start | bytes 737288 | tf_op jit(solution)/shard_map/ppermute | solution.py:412
  38.8 2.6 %collective-permute-start.5 = (bf16[3,64,640]{2,1,0:T(8,128)(2,1)S(1)}, bf16[3,64,640]{2,1,0:T(8,128)(2,1)S(1)}, u32[]{:S(2)}, u32[]{:S(2)}) collective-permute-start(bf16[3,64,640]{2,1,0:T(8,128)(2,1)S(1)} %get-tuple-element.54), channel_id=1, source_target_pairs={{1,2},{3,4},{5,6},{2,1},{4,3},{6,5},{9,10},{11,12},{13,14},{10,9},... | collective-permute-start | bytes 737288 | tf_op jit(solution)/shard_map/ppermute | solution.py:412
  41.4 0.0 collective-permute-done.4
  41.4 5.2 %collective-permute-done.5 = bf16[3,64,640]{2,1,0:T(8,128)(2,1)S(1)} collective-permute-done((bf16[3,64,640]{2,1,0:T(8,128)(2,1)S(1)}, bf16[3,64,640]{2,1,0:T(8,128)(2,1)S(1)}, u32[]{:S(2)}, u32[]{:S(2)}) %collective-permute-start.5) | collective-permute-done | bytes 245792 | tf_op jit(solution)/shard_map/ppermute | solution.py:412
  46.5 0.0 all-to-all-done
  46.5 0.8 %sum_pieces.1 = bf16[1280,128]{1,0:T(8,128)(2,1)} custom-call(bf16[1280,128]{1,0:T(8,128)(2,1)S(1)} %bitcast.42), custom_call_target="tpu_custom_call" | custom-call | tf_op jit(solution)/shard_map/sum_pieces/pallas_call | solution.py:283
  47.3 8.6 %all-to-all-start.1 = ((bf16[128,5,2,128]{3,2,1,0:T(2,128)(2,1)}), bf16[128,5,2,128]{3,2,1,0:T(2,128)(2,1)S(1)}, u32[]{:S(2)}, u32[]{:S(2)}) async-start(bf16[128,5,2,128]{3,2,1,0:T(2,128)(2,1)} %bitcast.17), calls=%async_computation.1 | async-start | bytes 655360 | tf_op jit(solution)/shard_map/all_to_all | solution.py:445
  55.9 0.1 convert_add_fusion
  56.0 0.7 collective-permute-start.7
  56.7 3.9 %collective-permute-start.6 = (bf16[64,640]{1,0:T(8,128)(2,1)S(1)}, bf16[64,640]{1,0:T(8,128)(2,1)S(1)}, u32[]{:S(2)}, u32[]{:S(2)}) collective-permute-start(bf16[64,640]{1,0:T(8,128)(2,1)S(1)} %get-tuple-element.69), channel_id=1, source_target_pairs={{0,8},{16,24},{32,40},{48,56},{64,72},{80,88},{96,104},{112,120},{... | collective-permute-start | bytes 245768 | tf_op jit(solution)/shard_map/ppermute | solution.py:412
  60.6 1.4 %local_scatter_blocks.1.gfeat_i = bf16[64,2048]{1,0:T(8,128)(2,1)} custom-call(s32[1]{0:T(128)} %bitcast.26.counts, s32[27,1,2048]{2,1,0:T(1,128)S(1)} %bitcast.31, s32[27,1,2048]{2,1,0:T(1,128)S(1)} %bitcast.36, bf16[64,2048]{1,0:T(8,128)(2,1)S(1)} %get-tuple-element.57.gpre, bf16[64,1728]{1,0:T(8,128)(2,1)S(1)} %get-tuple-element.52.w_t), custom_call_target="tpu_custom_call" | custom-call | tf_op jit(solution)/shard_map/local_scatter_blocks/pallas_call | solution.py:236
  62.0 2.4 %collective-permute-done.6.left = bf16[64,640]{1,0:T(8,128)(2,1)S(1)} collective-permute-done((bf16[64,640]{1,0:T(8,128)(2,1)S(1)}, bf16[64,640]{1,0:T(8,128)(2,1)S(1)}, u32[]{:S(2)}, u32[]{:S(2)}) %collective-permute-start.6) | collective-permute-done | bytes 81952 | tf_op jit(solution)/shard_map/ppermute | solution.py:412
  64.4 0.7 add_incoming.1
  65.1 2.6 %all-to-all-done.1 = bf16[128,5,2,128]{3,2,1,0:T(2,128)(2,1)S(1)} async-done(((bf16[128,5,2,128]{3,2,1,0:T(2,128)(2,1)}), bf16[128,5,2,128]{3,2,1,0:T(2,128)(2,1)S(1)}, u32[]{:S(2)}, u32[]{:S(2)}) %all-to-all-start.1) | async-done | bytes 327712 | tf_op jit(solution)/shard_map/all_to_all | solution.py:445
  67.7 1.2 %unpack_weights.1 = (f32[27,64,64]{2,1,0:T(8,128)}, f32[8,64,64]{2,1,0:T(8,128)}) custom-call(bf16[1280,128]{1,0:T(8,128)(2,1)S(1)} %bitcast.41), custom_call_target="tpu_custom_call" | custom-call | tf_op jit(solution)/shard_map/unpack_weights/pallas_call | solution.py:398
  (12 shorter events, 0.1 us)
Async XLA Ops:
  1.5 8.1 %collective-permute-start.1 = (bf16[64,640]{1,0:T(8,128)(2,1)S(1)}, bf16[64,640]{1,0:T(8,128)(2,1)S(1)}, u32[]{:S(2)}, u32[]{:S(2)}) collective-permute-start(bf16[64,640]{1,0:T(8,128)(2,1)S(1)} %pack_border.1), channel_id=1, source_target_pairs={{8,16},{24,32},{40,48},{56,64},{72,80},{88,96},{104,112},{16,8},{3... | collective-permute-start | bytes 245768 | tf_op jit(solution)/shard_map/ppermute | solution.py:412
  2.2 7.5 %collective-permute-start = (bf16[64,640]{1,0:T(8,128)(2,1)S(1)}, bf16[64,640]{1,0:T(8,128)(2,1)S(1)}, u32[]{:S(2)}, u32[]{:S(2)}) collective-permute-start(bf16[64,640]{1,0:T(8,128)(2,1)S(1)} %pack_border.1), channel_id=1, source_target_pairs={{0,8},{16,24},{32,40},{48,56},{64,72},{80,88},{96,104},{112,120},{... | collective-permute-start | bytes 245768 | tf_op jit(solution)/shard_map/ppermute | solution.py:412
  9.6 4.6 %copy-start.2 = (bf16[1,1,64,2048]{3,2,1,0:T(8,128)(2,1)S(1)}, bf16[1,1,64,2048]{3,2,1,0:T(8,128)(2,1)}, u32[]{:S(2)}) copy-start(bf16[1,1,64,2048]{3,2,1,0:T(8,128)(2,1)} %param.8) | copy-start | bytes 786436
  9.7 4.6 %copy-start = (s32[1,1,27,2048]{3,1,2,0:T(1,128)S(1)}, s32[1,1,27,2048]{3,1,2,0:T(1,128)}, u32[]{:S(2)}) copy-start(s32[1,1,27,2048]{3,1,2,0:T(1,128)} %param.10) | copy-start | bytes 663556
  9.7 4.6 %copy-start.1 = (s32[1,1,27,2048]{3,1,2,0:T(1,128)S(1)}, s32[1,1,27,2048]{3,1,2,0:T(1,128)}, u32[]{:S(2)}) copy-start(s32[1,1,27,2048]{3,1,2,0:T(1,128)} %param.11) | copy-start | bytes 663556
  9.7 4.6 %copy-start.3 = (bf16[1,1,64,512]{3,2,1,0:T(8,128)(2,1)S(1)}, bf16[1,1,64,512]{3,2,1,0:T(8,128)(2,1)}, u32[]{:S(2)}) copy-start(bf16[1,1,64,512]{3,2,1,0:T(8,128)(2,1)} %param.15) | copy-start | bytes 196612
  9.8 8.2 %collective-permute-start.3 = (bf16[3,64,640]{2,1,0:T(8,128)(2,1)S(1)}, bf16[3,64,640]{2,1,0:T(8,128)(2,1)S(1)}, u32[]{:S(2)}, u32[]{:S(2)}) collective-permute-start(bf16[3,64,640]{2,1,0:T(8,128)(2,1)S(1)} %pad_maximum_fusion.column), channel_id=1, source_target_pairs={{1,2},{3,4},{5,6},{2,1},{4,3},{6,5},{9,10},{11,12},{13,14},{10,9},... | collective-permute-start | bytes 737288 | tf_op jit(solution)/shard_map/ppermute | solution.py:412
  14.1 3.9 %collective-permute-start.2 = (bf16[3,64,640]{2,1,0:T(8,128)(2,1)S(1)}, bf16[3,64,640]{2,1,0:T(8,128)(2,1)S(1)}, u32[]{:S(2)}, u32[]{:S(2)}) collective-permute-start(bf16[3,64,640]{2,1,0:T(8,128)(2,1)S(1)} %pad_maximum_fusion.column), channel_id=1, source_target_pairs={{0,1},{2,3},{4,5},{6,7},{1,0},{3,2},{5,4},{7,6},{8,9},{10,11},{12,... | collective-permute-start | bytes 737288 | tf_op jit(solution)/shard_map/ppermute | solution.py:412
  14.2 0.7 %copy-start.4 = (s32[1,1,2,2048]{3,2,1,0:T(2,128)S(1)}, s32[1,1,2,2048]{3,2,1,0:T(2,128)}, u32[]{:S(2)}) copy-start(s32[1,1,2,2048]{3,2,1,0:T(2,128)} %param.12) | copy-start | bytes 49156
  22.1 24.5 %all-to-all-start = ((bf16[128,5,2,128]{3,2,1,0:T(2,128)(2,1)}), bf16[128,5,2,128]{3,2,1,0:T(2,128)(2,1)S(1)}, u32[]{:S(2)}, u32[]{:S(2)}) async-start(bf16[128,5,2,128]{3,2,1,0:T(2,128)(2,1)} %bitcast.10), calls=%async_computation | async-start | bytes 655360 | tf_op jit(solution)/shard_map/all_to_all | solution.py:435
  37.4 3.9 %collective-permute-start.4 = (bf16[3,64,640]{2,1,0:T(8,128)(2,1)S(1)}, bf16[3,64,640]{2,1,0:T(8,128)(2,1)S(1)}, u32[]{:S(2)}, u32[]{:S(2)}) collective-permute-start(bf16[3,64,640]{2,1,0:T(8,128)(2,1)S(1)} %get-tuple-element.53), channel_id=1, source_target_pairs={{0,1},{2,3},{4,5},{6,7},{1,0},{3,2},{5,4},{7,6},{8,9},{10,11},{12,... | collective-permute-start | bytes 737288 | tf_op jit(solution)/shard_map/ppermute | solution.py:412
  38.8 7.8 %collective-permute-start.5 = (bf16[3,64,640]{2,1,0:T(8,128)(2,1)S(1)}, bf16[3,64,640]{2,1,0:T(8,128)(2,1)S(1)}, u32[]{:S(2)}, u32[]{:S(2)}) collective-permute-start(bf16[3,64,640]{2,1,0:T(8,128)(2,1)S(1)} %get-tuple-element.54), channel_id=1, source_target_pairs={{1,2},{3,4},{5,6},{2,1},{4,3},{6,5},{9,10},{11,12},{13,14},{10,9},... | collective-permute-start | bytes 737288 | tf_op jit(solution)/shard_map/ppermute | solution.py:412
  47.3 20.3 %all-to-all-start.1 = ((bf16[128,5,2,128]{3,2,1,0:T(2,128)(2,1)}), bf16[128,5,2,128]{3,2,1,0:T(2,128)(2,1)S(1)}, u32[]{:S(2)}, u32[]{:S(2)}) async-start(bf16[128,5,2,128]{3,2,1,0:T(2,128)(2,1)} %bitcast.17), calls=%async_computation.1 | async-start | bytes 655360 | tf_op jit(solution)/shard_map/all_to_all | solution.py:445
  56.0 6.0 %collective-permute-start.7 = (bf16[64,640]{1,0:T(8,128)(2,1)S(1)}, bf16[64,640]{1,0:T(8,128)(2,1)S(1)}, u32[]{:S(2)}, u32[]{:S(2)}) collective-permute-start(bf16[64,640]{1,0:T(8,128)(2,1)S(1)} %get-tuple-element.68), channel_id=1, source_target_pairs={{8,16},{24,32},{40,48},{56,64},{72,80},{88,96},{104,112},{16,8},{3... | collective-permute-start | bytes 245768 | tf_op jit(solution)/shard_map/ppermute | solution.py:412
  56.7 7.7 %collective-permute-start.6 = (bf16[64,640]{1,0:T(8,128)(2,1)S(1)}, bf16[64,640]{1,0:T(8,128)(2,1)S(1)}, u32[]{:S(2)}, u32[]{:S(2)}) collective-permute-start(bf16[64,640]{1,0:T(8,128)(2,1)S(1)} %get-tuple-element.69), channel_id=1, source_target_pairs={{0,8},{16,24},{32,40},{48,56},{64,72},{80,88},{96,104},{112,120},{... | collective-permute-start | bytes 245768 | tf_op jit(solution)/shard_map/ppermute | solution.py:412

commit v5 on v4

--- a/solution.py
+++ b/solution.py
@@ -56,13 +56,15 @@
     low = low.astype(BF)
     low_ids = lax.broadcasted_iota(jnp.int32, (L, VB), 0).astype(F32).astype(BF)
     local = jnp.concatenate([feat[:, i * L:(i + 1) * L] for i in range(H)], axis=0)
+    slabs = {}
     for k in range(K):
         one_hot = pick(low[k:k + 1, :] == low_ids)
         parts = [mm(local, one_hot)]
         if remote and DIRS[k] != 4:
-            slab = halo[DIRS[k] % 3][DIRS[k] // 3, :, 0:VB]
-            slab = jnp.concatenate([slab[:, i * L:(i + 1) * L] for i in range(H)], axis=0)
-            parts.append(mm(slab, one_hot))
+            if DIRS[k] not in slabs:
+                slab = halo[DIRS[k] % 3][DIRS[k] // 3, :, 0:VB]
+                slabs[DIRS[k]] = jnp.concatenate([slab[:, i * L:(i + 1) * L] for i in range(H)], axis=0)
+            parts.append(mm(slabs[DIRS[k]], one_hot))
         high_k = high[k:k + 1, :]
         pieces = [part[i * C:(i + 1) * C, :] for part in parts for i in range(H)]
         got = pieces[0]
@@ -246,6 +248,10 @@
     )(counts, rows, frm, gpre_all, w_t)
 
 
+def in_hbm(array):
+    return pltpu.with_memory_space_constraint(array, pltpu.HBM)
+
+
 def border_pack_kernel(feat, grad, out, sems):
     a = pltpu.make_async_copy(feat.at[:, 0:VB], out.at[:, 0:VB], sems.at[0])
     b = pltpu.make_async_copy(grad.at[:, 0:CQ], out.at[:, VB:], sems.at[1])
@@ -264,7 +270,7 @@
         scratch_shapes=[pltpu.SemaphoreType.DMA((2,))],
         compiler_params=SMALL,
         name="pack_border",
-    )(pltpu.with_memory_space_constraint(feat, pltpu.HBM), pltpu.with_memory_space_constraint(grad, pltpu.HBM))
+    )(in_hbm(feat), in_hbm(grad))
 
 
 def sum_kernel(pieces, out):
@@ -424,8 +430,9 @@
     near, far = swapped(border, "gx", True), swapped(border, "gx", False)
     counts = counts.reshape(1)
     coarse_all, gpre_all, gsub, gdown, w_cat, w_t, wd_cat, wd_t = first_call(
-        counts, *[pltpu.with_memory_space_constraint(a, pltpu.HBM) for a in (feat, rows, frm, dmap, grad, w_sub, w_down)])
+        counts, *[in_hbm(a) for a in (feat, rows, frm, dmap, grad, w_sub, w_down)])
     near, far, gsub = lax.optimization_barrier((near, far, gsub))
+    dmap = in_hbm(dmap)
     column = jnp.stack([jnp.where(even_x, far, near), border, jnp.where(even_x, near, far)])
     near, far = swapped(column, "gy", True), swapped(column, "gy", False)
     coarse_all, gpre_all, gsub, gdown = rest_call(
@@ -435,13 +442,12 @@
     pieces = lax.all_to_all(packed.reshape(count, PAIRS, 2, 2 * C), ("gx", "gy"), 0, 0, tiled=True)
     gfeat, mid, out_near, out_far = border_scatter_call(side, rows, frm, dmap, gpre, split, w_t)
     near, far = swapped(out_near, "gy", True), swapped(out_far, "gy", False)
-    pieces, near, far = lax.optimization_barrier((pieces, near, far))
+    shape = pieces.shape
+    spread = sum_call(pieces.reshape(count * PIECE, 2 * C))
+    spread, gpre_all, mid = lax.optimization_barrier((spread, gpre_all, mid))
     total = mid + near.astype(F32) + far.astype(F32)
     near = swapped(jnp.where(even_x, total[2], total[0]).astype(BF), "gx", True)
     far = swapped(jnp.where(even_x, total[0], total[2]).astype(BF), "gx", False)
-    shape = pieces.shape
-    spread = sum_call(pieces.reshape(count * PIECE, 2 * C))
-    spread, gpre_all = lax.optimization_barrier((spread, gpre_all))
     gathered = lax.all_to_all(spread.reshape(shape), ("gx", "gy"), 0, 0, tiled=True).reshape(-1, 2 * C)
     gfeat_all = local_scatter_call(counts, rows, frm, gpre_all, w_t)
     coarse_out, grad_features = finish_call(coarse_all, gfeat_all, coarse, gfeat, total[1], near, far)

time: 69.6 us -> 66.3 us (0.953); the launches traced: 68.9 us -> 66.3 us
  Pallas kernels: 14.8 us -> 29.1 us
  waiting for transfers between devices: 12.4 us -> 4.2 us
  starting transfers between devices: 39.3 us -> 31.3 us
    ppermute x8, waiting for transfers between devices: 9.8 us -> 0.02 us  [swapped(): return lax.ppermute(block, axis, pairs + [(b, a) for a, b in pairs])]
    pallas_call x1, Pallas kernels: 0.84 us -> 6.37 us  [rest_call(): pl.pallas_call(rest_kernel, grid=(2,), in_specs=[pl.BlockSpec(memory_spac...]
    pallas_call x1, Pallas kernels: 1.37 us -> 6.3 us  [local_scatter_call(): pl.pallas_call(local_scatter_kernel, grid=(3,), in_specs=[pl.BlockSpec(me...]
    all_to_all x1, waiting for transfers between devices: 0.01 us -> 4.12 us  [shards(): lax.all_to_all(packed.reshape(count, PAIRS, 2, 2 * C), ('gx', 'gy'), 0, 0...]
    all_to_all x1, starting transfers between devices: 8.58 us -> 4.92 us  [shards(): lax.all_to_all(spread.reshape(shape), ('gx', 'gy'), 0, 0, tiled=True)]
    all_to_all x1, waiting for transfers between devices: 2.59 us -> 0.06 us  [shards(): lax.all_to_all(spread.reshape(shape), ('gx', 'gy'), 0, 0, tiled=True)]
    pallas_call x1, Pallas kernels: 2.05 us -> 4.51 us  [first_call(): pl.pallas_call(first_kernel, grid=(1,), in_specs=[pl.BlockSpec(memory_spa...]
    ppermute x8, starting transfers between devices: 18.4 us -> 16 us  [swapped(): return lax.ppermute(block, axis, pairs + [(b, a) for a, b in pairs])]
  transfers between devices with their start and end apart: 10 -> 10, of which waited for: 4 -> 2; matrix products, arithmetic and copies ran while one was open for 0% -> 0% of each run, Pallas kernels for 11% -> 34%
where the time goes in v5:
time: 66.3 us
  starting transfers between devices  31.3 us (47%)
  Pallas kernels  29.1 us (44%)
  waiting for transfers between devices  4.2 us (6%)
  between operations  1.49 us (2%)
    ppermute x8, starting transfers between devices, swapped(): return lax.ppermute(block, axis, pairs + [(b, a) for a, b in pairs])  16 us
    all_to_all x1, starting transfers between devices, shards(): lax.all_to_all(packed.reshape(count, PAIRS, 2, 2 * C), ('gx', 'gy'), 0, 0...  10.3 us
    pallas_call x1, Pallas kernels, rest_call(): pl.pallas_call(rest_kernel, grid=(2,), in_specs=[pl.BlockSpec(memory_spac...  6.37 us
    pallas_call x1, Pallas kernels, local_scatter_call(): pl.pallas_call(local_scatter_kernel, grid=(3,), in_specs=[pl.BlockSpec(me...  6.3 us
    all_to_all x1, starting transfers between devices, shards(): lax.all_to_all(spread.reshape(shape), ('gx', 'gy'), 0, 0, tiled=True)  4.92 us
    pallas_call x1, Pallas kernels, border_call(): pl.pallas_call(border_kernel, grid=(1,), in_specs=[pl.BlockSpec(memory_sp...  4.76 us
    pallas_call x1, Pallas kernels, first_call(): pl.pallas_call(first_kernel, grid=(1,), in_specs=[pl.BlockSpec(memory_spa...  4.51 us
    all_to_all x1, waiting for transfers between devices, shards(): lax.all_to_all(packed.reshape(count, PAIRS, 2, 2 * C), ('gx', 'gy'), 0, 0...  4.12 us
  transfers between devices with their start and end apart: 10, of which 2 were waited for; matrix products, arithmetic and copies ran while one was open for 0% of the time, Pallas kernels for 34%

profile of v5, /device:TPU:1, one launch (start us, length us, event | category | flops | bytes accessed | tf_op | source)
XLA Modules:
  0.0 66.3 jit_solution(1082514342177086762)
XLA Ops:
  0.6 0.9 %pack_border.1 = bf16[64,640]{1,0:T(8,128)(2,1)S(1)} custom-call(bf16[64,2048]{1,0:T(8,128)(2,1)} %bitcast.37, bf16[64,512]{1,0:T(8,128)(2,1)} %bitcast.43), custom_call_target="tpu_custom_call" | custom-call | tf_op jit(solution)/shard_map/pack_border/pallas_call | solution.py:265
  1.5 0.7 %collective-permute-start.1 = (bf16[64,640]{1,0:T(8,128)(2,1)S(1)}, bf16[64,640]{1,0:T(8,128)(2,1)S(1)}, u32[]{:S(2)}, u32[]{:S(2)}) collective-permute-start(bf16[64,640]{1,0:T(8,128)(2,1)S(1)} %pack_border.1), channel_id=1, source_target_pairs={{8,16},{24,32},{40,48},{56,64},{72,80},{88,96},{104,112},{16,8},{3... | collective-permute-start | bytes 245768 | tf_op jit(solution)/shard_map/ppermute | solution.py:418
  2.2 4.7 %collective-permute-start = (bf16[64,640]{1,0:T(8,128)(2,1)S(1)}, bf16[64,640]{1,0:T(8,128)(2,1)S(1)}, u32[]{:S(2)}, u32[]{:S(2)}) collective-permute-start(bf16[64,640]{1,0:T(8,128)(2,1)S(1)} %pack_border.1), channel_id=1, source_target_pairs={{0,8},{16,24},{32,40},{48,56},{64,72},{80,88},{96,104},{112,120},{... | collective-permute-start | bytes 245768 | tf_op jit(solution)/shard_map/ppermute | solution.py:418
  7.6 4.5 %first_local_block.1 = (bf16[64,512]{1,0:T(8,128)(2,1)}, bf16[64,2048]{1,0:T(8,128)(2,1)S(1)}, f32[64,1728]{1,0:T(8,128)S(1)}, f32[512,64]{1,0:T(8,128)S(1)}, bf...) custom-call(s32[1]{0:T(128)} %bitcast.24.counts, ...), custom_call_target="tpu_custom_call" | custom-call | tf_op jit(solution)/shard_map/first_local_block/pallas_call | solution.py:207
  12.1 0.0 collective-permute-done.1
  12.1 0.0 collective-permute-done
  12.1 0.0 copy-start.2
  12.1 0.0 copy-start
  12.1 0.0 copy-start.1
  12.2 0.0 copy-start.3
  12.2 2.1 %collective-permute-start.3 = (bf16[3,64,640]{2,1,0:T(8,128)(2,1)S(1)}, bf16[3,64,640]{2,1,0:T(8,128)(2,1)S(1)}, u32[]{:S(2)}, u32[]{:S(2)}) collective-permute-start(bf16[3,64,640]{2,1,0:T(8,128)(2,1)S(1)} %pad_maximum_fusion.column), channel_id=1, source_target_pairs={{1,2},{3,4},{5,6},{2,1},{4,3},{6,5},{9,10},{11,12},{13,14},{10,9},... | collective-permute-start | bytes 737288 | tf_op jit(solution)/shard_map/ppermute | solution.py:418
  14.3 0.1 collective-permute-start.2
  14.4 6.4 %other_local_blocks.1 = (bf16[64,512]{1,0:T(8,128)(2,1)}, bf16[64,2048]{1,0:T(8,128)(2,1)S(1)}, f32[64,1728]{1,0:T(8,128)S(1)}, f32[512,64]{1,0:T(8,128)S(1)}) custom-call(s32[1]{0:T(128)} %bitcast.25.counts, bf16[64,2048]{1,0:T(8,128)(2,1)S(1)} %bitcast.39, s32[27,1,2048]{2,1,0:T(1,128)S(1)} %bitcast.28, ...), custom_call_target="tpu_custom_call", output_to_operand_aliasing={{0}: (11, {}), {1}: (12, {})} | custom-call | tf_op jit(solution)/shard_map/other_local_blocks/pallas_call | solution.py:222
  20.8 4.8 %border_block.1 = (f32[64,128]{1,0:T(8,128)S(1)}, bf16[1280,128]{1,0:T(8,128)(2,1)}, bf16[64,512]{1,0:T(8,128)(2,1)S(1)}, bf16[128,512]{1,0:T(8,128)(2,1)S(1)}) custom-call(s32[1]{0:T(128)} %bitcast.6.side, bf16[64,2048]{1,0:T(8,128)(2,1)S(1)} %bitcast.40, s32[27,1,2048]{2,1,0:T(1,128)S(1)} %bitcast.29, s32[27,1,2048]{2,1,0:T(1,128)S(1)} %bitcast.34, ...), custom_call_target="tpu_custom_call" | custom-call | tf_op jit(solution)/shard_map/border_block/pallas_call | solution.py:322
  25.6 10.3 %all-to-all-start = ((bf16[128,5,2,128]{3,2,1,0:T(2,128)(2,1)}), bf16[128,5,2,128]{3,2,1,0:T(2,128)(2,1)S(1)}, u32[]{:S(2)}, u32[]{:S(2)}) async-start(bf16[128,5,2,128]{3,2,1,0:T(2,128)(2,1)} %bitcast.10), calls=%async_computation | async-start | bytes 655360 | tf_op jit(solution)/shard_map/all_to_all | solution.py:442
  35.9 3.7 %border_scatter_block.1 = (f32[64,512]{1,0:T(8,128)S(1)}, f32[3,64,640]{2,1,0:T(8,128)S(1)}, bf16[3,64,640]{2,1,0:T(8,128)(2,1)S(1)}, bf16[3,64,640]{2,1,0:T(8,128)(2,1)S(1)}) custom-call(s32[1]{0:T(128)} %bitcast.6.side, s32[27,1,2048]{2,1,0:T(1,128)S(1)} %bitcast.30, s32[27,1,2048]{2,1,0:T(1,128)S(1)} %bitcast.35, s32[2,2048]{1,0:T(2,128)} %bitcast.52, ...), custom_call_target="tpu_custom_call" | custom-call | tf_op jit(solution)/shard_map/border_scatter_block/pallas_call | solution.py:356
  39.5 1.3 %collective-permute-start.4 = (bf16[3,64,640]{2,1,0:T(8,128)(2,1)S(1)}, bf16[3,64,640]{2,1,0:T(8,128)(2,1)S(1)}, u32[]{:S(2)}, u32[]{:S(2)}) collective-permute-start(bf16[3,64,640]{2,1,0:T(8,128)(2,1)S(1)} %get-tuple-element.57), channel_id=1, source_target_pairs={{0,1},{2,3},{4,5},{6,7},{1,0},{3,2},{5,4},{7,6},{8,9},{10,11},{12,... | collective-permute-start | bytes 737288 | tf_op jit(solution)/shard_map/ppermute | solution.py:418
  40.9 2.6 %collective-permute-start.5 = (bf16[3,64,640]{2,1,0:T(8,128)(2,1)S(1)}, bf16[3,64,640]{2,1,0:T(8,128)(2,1)S(1)}, u32[]{:S(2)}, u32[]{:S(2)}) collective-permute-start(bf16[3,64,640]{2,1,0:T(8,128)(2,1)S(1)} %get-tuple-element.58), channel_id=1, source_target_pairs={{1,2},{3,4},{5,6},{2,1},{4,3},{6,5},{9,10},{11,12},{13,14},{10,9},... | collective-permute-start | bytes 737288 | tf_op jit(solution)/shard_map/ppermute | solution.py:418
  43.5 4.1 %all-to-all-done = bf16[128,5,2,128]{3,2,1,0:T(2,128)(2,1)S(1)} async-done(((bf16[128,5,2,128]{3,2,1,0:T(2,128)(2,1)}), bf16[128,5,2,128]{3,2,1,0:T(2,128)(2,1)S(1)}, u32[]{:S(2)}, u32[]{:S(2)}) %all-to-all-start) | async-done | bytes 327712 | tf_op jit(solution)/shard_map/all_to_all | solution.py:442
  47.6 0.8 %sum_pieces.1 = bf16[1280,128]{1,0:T(8,128)(2,1)} custom-call(bf16[1280,128]{1,0:T(8,128)(2,1)S(1)} %bitcast.42), custom_call_target="tpu_custom_call" | custom-call | tf_op jit(solution)/shard_map/sum_pieces/pallas_call | solution.py:289
  48.4 4.9 %all-to-all-start.1 = ((bf16[128,5,2,128]{3,2,1,0:T(2,128)(2,1)}), bf16[128,5,2,128]{3,2,1,0:T(2,128)(2,1)S(1)}, u32[]{:S(2)}, u32[]{:S(2)}) async-start(bf16[128,5,2,128]{3,2,1,0:T(2,128)(2,1)} %bitcast.17), calls=%async_computation.1 | async-start | bytes 655360 | tf_op jit(solution)/shard_map/all_to_all | solution.py:451
  53.3 0.0 collective-permute-done.4
  53.3 0.0 collective-permute-done.5
  53.4 0.1 convert_add_fusion
  53.5 0.7 %collective-permute-start.7 = (bf16[64,640]{1,0:T(8,128)(2,1)S(1)}, bf16[64,640]{1,0:T(8,128)(2,1)S(1)}, u32[]{:S(2)}, u32[]{:S(2)}) collective-permute-start(bf16[64,640]{1,0:T(8,128)(2,1)S(1)} %get-tuple-element.64), channel_id=1, source_target_pairs={{8,16},{24,32},{40,48},{56,64},{72,80},{88,96},{104,112},{16,8},{3... | collective-permute-start | bytes 245768 | tf_op jit(solution)/shard_map/ppermute | solution.py:418
  54.1 3.9 %collective-permute-start.6 = (bf16[64,640]{1,0:T(8,128)(2,1)S(1)}, bf16[64,640]{1,0:T(8,128)(2,1)S(1)}, u32[]{:S(2)}, u32[]{:S(2)}) collective-permute-start(bf16[64,640]{1,0:T(8,128)(2,1)S(1)} %get-tuple-element.65), channel_id=1, source_target_pairs={{0,8},{16,24},{32,40},{48,56},{64,72},{80,88},{96,104},{112,120},{... | collective-permute-start | bytes 245768 | tf_op jit(solution)/shard_map/ppermute | solution.py:418
  58.1 6.3 %local_scatter_blocks.1.gfeat_i = bf16[64,2048]{1,0:T(8,128)(2,1)} custom-call(s32[1]{0:T(128)} %bitcast.26.counts, s32[27,1,2048]{2,1,0:T(1,128)S(1)} %bitcast.31, s32[27,1,2048]{2,1,0:T(1,128)S(1)} %bitcast.36, bf16[64,2048]{1,0:T(8,128)(2,1)S(1)} %get-tuple-element.53.gpre, bf16[64,1728]{1,0:T(8,128)(2,1)S(1)} %get-tuple-element.51.w_t), custom_call_target="tpu_custom_call" | custom-call | tf_op jit(solution)/shard_map/local_scatter_blocks/pallas_call | solution.py:238
  64.4 0.0 collective-permute-done.7.right
  64.4 0.0 collective-permute-done.6.left
  64.4 0.7 %add_incoming.1 = (bf16[64,512]{1,0:T(8,128)(2,1)}, bf16[64,2048]{1,0:T(8,128)(2,1)}) custom-call(bf16[64,512]{1,0:T(8,128)(2,1)} %get-tuple-element.42.coarse_i, bf16[64,2048]{1,0:T(8,128)(2,1)} %local_scatter_blocks.1.gfeat_i, f32[64,128]{1,0:T(8,128)S(1)} %get-tuple-element.54.coarse, ...), custom_call_target="tpu_custom_call", output_to_operand_aliasing={{0}: (0, {}), {1}: (1, {})} | custom-call | tf_op jit(solution)/shard_map/add_incoming/pallas_call | solution.py:378
  65.0 0.1 all-to-all-done.1
  65.1 1.2 %unpack_weights.1 = (f32[27,64,64]{2,1,0:T(8,128)}, f32[8,64,64]{2,1,0:T(8,128)}) custom-call(bf16[1280,128]{1,0:T(8,128)(2,1)S(1)} %bitcast.41), custom_call_target="tpu_custom_call" | custom-call | tf_op jit(solution)/shard_map/unpack_weights/pallas_call | solution.py:404
  (10 shorter events, 0.1 us)
Async XLA Ops:
  1.5 10.6 %collective-permute-start.1 = (bf16[64,640]{1,0:T(8,128)(2,1)S(1)}, bf16[64,640]{1,0:T(8,128)(2,1)S(1)}, u32[]{:S(2)}, u32[]{:S(2)}) collective-permute-start(bf16[64,640]{1,0:T(8,128)(2,1)S(1)} %pack_border.1), channel_id=1, source_target_pairs={{8,16},{24,32},{40,48},{56,64},{72,80},{88,96},{104,112},{16,8},{3... | collective-permute-start | bytes 245768 | tf_op jit(solution)/shard_map/ppermute | solution.py:418
  2.2 9.9 %collective-permute-start = (bf16[64,640]{1,0:T(8,128)(2,1)S(1)}, bf16[64,640]{1,0:T(8,128)(2,1)S(1)}, u32[]{:S(2)}, u32[]{:S(2)}) collective-permute-start(bf16[64,640]{1,0:T(8,128)(2,1)S(1)} %pack_border.1), channel_id=1, source_target_pairs={{0,8},{16,24},{32,40},{48,56},{64,72},{80,88},{96,104},{112,120},{... | collective-permute-start | bytes 245768 | tf_op jit(solution)/shard_map/ppermute | solution.py:418
  12.1 2.3 %copy-start.2 = (bf16[1,1,64,2048]{3,2,1,0:T(8,128)(2,1)S(1)}, bf16[1,1,64,2048]{3,2,1,0:T(8,128)(2,1)}, u32[]{:S(2)}) copy-start(bf16[1,1,64,2048]{3,2,1,0:T(8,128)(2,1)} %param.8) | copy-start | bytes 786436
  12.1 2.3 %copy-start = (s32[1,1,27,2048]{3,1,2,0:T(1,128)S(1)}, s32[1,1,27,2048]{3,1,2,0:T(1,128)}, u32[]{:S(2)}) copy-start(s32[1,1,27,2048]{3,1,2,0:T(1,128)} %param.10) | copy-start | bytes 663556
  12.1 2.3 %copy-start.1 = (s32[1,1,27,2048]{3,1,2,0:T(1,128)S(1)}, s32[1,1,27,2048]{3,1,2,0:T(1,128)}, u32[]{:S(2)}) copy-start(s32[1,1,27,2048]{3,1,2,0:T(1,128)} %param.11) | copy-start | bytes 663556
  12.2 2.3 %copy-start.3 = (bf16[1,1,64,512]{3,2,1,0:T(8,128)(2,1)S(1)}, bf16[1,1,64,512]{3,2,1,0:T(8,128)(2,1)}, u32[]{:S(2)}) copy-start(bf16[1,1,64,512]{3,2,1,0:T(8,128)(2,1)} %param.15) | copy-start | bytes 196612
  12.2 8.6 %collective-permute-start.3 = (bf16[3,64,640]{2,1,0:T(8,128)(2,1)S(1)}, bf16[3,64,640]{2,1,0:T(8,128)(2,1)S(1)}, u32[]{:S(2)}, u32[]{:S(2)}) collective-permute-start(bf16[3,64,640]{2,1,0:T(8,128)(2,1)S(1)} %pad_maximum_fusion.column), channel_id=1, source_target_pairs={{1,2},{3,4},{5,6},{2,1},{4,3},{6,5},{9,10},{11,12},{13,14},{10,9},... | collective-permute-start | bytes 737288 | tf_op jit(solution)/shard_map/ppermute | solution.py:418
  14.3 6.5 %collective-permute-start.2 = (bf16[3,64,640]{2,1,0:T(8,128)(2,1)S(1)}, bf16[3,64,640]{2,1,0:T(8,128)(2,1)S(1)}, u32[]{:S(2)}, u32[]{:S(2)}) collective-permute-start(bf16[3,64,640]{2,1,0:T(8,128)(2,1)S(1)} %pad_maximum_fusion.column), channel_id=1, source_target_pairs={{0,1},{2,3},{4,5},{6,7},{1,0},{3,2},{5,4},{7,6},{8,9},{10,11},{12,... | collective-permute-start | bytes 737288 | tf_op jit(solution)/shard_map/ppermute | solution.py:418
  25.6 22.1 %all-to-all-start = ((bf16[128,5,2,128]{3,2,1,0:T(2,128)(2,1)}), bf16[128,5,2,128]{3,2,1,0:T(2,128)(2,1)S(1)}, u32[]{:S(2)}, u32[]{:S(2)}) async-start(bf16[128,5,2,128]{3,2,1,0:T(2,128)(2,1)} %bitcast.10), calls=%async_computation | async-start | bytes 655360 | tf_op jit(solution)/shard_map/all_to_all | solution.py:442
  39.5 13.8 %collective-permute-start.4 = (bf16[3,64,640]{2,1,0:T(8,128)(2,1)S(1)}, bf16[3,64,640]{2,1,0:T(8,128)(2,1)S(1)}, u32[]{:S(2)}, u32[]{:S(2)}) collective-permute-start(bf16[3,64,640]{2,1,0:T(8,128)(2,1)S(1)} %get-tuple-element.57), channel_id=1, source_target_pairs={{0,1},{2,3},{4,5},{6,7},{1,0},{3,2},{5,4},{7,6},{8,9},{10,11},{12,... | collective-permute-start | bytes 737288 | tf_op jit(solution)/shard_map/ppermute | solution.py:418
  40.9 12.5 %collective-permute-start.5 = (bf16[3,64,640]{2,1,0:T(8,128)(2,1)S(1)}, bf16[3,64,640]{2,1,0:T(8,128)(2,1)S(1)}, u32[]{:S(2)}, u32[]{:S(2)}) collective-permute-start(bf16[3,64,640]{2,1,0:T(8,128)(2,1)S(1)} %get-tuple-element.58), channel_id=1, source_target_pairs={{1,2},{3,4},{5,6},{2,1},{4,3},{6,5},{9,10},{11,12},{13,14},{10,9},... | collective-permute-start | bytes 737288 | tf_op jit(solution)/shard_map/ppermute | solution.py:418
  48.4 16.7 %all-to-all-start.1 = ((bf16[128,5,2,128]{3,2,1,0:T(2,128)(2,1)}), bf16[128,5,2,128]{3,2,1,0:T(2,128)(2,1)S(1)}, u32[]{:S(2)}, u32[]{:S(2)}) async-start(bf16[128,5,2,128]{3,2,1,0:T(2,128)(2,1)} %bitcast.17), calls=%async_computation.1 | async-start | bytes 655360 | tf_op jit(solution)/shard_map/all_to_all | solution.py:451
  53.5 10.9 %collective-permute-start.7 = (bf16[64,640]{1,0:T(8,128)(2,1)S(1)}, bf16[64,640]{1,0:T(8,128)(2,1)S(1)}, u32[]{:S(2)}, u32[]{:S(2)}) collective-permute-start(bf16[64,640]{1,0:T(8,128)(2,1)S(1)} %get-tuple-element.64), channel_id=1, source_target_pairs={{8,16},{24,32},{40,48},{56,64},{72,80},{88,96},{104,112},{16,8},{3... | collective-permute-start | bytes 245768 | tf_op jit(solution)/shard_map/ppermute | solution.py:418
  54.1 10.2 %collective-permute-start.6 = (bf16[64,640]{1,0:T(8,128)(2,1)S(1)}, bf16[64,640]{1,0:T(8,128)(2,1)S(1)}, u32[]{:S(2)}, u32[]{:S(2)}) collective-permute-start(bf16[64,640]{1,0:T(8,128)(2,1)S(1)} %get-tuple-element.65), channel_id=1, source_target_pairs={{0,8},{16,24},{32,40},{48,56},{64,72},{80,88},{96,104},{112,120},{... | collective-permute-start | bytes 245768 | tf_op jit(solution)/shard_map/ppermute | solution.py:418

commit v6 on v5

--- a/solution.py
+++ b/solution.py
@@ -128,7 +128,7 @@
 def one_local(block, counts, feat, rows, frm, dmap, grad, w_cat, wd_cat, wd_t, outs, source):
     coarse_o, gpre_o, gsub_o, gdown_o = outs
 
-    @pl.when(block < counts[0])
+    @pl.when(block < counts[0, 0])
     def _():
         coarse, gpre, gsub, gdown, _ = forward_work(
             False, block * VB, feat, rows, frm, dmap, grad, None, w_cat, wd_cat, wd_t, source)
@@ -137,7 +137,7 @@
         gsub_o[...] += gsub
         gdown_o[...] += gdown
 
-    @pl.when(block >= counts[0])
+    @pl.when(block >= counts[0, 0])
     def _():
         coarse_o[...] = jnp.zeros_like(coarse_o)
 
@@ -167,16 +167,23 @@
 def local_scatter_kernel(counts, rows, frm, gpre, w_t, gfeat_o, spread):
     block = pl.program_id(0) + 1
 
-    @pl.when(block < counts[0])
+    @pl.when(block < counts[0, 0])
     def _():
         gfeat_o[...] = scatter_work(False, block * VB, rows, frm, gpre[...], w_t, spread).astype(BF)
 
-    @pl.when(block >= counts[0])
+    @pl.when(block >= counts[0, 0])
     def _():
         gfeat_o[...] = jnp.zeros_like(gfeat_o)
 
 
+WHOLE = pl.BlockSpec(memory_space=pltpu.VMEM)
+
+
 def full(shape):
+    return WHOLE
+
+
+def piped(shape):
     return pl.BlockSpec(shape, lambda i: (0,) * len(shape))
 
 
@@ -207,7 +214,7 @@
     return pl.pallas_call(
         first_kernel,
         grid=(1,),
-        in_specs=[pl.BlockSpec(memory_space=pltpu.SMEM)] + table_specs(1) + [full((K, C, C)), full((8, C, C))],
+        in_specs=[pl.BlockSpec(memory_space=pltpu.SMEM)] + table_specs(1) + [piped((K, C, C)), piped((8, C, C))],
         out_specs=[columns((C, CQ), 1), columns((C, VB), 1), full((C, KC)), full((8 * C, C))]
         + [full(w) for w in weights],
         out_shape=[sd((C, CROWS), BF), sd((C, ROWS), BF), sd((C, KC), F32), sd((8 * C, C), F32)]
@@ -264,9 +271,9 @@
 def border_pack(feat, grad):
     return pl.pallas_call(
         border_pack_kernel,
-        in_specs=[pl.BlockSpec(memory_space=pltpu.HBM), pl.BlockSpec(memory_space=pltpu.HBM)],
-        out_specs=pl.BlockSpec(memory_space=pltpu.VMEM),
-        out_shape=jax.ShapeDtypeStruct((C, WIDE), BF),
+        in_specs=[pl.BlockSpec(memory_space=pltpu.HBM)] * 2,
+        out_specs=WHOLE,
+        out_shape=sd((C, WIDE), BF),
         scratch_shapes=[pltpu.SemaphoreType.DMA((2,))],
         compiler_params=SMALL,
         name="pack_border",
@@ -290,7 +297,7 @@
         sum_kernel,
         grid=(1,),
         in_specs=[full(pieces.shape)],
-        out_specs=full(pieces.shape),
+        out_specs=piped(pieces.shape),
         out_shape=jax.ShapeDtypeStruct(pieces.shape, BF),
         compiler_params=SMALL,
         name="sum_pieces",
@@ -324,7 +331,7 @@
         grid=(1,),
         in_specs=[pl.BlockSpec(memory_space=pltpu.SMEM)] + table_specs(0) + [slab, slab, slab, full((C, KC)), full((C, 8 * C)), full((C, 8 * C)),
                                    full((C, KC)), full((8 * C, C))],
-        out_specs=[full((C, CQ)), full((count * PIECE, 2 * C)), full((C, VB)), full((2 * C, VB))],
+        out_specs=[full((C, CQ)), piped((count * PIECE, 2 * C)), full((C, VB)), full((2 * C, VB))],
         out_shape=[sd((C, CQ), F32), sd((count * PIECE, 2 * C), BF), sd((C, VB), BF), sd((2 * C, VB), BF)],
         scratch_shapes=[SOURCE, pltpu.VMEM((3, C, WIDE), BF), pltpu.VMEM((3, C, WIDE), BF)],
         compiler_params=LIMIT,
@@ -405,7 +412,7 @@
         functools.partial(weights_kernel, scale),
         grid=(1,),
         in_specs=[full(packed.shape)],
-        out_specs=[full((K, C, C)), full((8, C, C))],
+        out_specs=[piped((K, C, C)), piped((8, C, C))],
         out_shape=[sd((K, C, C), F32), sd((8, C, C), F32)],
         compiler_params=SMALL,
         name="unpack_weights",
@@ -428,11 +435,9 @@
     even_x, even_y = lax.axis_index("gx") % 2 == 0, lax.axis_index("gy") % 2 == 0
     side = even_y.astype(jnp.int32).reshape(1)
     near, far = swapped(border, "gx", True), swapped(border, "gx", False)
-    counts = counts.reshape(1)
     coarse_all, gpre_all, gsub, gdown, w_cat, w_t, wd_cat, wd_t = first_call(
-        counts, *[in_hbm(a) for a in (feat, rows, frm, dmap, grad, w_sub, w_down)])
+        counts, *[in_hbm(a) for a in (feat, rows, frm)], dmap, *[in_hbm(a) for a in (grad, w_sub, w_down)])
     near, far, gsub = lax.optimization_barrier((near, far, gsub))
-    dmap = in_hbm(dmap)
     column = jnp.stack([jnp.where(even_x, far, near), border, jnp.where(even_x, near, far)])
     near, far = swapped(column, "gy", True), swapped(column, "gy", False)
     coarse_all, gpre_all, gsub, gdown = rest_call(

time: 66.3 us -> 64 us (0.965)
  Pallas kernels: 29.1 us -> 19.1 us
  waiting for transfers between devices: 4.2 us -> 12.6 us
  starting transfers between devices: 31.3 us -> 30 us
    pallas_call x1, Pallas kernels: 6.37 us -> 0.87 us  [rest_call(): pl.pallas_call(rest_kernel, grid=(2,), in_specs=[pl.BlockSpec(memory_spac...]
    ppermute x8, waiting for transfers between devices: 0.02 us -> 5.18 us  [swapped(): return lax.ppermute(block, axis, pairs + [(b, a) for a, b in pairs])]
    pallas_call x1, Pallas kernels: 6.3 us -> 3.19 us  [local_scatter_call(): pl.pallas_call(local_scatter_kernel, grid=(3,), in_specs=[pl.BlockSpec(me...]
    all_to_all x1, waiting for transfers between devices: 0.06 us -> 2.57 us  [shards(): lax.all_to_all(spread.reshape(shape), ('gx', 'gy'), 0, 0, tiled=True)]
    all_to_all x1, starting transfers between devices: 10.3 us -> 9.49 us  [shards(): lax.all_to_all(packed.reshape(count, PAIRS, 2, 2 * C), ('gx', 'gy'), 0, 0...]
    pallas_call x1, Pallas kernels: 3.68 us -> 2.98 us  [border_scatter_call(): pl.pallas_call(border_scatter_kernel, grid=(1,), in_specs=[pl.BlockSpec(m...]
    all_to_all x1, waiting for transfers between devices: 4.12 us -> 4.82 us  [shards(): lax.all_to_all(packed.reshape(count, PAIRS, 2, 2 * C), ('gx', 'gy'), 0, 0...]
    pallas_call x1, Pallas kernels: 4.76 us -> 4.08 us  [border_call(): pl.pallas_call(border_kernel, grid=(1,), in_specs=[pl.BlockSpec(memory_sp...]
  transfers between devices with their start and end apart: 10 -> 10, of which waited for: 2 -> 4; matrix products, arithmetic and copies ran while one was open for 0% -> 0% of each run, Pallas kernels for 34% -> 21%
where the time goes in v6:
time: 64 us; the launch traced here: 63.5 us
  starting transfers between devices  30 us (47%)
  Pallas kernels  19.1 us (30%)
  waiting for transfers between devices  12.6 us (20%)
  between operations  1.5 us (2%)
    ppermute x8, starting transfers between devices, swapped(): return lax.ppermute(block, axis, pairs + [(b, a) for a, b in pairs])  16 us
    all_to_all x1, starting transfers between devices, shards(): lax.all_to_all(packed.reshape(count, PAIRS, 2, 2 * C), ('gx', 'gy'), 0, 0...  9.49 us
    ppermute x8, waiting for transfers between devices, swapped(): return lax.ppermute(block, axis, pairs + [(b, a) for a, b in pairs])  5.18 us
    all_to_all x1, waiting for transfers between devices, shards(): lax.all_to_all(packed.reshape(count, PAIRS, 2, 2 * C), ('gx', 'gy'), 0, 0...  4.82 us
    pallas_call x1, Pallas kernels, first_call(): pl.pallas_call(first_kernel, grid=(1,), in_specs=[pl.BlockSpec(memory_spa...  4.51 us
    all_to_all x1, starting transfers between devices, shards(): lax.all_to_all(spread.reshape(shape), ('gx', 'gy'), 0, 0, tiled=True)  4.44 us
    pallas_call x1, Pallas kernels, border_call(): pl.pallas_call(border_kernel, grid=(1,), in_specs=[pl.BlockSpec(memory_sp...  4.08 us
    pallas_call x1, Pallas kernels, local_scatter_call(): pl.pallas_call(local_scatter_kernel, grid=(3,), in_specs=[pl.BlockSpec(me...  3.19 us
  transfers between devices with their start and end apart: 10, of which 4 were waited for; matrix products, arithmetic and copies ran while one was open for 0% of the time, Pallas kernels for 21%

profile of v6, /device:TPU:1, one launch (start us, length us, event | category | flops | bytes accessed | tf_op | source)
XLA Modules:
  0.0 63.5 jit_solution(2990826352134485683)
XLA Ops:
  0.6 0.9 %pack_border.1 = bf16[64,640]{1,0:T(8,128)(2,1)S(1)} custom-call(bf16[64,2048]{1,0:T(8,128)(2,1)} %bitcast.33, bf16[64,512]{1,0:T(8,128)(2,1)} %bitcast.39), custom_call_target="tpu_custom_call" | custom-call | tf_op jit(solution)/shard_map/pack_border/pallas_call | solution.py:272
  1.5 0.7 %collective-permute-start.1 = (bf16[64,640]{1,0:T(8,128)(2,1)S(1)}, bf16[64,640]{1,0:T(8,128)(2,1)S(1)}, u32[]{:S(2)}, u32[]{:S(2)}) collective-permute-start(bf16[64,640]{1,0:T(8,128)(2,1)S(1)} %pack_border.1), channel_id=1, source_target_pairs={{8,16},{24,32},{40,48},{56,64},{72,80},{88,96},{104,112},{16,8},{3... | collective-permute-start | bytes 245768 | tf_op jit(solution)/shard_map/ppermute | solution.py:425
  2.2 4.7 %collective-permute-start = (bf16[64,640]{1,0:T(8,128)(2,1)S(1)}, bf16[64,640]{1,0:T(8,128)(2,1)S(1)}, u32[]{:S(2)}, u32[]{:S(2)}) collective-permute-start(bf16[64,640]{1,0:T(8,128)(2,1)S(1)} %pack_border.1), channel_id=1, source_target_pairs={{0,8},{16,24},{32,40},{48,56},{64,72},{80,88},{96,104},{112,120},{... | collective-permute-start | bytes 245768 | tf_op jit(solution)/shard_map/ppermute | solution.py:425
  7.6 0.1 copy-done.4
  7.7 4.5 %first_local_block.1 = (bf16[64,512]{1,0:T(8,128)(2,1)}, bf16[64,2048]{1,0:T(8,128)(2,1)S(1)}, f32[64,1728]{1,0:T(8,128)S(1)}, f32[512,64]{1,0:T(8,128)S(1)}, bf...) custom-call(s32[1,1]{1,0:T(1,128)S(6)} %copy.20.counts, ...), custom_call_target="tpu_custom_call" | custom-call | tf_op jit(solution)/shard_map/first_local_block/pallas_call | solution.py:214
  12.2 0.0 collective-permute-done.1
  12.2 0.0 copy-start.2
  12.2 0.0 copy-start
  12.2 0.0 copy-start.1
  12.2 0.0 copy-start.3
  12.3 2.1 %collective-permute-start.3 = (bf16[3,64,640]{2,1,0:T(8,128)(2,1)S(1)}, bf16[3,64,640]{2,1,0:T(8,128)(2,1)S(1)}, u32[]{:S(2)}, u32[]{:S(2)}) collective-permute-start(bf16[3,64,640]{2,1,0:T(8,128)(2,1)S(1)} %pad_maximum_fusion.column), channel_id=1, source_target_pairs={{1,2},{3,4},{5,6},{2,1},{4,3},{6,5},{9,10},{11,12},{13,14},{10,9},... | collective-permute-start | bytes 737288 | tf_op jit(solution)/shard_map/ppermute | solution.py:425
  14.4 0.1 collective-permute-start.2
  14.5 0.9 %other_local_blocks.1 = (bf16[64,512]{1,0:T(8,128)(2,1)}, bf16[64,2048]{1,0:T(8,128)(2,1)S(1)}, f32[64,1728]{1,0:T(8,128)S(1)}, f32[512,64]{1,0:T(8,128)S(1)}) custom-call(s32[1,1]{1,0:T(1,128)S(6)} %copy.20.counts, bf16[64,2048]{1,0:T(8,128)(2,1)S(1)} %bitcast.35, s32[27,1,2048]{2,1,0:T(1,128)S(1)} %bitcast.24, ...), custom_call_target="tpu_custom_call", output_to_operand_aliasing={{0}: (11, {}), {1}: (12, {})} | custom-call | tf_op jit(solution)/shard_map/other_local_blocks/pallas_call | solution.py:229
  15.4 4.6 %collective-permute-done.3.far = bf16[3,64,640]{2,1,0:T(8,128)(2,1)S(1)} collective-permute-done((bf16[3,64,640]{2,1,0:T(8,128)(2,1)S(1)}, bf16[3,64,640]{2,1,0:T(8,128)(2,1)S(1)}, u32[]{:S(2)}, u32[]{:S(2)}) %collective-permute-start.3) | collective-permute-done | bytes 245792 | tf_op jit(solution)/shard_map/ppermute | solution.py:425
  19.9 0.0 collective-permute-done.2.near
  19.9 4.1 %border_block.1 = (f32[64,128]{1,0:T(8,128)S(1)}, bf16[1280,128]{1,0:T(8,128)(2,1)}, bf16[64,512]{1,0:T(8,128)(2,1)S(1)}, bf16[128,512]{1,0:T(8,128)(2,1)S(1)}) custom-call(s32[1]{0:T(128)} %bitcast.5.side, bf16[64,2048]{1,0:T(8,128)(2,1)S(1)} %bitcast.36, s32[27,1,2048]{2,1,0:T(1,128)S(1)} %bitcast.25, s32[27,1,2048]{2,1,0:T(1,128)S(1)} %bitcast.30, ...), custom_call_target="tpu_custom_call" | custom-call | tf_op jit(solution)/shard_map/border_block/pallas_call | solution.py:329
  24.0 9.5 %all-to-all-start = ((bf16[128,5,2,128]{3,2,1,0:T(2,128)(2,1)}), bf16[128,5,2,128]{3,2,1,0:T(2,128)(2,1)S(1)}, u32[]{:S(2)}, u32[]{:S(2)}) async-start(bf16[128,5,2,128]{3,2,1,0:T(2,128)(2,1)} %bitcast.9), calls=%async_computation | async-start | bytes 655360 | tf_op jit(solution)/shard_map/all_to_all | solution.py:447
  33.5 3.0 %border_scatter_block.1 = (f32[64,512]{1,0:T(8,128)S(1)}, f32[3,64,640]{2,1,0:T(8,128)S(1)}, bf16[3,64,640]{2,1,0:T(8,128)(2,1)S(1)}, bf16[3,64,640]{2,1,0:T(8,128)(2,1)S(1)}) custom-call(s32[1]{0:T(128)} %bitcast.5.side, s32[27,1,2048]{2,1,0:T(1,128)S(1)} %bitcast.26, s32[27,1,2048]{2,1,0:T(1,128)S(1)} %bitcast.31, s32[2,2048]{1,0:T(2,128)S(1)} %bitcast.47, ...), custom_call_target="tpu_custom_call" | custom-call | tf_op jit(solution)/shard_map/border_scatter_block/pallas_call | solution.py:363
  36.5 1.3 %collective-permute-start.4 = (bf16[3,64,640]{2,1,0:T(8,128)(2,1)S(1)}, bf16[3,64,640]{2,1,0:T(8,128)(2,1)S(1)}, u32[]{:S(2)}, u32[]{:S(2)}) collective-permute-start(bf16[3,64,640]{2,1,0:T(8,128)(2,1)S(1)} %get-tuple-element.57), channel_id=1, source_target_pairs={{0,1},{2,3},{4,5},{6,7},{1,0},{3,2},{5,4},{7,6},{8,9},{10,11},{12,... | collective-permute-start | bytes 737288 | tf_op jit(solution)/shard_map/ppermute | solution.py:425
  37.8 2.6 %collective-permute-start.5 = (bf16[3,64,640]{2,1,0:T(8,128)(2,1)S(1)}, bf16[3,64,640]{2,1,0:T(8,128)(2,1)S(1)}, u32[]{:S(2)}, u32[]{:S(2)}) collective-permute-start(bf16[3,64,640]{2,1,0:T(8,128)(2,1)S(1)} %get-tuple-element.58), channel_id=1, source_target_pairs={{1,2},{3,4},{5,6},{2,1},{4,3},{6,5},{9,10},{11,12},{13,14},{10,9},... | collective-permute-start | bytes 737288 | tf_op jit(solution)/shard_map/ppermute | solution.py:425
  40.5 4.8 %all-to-all-done = bf16[128,5,2,128]{3,2,1,0:T(2,128)(2,1)S(1)} async-done(((bf16[128,5,2,128]{3,2,1,0:T(2,128)(2,1)}), bf16[128,5,2,128]{3,2,1,0:T(2,128)(2,1)S(1)}, u32[]{:S(2)}, u32[]{:S(2)}) %all-to-all-start) | async-done | bytes 327712 | tf_op jit(solution)/shard_map/all_to_all | solution.py:447
  45.3 0.8 %sum_pieces.1 = bf16[1280,128]{1,0:T(8,128)(2,1)} custom-call(bf16[1280,128]{1,0:T(8,128)(2,1)S(1)} %bitcast.38), custom_call_target="tpu_custom_call" | custom-call | tf_op jit(solution)/shard_map/sum_pieces/pallas_call | solution.py:296
  46.1 4.4 %all-to-all-start.1 = ((bf16[128,5,2,128]{3,2,1,0:T(2,128)(2,1)}), bf16[128,5,2,128]{3,2,1,0:T(2,128)(2,1)S(1)}, u32[]{:S(2)}, u32[]{:S(2)}) async-start(bf16[128,5,2,128]{3,2,1,0:T(2,128)(2,1)} %bitcast.16), calls=%async_computation.1 | async-start | bytes 655360 | tf_op jit(solution)/shard_map/all_to_all | solution.py:456
  50.5 0.0 collective-permute-done.4
  50.5 0.1 convert_add_fusion
  50.7 0.7 %collective-permute-start.7 = (bf16[64,640]{1,0:T(8,128)(2,1)S(1)}, bf16[64,640]{1,0:T(8,128)(2,1)S(1)}, u32[]{:S(2)}, u32[]{:S(2)}) collective-permute-start(bf16[64,640]{1,0:T(8,128)(2,1)S(1)} %get-tuple-element.64), channel_id=1, source_target_pairs={{8,16},{24,32},{40,48},{56,64},{72,80},{88,96},{104,112},{16,8},{3... | collective-permute-start | bytes 245768 | tf_op jit(solution)/shard_map/ppermute | solution.py:425
  51.3 3.9 %collective-permute-start.6 = (bf16[64,640]{1,0:T(8,128)(2,1)S(1)}, bf16[64,640]{1,0:T(8,128)(2,1)S(1)}, u32[]{:S(2)}, u32[]{:S(2)}) collective-permute-start(bf16[64,640]{1,0:T(8,128)(2,1)S(1)} %get-tuple-element.65), channel_id=1, source_target_pairs={{0,8},{16,24},{32,40},{48,56},{64,72},{80,88},{96,104},{112,120},{... | collective-permute-start | bytes 245768 | tf_op jit(solution)/shard_map/ppermute | solution.py:425
  55.2 3.2 %local_scatter_blocks.1.gfeat_i = bf16[64,2048]{1,0:T(8,128)(2,1)} custom-call(s32[1,1]{1,0:T(1,128)S(6)} %copy.20.counts, s32[27,1,2048]{2,1,0:T(1,128)S(1)} %bitcast.27, s32[27,1,2048]{2,1,0:T(1,128)S(1)} %bitcast.32, bf16[64,2048]{1,0:T(8,128)(2,1)S(1)} %get-tuple-element.53.gpre, bf16[64,1728]{1,0:T(8,128)(2,1)S(1)} %get-tuple-element.51.w_t), custom_call_target="tpu_custom_call" | custom-call | tf_op jit(solution)/shard_map/local_scatter_blocks/pallas_call | solution.py:245
  58.4 0.6 collective-permute-done.6.left
  59.0 0.7 %add_incoming.1 = (bf16[64,512]{1,0:T(8,128)(2,1)}, bf16[64,2048]{1,0:T(8,128)(2,1)}) custom-call(bf16[64,512]{1,0:T(8,128)(2,1)} %get-tuple-element.42.coarse_i, bf16[64,2048]{1,0:T(8,128)(2,1)} %local_scatter_blocks.1.gfeat_i, f32[64,128]{1,0:T(8,128)S(1)} %get-tuple-element.54.coarse, ...), custom_call_target="tpu_custom_call", output_to_operand_aliasing={{0}: (0, {}), {1}: (1, {})} | custom-call | tf_op jit(solution)/shard_map/add_incoming/pallas_call | solution.py:385
  59.7 2.6 %all-to-all-done.1 = bf16[128,5,2,128]{3,2,1,0:T(2,128)(2,1)S(1)} async-done(((bf16[128,5,2,128]{3,2,1,0:T(2,128)(2,1)}), bf16[128,5,2,128]{3,2,1,0:T(2,128)(2,1)S(1)}, u32[]{:S(2)}, u32[]{:S(2)}) %all-to-all-start.1) | async-done | bytes 327712 | tf_op jit(solution)/shard_map/all_to_all | solution.py:456
  62.3 1.2 %unpack_weights.1 = (f32[27,64,64]{2,1,0:T(8,128)}, f32[8,64,64]{2,1,0:T(8,128)}) custom-call(bf16[1280,128]{1,0:T(8,128)(2,1)S(1)} %bitcast.37), custom_call_target="tpu_custom_call" | custom-call | tf_op jit(solution)/shard_map/unpack_weights/pallas_call | solution.py:411
  (12 shorter events, 0.1 us)
Async XLA Ops:
  1.5 10.7 %collective-permute-start.1 = (bf16[64,640]{1,0:T(8,128)(2,1)S(1)}, bf16[64,640]{1,0:T(8,128)(2,1)S(1)}, u32[]{:S(2)}, u32[]{:S(2)}) collective-permute-start(bf16[64,640]{1,0:T(8,128)(2,1)S(1)} %pack_border.1), channel_id=1, source_target_pairs={{8,16},{24,32},{40,48},{56,64},{72,80},{88,96},{104,112},{16,8},{3... | collective-permute-start | bytes 245768 | tf_op jit(solution)/shard_map/ppermute | solution.py:425
  2.2 10.0 %collective-permute-start = (bf16[64,640]{1,0:T(8,128)(2,1)S(1)}, bf16[64,640]{1,0:T(8,128)(2,1)S(1)}, u32[]{:S(2)}, u32[]{:S(2)}) collective-permute-start(bf16[64,640]{1,0:T(8,128)(2,1)S(1)} %pack_border.1), channel_id=1, source_target_pairs={{0,8},{16,24},{32,40},{48,56},{64,72},{80,88},{96,104},{112,120},{... | collective-permute-start | bytes 245768 | tf_op jit(solution)/shard_map/ppermute | solution.py:425
  6.9 0.7 %copy-start.4 = (s32[1,1,2,2048]{3,2,1,0:T(2,128)S(1)}, s32[1,1,2,2048]{3,2,1,0:T(2,128)}, u32[]{:S(2)}) copy-start(s32[1,1,2,2048]{3,2,1,0:T(2,128)} %param.12) | copy-start | bytes 49156
  12.2 2.3 %copy-start.2 = (bf16[1,1,64,2048]{3,2,1,0:T(8,128)(2,1)S(1)}, bf16[1,1,64,2048]{3,2,1,0:T(8,128)(2,1)}, u32[]{:S(2)}) copy-start(bf16[1,1,64,2048]{3,2,1,0:T(8,128)(2,1)} %param.8) | copy-start | bytes 786436
  12.2 2.3 %copy-start = (s32[1,1,27,2048]{3,1,2,0:T(1,128)S(1)}, s32[1,1,27,2048]{3,1,2,0:T(1,128)}, u32[]{:S(2)}) copy-start(s32[1,1,27,2048]{3,1,2,0:T(1,128)} %param.10) | copy-start | bytes 663556
  12.2 2.3 %copy-start.1 = (s32[1,1,27,2048]{3,1,2,0:T(1,128)S(1)}, s32[1,1,27,2048]{3,1,2,0:T(1,128)}, u32[]{:S(2)}) copy-start(s32[1,1,27,2048]{3,1,2,0:T(1,128)} %param.11) | copy-start | bytes 663556
  12.2 2.3 %copy-start.3 = (bf16[1,1,64,512]{3,2,1,0:T(8,128)(2,1)S(1)}, bf16[1,1,64,512]{3,2,1,0:T(8,128)(2,1)}, u32[]{:S(2)}) copy-start(bf16[1,1,64,512]{3,2,1,0:T(8,128)(2,1)} %param.15) | copy-start | bytes 196612
  12.3 7.6 %collective-permute-start.3 = (bf16[3,64,640]{2,1,0:T(8,128)(2,1)S(1)}, bf16[3,64,640]{2,1,0:T(8,128)(2,1)S(1)}, u32[]{:S(2)}, u32[]{:S(2)}) collective-permute-start(bf16[3,64,640]{2,1,0:T(8,128)(2,1)S(1)} %pad_maximum_fusion.column), channel_id=1, source_target_pairs={{1,2},{3,4},{5,6},{2,1},{4,3},{6,5},{9,10},{11,12},{13,14},{10,9},... | collective-permute-start | bytes 737288 | tf_op jit(solution)/shard_map/ppermute | solution.py:425
  14.4 5.6 %collective-permute-start.2 = (bf16[3,64,640]{2,1,0:T(8,128)(2,1)S(1)}, bf16[3,64,640]{2,1,0:T(8,128)(2,1)S(1)}, u32[]{:S(2)}, u32[]{:S(2)}) collective-permute-start(bf16[3,64,640]{2,1,0:T(8,128)(2,1)S(1)} %pad_maximum_fusion.column), channel_id=1, source_target_pairs={{0,1},{2,3},{4,5},{6,7},{1,0},{3,2},{5,4},{7,6},{8,9},{10,11},{12,... | collective-permute-start | bytes 737288 | tf_op jit(solution)/shard_map/ppermute | solution.py:425
  24.0 21.3 %all-to-all-start = ((bf16[128,5,2,128]{3,2,1,0:T(2,128)(2,1)}), bf16[128,5,2,128]{3,2,1,0:T(2,128)(2,1)S(1)}, u32[]{:S(2)}, u32[]{:S(2)}) async-start(bf16[128,5,2,128]{3,2,1,0:T(2,128)(2,1)} %bitcast.9), calls=%async_computation | async-start | bytes 655360 | tf_op jit(solution)/shard_map/all_to_all | solution.py:447
  36.5 14.0 %collective-permute-start.4 = (bf16[3,64,640]{2,1,0:T(8,128)(2,1)S(1)}, bf16[3,64,640]{2,1,0:T(8,128)(2,1)S(1)}, u32[]{:S(2)}, u32[]{:S(2)}) collective-permute-start(bf16[3,64,640]{2,1,0:T(8,128)(2,1)S(1)} %get-tuple-element.57), channel_id=1, source_target_pairs={{0,1},{2,3},{4,5},{6,7},{1,0},{3,2},{5,4},{7,6},{8,9},{10,11},{12,... | collective-permute-start | bytes 737288 | tf_op jit(solution)/shard_map/ppermute | solution.py:425
  37.8 12.7 %collective-permute-start.5 = (bf16[3,64,640]{2,1,0:T(8,128)(2,1)S(1)}, bf16[3,64,640]{2,1,0:T(8,128)(2,1)S(1)}, u32[]{:S(2)}, u32[]{:S(2)}) collective-permute-start(bf16[3,64,640]{2,1,0:T(8,128)(2,1)S(1)} %get-tuple-element.58), channel_id=1, source_target_pairs={{1,2},{3,4},{5,6},{2,1},{4,3},{6,5},{9,10},{11,12},{13,14},{10,9},... | collective-permute-start | bytes 737288 | tf_op jit(solution)/shard_map/ppermute | solution.py:425
  46.1 16.2 %all-to-all-start.1 = ((bf16[128,5,2,128]{3,2,1,0:T(2,128)(2,1)}), bf16[128,5,2,128]{3,2,1,0:T(2,128)(2,1)S(1)}, u32[]{:S(2)}, u32[]{:S(2)}) async-start(bf16[128,5,2,128]{3,2,1,0:T(2,128)(2,1)} %bitcast.16), calls=%async_computation.1 | async-start | bytes 655360 | tf_op jit(solution)/shard_map/all_to_all | solution.py:456
  50.7 7.8 %collective-permute-start.7 = (bf16[64,640]{1,0:T(8,128)(2,1)S(1)}, bf16[64,640]{1,0:T(8,128)(2,1)S(1)}, u32[]{:S(2)}, u32[]{:S(2)}) collective-permute-start(bf16[64,640]{1,0:T(8,128)(2,1)S(1)} %get-tuple-element.64), channel_id=1, source_target_pairs={{8,16},{24,32},{40,48},{56,64},{72,80},{88,96},{104,112},{16,8},{3... | collective-permute-start | bytes 245768 | tf_op jit(solution)/shard_map/ppermute | solution.py:425
  51.3 7.7 %collective-permute-start.6 = (bf16[64,640]{1,0:T(8,128)(2,1)S(1)}, bf16[64,640]{1,0:T(8,128)(2,1)S(1)}, u32[]{:S(2)}, u32[]{:S(2)}) collective-permute-start(bf16[64,640]{1,0:T(8,128)(2,1)S(1)} %get-tuple-element.65), channel_id=1, source_target_pairs={{0,8},{16,24},{32,40},{48,56},{64,72},{80,88},{96,104},{112,120},{... | collective-permute-start | bytes 245768 | tf_op jit(solution)/shard_map/ppermute | solution.py:425

commit v7 on v6

--- a/solution.py
+++ b/solution.py
@@ -118,9 +118,12 @@
     return mm(w_t[...], spread[:, 0:VB])
 
 
-def prepare_weights(w_sub, w_down, w_cat, w_t, wd_cat, wd_t):
+def prepare_sub(w_sub, w_cat, w_t):
     w_cat[...] = jnp.concatenate([w_sub[k] for k in range(K)], axis=1)
     w_t[...] = w_sub[...].reshape(KC, C).T
+
+
+def prepare_down(w_down, wd_cat, wd_t):
     wd_cat[...] = jnp.concatenate([w_down[k] for k in range(8)], axis=1)
     wd_t[...] = w_down[...].reshape(8 * C, C).T
 
@@ -142,25 +145,21 @@
         coarse_o[...] = jnp.zeros_like(coarse_o)
 
 
-def first_kernel(counts, feat, rows, frm, dmap, grad, w_sub, w_down,
-                 coarse_o, gpre_o, gsub_o, gdown_o, w_cat, w_t, wd_cat, wd_t, source):
-    prepare_weights(w_sub, w_down, w_cat, w_t, wd_cat, wd_t)
-    gsub_o[...] = jnp.zeros_like(gsub_o)
-    gdown_o[...] = jnp.zeros_like(gdown_o)
-    one_local(1, counts, feat, rows, frm, dmap, grad, w_cat, wd_cat, wd_t,
-              (coarse_o, gpre_o, gsub_o, gdown_o), source)
-
-
-def rest_kernel(counts, feat, rows, frm, dmap, grad, w_cat, wd_cat, wd_t, gsub, gdown, coarse_a, gpre_a,
-                coarse_o, gpre_o, gsub_o, gdown_o, source):
+def local_kernel(counts, feat, rows, frm, dmap, grad, w_sub, w_down_h,
+                 coarse_o, gpre_o, gsub_o, gdown_o, w_cat, w_t, wd_cat, wd_t, source, w_down, sem):
     i = pl.program_id(0)
 
     @pl.when(i == 0)
     def _():
-        gsub_o[...] = gsub[...]
-        gdown_o[...] = gdown[...]
-
-    one_local(i + 2, counts, feat, rows, frm, dmap, grad, w_cat, wd_cat, wd_t,
+        copy = pltpu.make_async_copy(w_down_h, w_down, sem)
+        copy.start()
+        prepare_sub(w_sub, w_cat, w_t)
+        copy.wait()
+        prepare_down(w_down, wd_cat, wd_t)
+        gsub_o[...] = jnp.zeros_like(gsub_o)
+        gdown_o[...] = jnp.zeros_like(gdown_o)
+
+    one_local(i + 1, counts, feat, rows, frm, dmap, grad, w_cat, wd_cat, wd_t,
               (coarse_o, gpre_o, gsub_o, gdown_o), source)
 
 
@@ -209,36 +208,21 @@
     return jax.ShapeDtypeStruct(shape, dtype)
 
 
-def first_call(counts, feat, rows, frm, dmap, grad, w_sub, w_down):
+def local_call(counts, feat, rows, frm, dmap, grad, w_sub, w_down):
     weights = [(C, KC), (C, KC), (C, 8 * C), (C, 8 * C)]
     return pl.pallas_call(
-        first_kernel,
-        grid=(1,),
-        in_specs=[pl.BlockSpec(memory_space=pltpu.SMEM)] + table_specs(1) + [piped((K, C, C)), piped((8, C, C))],
+        local_kernel,
+        grid=(3,),
+        in_specs=[pl.BlockSpec(memory_space=pltpu.SMEM)] + table_specs(1)
+        + [full((K, C, C)), pl.BlockSpec(memory_space=pltpu.HBM)],
         out_specs=[columns((C, CQ), 1), columns((C, VB), 1), full((C, KC)), full((8 * C, C))]
         + [full(w) for w in weights],
         out_shape=[sd((C, CROWS), BF), sd((C, ROWS), BF), sd((C, KC), F32), sd((8 * C, C), F32)]
         + [sd(w, BF) for w in weights],
-        scratch_shapes=[SOURCE],
+        scratch_shapes=[SOURCE, pltpu.VMEM((8, C, C), BF), pltpu.SemaphoreType.DMA(())],
         compiler_params=LIMIT,
-        name="first_local_block",
-    )(counts, feat, rows, frm, dmap, grad, w_sub, w_down)
-
-
-def rest_call(counts, feat, rows, frm, dmap, grad, w_cat, wd_cat, wd_t, gsub, gdown, coarse_all, gpre_all):
-    return pl.pallas_call(
-        rest_kernel,
-        grid=(2,),
-        in_specs=[pl.BlockSpec(memory_space=pltpu.SMEM)] + table_specs(2)
-        + [full((C, KC)), full((C, 8 * C)), full((C, 8 * C)), full((C, KC)), full((8 * C, C)),
-           pl.BlockSpec(memory_space=pl.ANY), pl.BlockSpec(memory_space=pl.ANY)],
-        out_specs=[columns((C, CQ), 2), columns((C, VB), 2), full((C, KC)), full((8 * C, C))],
-        out_shape=[sd((C, CROWS), BF), sd((C, ROWS), BF), sd((C, KC), F32), sd((8 * C, C), F32)],
-        scratch_shapes=[SOURCE],
-        input_output_aliases={11: 0, 12: 1},
-        compiler_params=LIMIT,
-        name="other_local_blocks",
-    )(counts, feat, rows, frm, dmap, grad, w_cat, wd_cat, wd_t, gsub, gdown, coarse_all, gpre_all)
+        name="local_blocks",
+    )(counts, feat, rows, frm, dmap, grad, w_sub, in_hbm(w_down))
 
 
 def local_scatter_call(counts, rows, frm, gpre_all, w_t):
@@ -435,13 +419,10 @@
     even_x, even_y = lax.axis_index("gx") % 2 == 0, lax.axis_index("gy") % 2 == 0
     side = even_y.astype(jnp.int32).reshape(1)
     near, far = swapped(border, "gx", True), swapped(border, "gx", False)
-    coarse_all, gpre_all, gsub, gdown, w_cat, w_t, wd_cat, wd_t = first_call(
-        counts, *[in_hbm(a) for a in (feat, rows, frm)], dmap, *[in_hbm(a) for a in (grad, w_sub, w_down)])
-    near, far, gsub = lax.optimization_barrier((near, far, gsub))
     column = jnp.stack([jnp.where(even_x, far, near), border, jnp.where(even_x, near, far)])
     near, far = swapped(column, "gy", True), swapped(column, "gy", False)
-    coarse_all, gpre_all, gsub, gdown = rest_call(
-        counts, feat, rows, frm, dmap, grad, w_cat, wd_cat, wd_t, gsub, gdown, coarse_all, gpre_all)
+    coarse_all, gpre_all, gsub, gdown, w_cat, w_t, wd_cat, wd_t = local_call(
+        counts, feat, rows, frm, dmap, grad, w_sub, w_down)
     coarse, packed, gpre, split = border_call(
         count, side, feat, rows, frm, dmap, grad, near, column, far, w_cat, wd_cat, wd_t, gsub, gdown)
     pieces = lax.all_to_all(packed.reshape(count, PAIRS, 2, 2 * C), ("gx", "gy"), 0, 0, tiled=True)

time: 64 us -> 67.9 us (1.061)
  starting transfers between devices: 30 us -> 35.4 us
  waiting for transfers between devices: 12.6 us -> 8.04 us
  Pallas kernels: 19.1 us -> 21.9 us
    all_to_all x1, starting transfers between devices: 9.49 us -> 14.6 us  [shards(): lax.all_to_all(packed.reshape(count, PAIRS, 2, 2 * C), ('gx', 'gy'), 0, 0...]
    ppermute x8, waiting for transfers between devices: 5.18 us -> 1.17 us  [swapped(): return lax.ppermute(block, axis, pairs + [(b, a) for a, b in pairs])]
    pallas_call x2 -> x1, Pallas kernels: 5.38 us -> 6.83 us  [local_call(): pl.pallas_call(local_kernel, grid=(3,), in_specs=[pl.BlockSpec(memory_spa...]
    pallas_call x1, Pallas kernels: 3.19 us -> 4.49 us  [local_scatter_call(): pl.pallas_call(local_scatter_kernel, grid=(3,), in_specs=[pl.BlockSpec(me...]
    all_to_all x1, waiting for transfers between devices: 2.57 us -> 1.87 us  [shards(): lax.all_to_all(spread.reshape(shape), ('gx', 'gy'), 0, 0, tiled=True)]
  transfers between devices with their start and end apart: 10 -> 10, of which waited for: 4 -> 3; matrix products, arithmetic and copies ran while one was open for 0% -> 0% of each run, Pallas kernels for 21% -> 23%
where the time goes in v7:
time: 67.9 us; the launch traced here: 67.1 us
  starting transfers between devices  35.4 us (52%)
  Pallas kernels  21.9 us (32%)
  waiting for transfers between devices  8.04 us (12%)
  between operations  1.54 us (2%)
    ppermute x8, starting transfers between devices, swapped(): return lax.ppermute(block, axis, pairs + [(b, a) for a, b in pairs])  16.4 us
    all_to_all x1, starting transfers between devices, shards(): lax.all_to_all(packed.reshape(count, PAIRS, 2, 2 * C), ('gx', 'gy'), 0, 0...  14.6 us
    pallas_call x1, Pallas kernels, local_call(): pl.pallas_call(local_kernel, grid=(3,), in_specs=[pl.BlockSpec(memory_spa...  6.83 us
    all_to_all x1, waiting for transfers between devices, shards(): lax.all_to_all(packed.reshape(count, PAIRS, 2, 2 * C), ('gx', 'gy'), 0, 0...  5 us
    pallas_call x1, Pallas kernels, local_scatter_call(): pl.pallas_call(local_scatter_kernel, grid=(3,), in_specs=[pl.BlockSpec(me...  4.49 us
    all_to_all x1, starting transfers between devices, shards(): lax.all_to_all(spread.reshape(shape), ('gx', 'gy'), 0, 0, tiled=True)  4.44 us
    pallas_call x1, Pallas kernels, border_call(): pl.pallas_call(border_kernel, grid=(1,), in_specs=[pl.BlockSpec(memory_sp...  4.1 us
    pallas_call x1, Pallas kernels, border_scatter_call(): pl.pallas_call(border_scatter_kernel, grid=(1,), in_specs=[pl.BlockSpec(m...  2.98 us
  transfers between devices with their start and end apart: 10, of which 3 were waited for; matrix products, arithmetic and copies ran while one was open for 0% of the time, Pallas kernels for 23%

profile of v7, /device:TPU:1, one launch (start us, length us, event | category | flops | bytes accessed | tf_op | source)
XLA Modules:
  0.0 67.1 jit_solution(2710606381667083366)
XLA Ops:
  0.6 0.9 %pack_border.1 = bf16[64,640]{1,0:T(8,128)(2,1)S(1)} custom-call(bf16[64,2048]{1,0:T(8,128)(2,1)} %bitcast.31, bf16[64,512]{1,0:T(8,128)(2,1)} %bitcast.36), custom_call_target="tpu_custom_call" | custom-call | tf_op jit(solution)/shard_map/pack_border/pallas_call | solution.py:256
  1.6 2.2 %collective-permute-start.1 = (bf16[64,640]{1,0:T(8,128)(2,1)S(1)}, bf16[64,640]{1,0:T(8,128)(2,1)S(1)}, u32[]{:S(2)}, u32[]{:S(2)}) collective-permute-start(bf16[64,640]{1,0:T(8,128)(2,1)S(1)} %pack_border.1), channel_id=1, source_target_pairs={{0,8},{16,24},{32,40},{48,56},{64,72},{80,88},{96,104},{112,120},{... | collective-permute-start | bytes 245768 | tf_op jit(solution)/shard_map/ppermute | solution.py:409
  3.8 0.7 collective-permute-start
  4.4 1.2 %collective-permute-done.1 = bf16[64,640]{1,0:T(8,128)(2,1)S(1)} collective-permute-done((bf16[64,640]{1,0:T(8,128)(2,1)S(1)}, bf16[64,640]{1,0:T(8,128)(2,1)S(1)}, u32[]{:S(2)}, u32[]{:S(2)}) %collective-permute-start.1) | collective-permute-done | bytes 81952 | tf_op jit(solution)/shard_map/ppermute | solution.py:409
  5.6 0.0 collective-permute-done
  5.6 0.0 copy-start
  5.6 0.0 copy-start.1
  5.7 0.0 copy-start.3
  5.7 5.1 %collective-permute-start.3 = (bf16[3,64,640]{2,1,0:T(8,128)(2,1)S(1)}, bf16[3,64,640]{2,1,0:T(8,128)(2,1)S(1)}, u32[]{:S(2)}, u32[]{:S(2)}) collective-permute-start(bf16[3,64,640]{2,1,0:T(8,128)(2,1)S(1)} %pad_maximum_fusion.column), channel_id=1, source_target_pairs={{1,2},{3,4},{5,6},{2,1},{4,3},{6,5},{9,10},{11,12},{13,14},{10,9},... | collective-permute-start | bytes 737288 | tf_op jit(solution)/shard_map/ppermute | solution.py:409
  10.8 0.1 collective-permute-start.2
  10.9 0.0 copy-start.5
  11.7 6.8 %local_blocks.1 = (bf16[64,512]{1,0:T(8,128)(2,1)}, bf16[64,2048]{1,0:T(8,128)(2,1)S(1)}, f32[64,1728]{1,0:T(8,128)S(1)}, f32[512,64]{1,0:T(8,128)S(1)}, bf16[64...) custom-call(s32[1,1]{1,0:T(1,128)S(6)} %copy.16.counts, ...), custom_call_target="tpu_custom_call" | custom-call | tf_op jit(solution)/shard_map/local_blocks/pallas_call | solution.py:213
  18.5 0.0 collective-permute-done.2.near
  18.5 4.1 %border_block.1 = (f32[64,128]{1,0:T(8,128)S(1)}, bf16[1280,128]{1,0:T(8,128)(2,1)}, bf16[64,512]{1,0:T(8,128)(2,1)S(1)}, bf16[128,512]{1,0:T(8,128)(2,1)S(1)}) custom-call(s32[1]{0:T(128)} %bitcast.5.side, bf16[64,2048]{1,0:T(8,128)(2,1)S(1)} %bitcast.33, s32[27,1,2048]{2,1,0:T(1,128)S(1)} %bitcast.24, s32[27,1,2048]{2,1,0:T(1,128)S(1)} %bitcast.28, ...), custom_call_target="tpu_custom_call" | custom-call | tf_op jit(solution)/shard_map/border_block/pallas_call | solution.py:313
  22.6 14.6 %all-to-all-start = ((bf16[128,5,2,128]{3,2,1,0:T(2,128)(2,1)}), bf16[128,5,2,128]{3,2,1,0:T(2,128)(2,1)S(1)}, u32[]{:S(2)}, u32[]{:S(2)}) async-start(bf16[128,5,2,128]{3,2,1,0:T(2,128)(2,1)} %bitcast.9), calls=%async_computation | async-start | bytes 655360 | tf_op jit(solution)/shard_map/all_to_all | solution.py:428
  37.2 3.0 %border_scatter_block.1 = (f32[64,512]{1,0:T(8,128)S(1)}, f32[3,64,640]{2,1,0:T(8,128)S(1)}, bf16[3,64,640]{2,1,0:T(8,128)(2,1)S(1)}, bf16[3,64,640]{2,1,0:T(8,128)(2,1)S(1)}) custom-call(s32[1]{0:T(128)} %bitcast.5.side, s32[27,1,2048]{2,1,0:T(1,128)S(1)} %bitcast.25, s32[27,1,2048]{2,1,0:T(1,128)S(1)} %bitcast.29, s32[2,2048]{1,0:T(2,128)S(1)} %bitcast.42, ...), custom_call_target="tpu_custom_call" | custom-call | tf_op jit(solution)/shard_map/border_scatter_block/pallas_call | solution.py:347
  40.2 1.1 %collective-permute-start.4 = (bf16[3,64,640]{2,1,0:T(8,128)(2,1)S(1)}, bf16[3,64,640]{2,1,0:T(8,128)(2,1)S(1)}, u32[]{:S(2)}, u32[]{:S(2)}) collective-permute-start(bf16[3,64,640]{2,1,0:T(8,128)(2,1)S(1)} %get-tuple-element.43), channel_id=1, source_target_pairs={{0,1},{2,3},{4,5},{6,7},{1,0},{3,2},{5,4},{7,6},{8,9},{10,11},{12,... | collective-permute-start | bytes 737288 | tf_op jit(solution)/shard_map/ppermute | solution.py:409
  41.4 2.6 %collective-permute-start.5 = (bf16[3,64,640]{2,1,0:T(8,128)(2,1)S(1)}, bf16[3,64,640]{2,1,0:T(8,128)(2,1)S(1)}, u32[]{:S(2)}, u32[]{:S(2)}) collective-permute-start(bf16[3,64,640]{2,1,0:T(8,128)(2,1)S(1)} %get-tuple-element.44), channel_id=1, source_target_pairs={{1,2},{3,4},{5,6},{2,1},{4,3},{6,5},{9,10},{11,12},{13,14},{10,9},... | collective-permute-start | bytes 737288 | tf_op jit(solution)/shard_map/ppermute | solution.py:409
  44.0 5.0 %all-to-all-done = bf16[128,5,2,128]{3,2,1,0:T(2,128)(2,1)S(1)} async-done(((bf16[128,5,2,128]{3,2,1,0:T(2,128)(2,1)}), bf16[128,5,2,128]{3,2,1,0:T(2,128)(2,1)S(1)}, u32[]{:S(2)}, u32[]{:S(2)}) %all-to-all-start) | async-done | bytes 327712 | tf_op jit(solution)/shard_map/all_to_all | solution.py:428
  49.0 0.8 %sum_pieces.1 = bf16[1280,128]{1,0:T(8,128)(2,1)} custom-call(bf16[1280,128]{1,0:T(8,128)(2,1)S(1)} %bitcast.35), custom_call_target="tpu_custom_call" | custom-call | tf_op jit(solution)/shard_map/sum_pieces/pallas_call | solution.py:280
  49.8 4.4 %all-to-all-start.1 = ((bf16[128,5,2,128]{3,2,1,0:T(2,128)(2,1)}), bf16[128,5,2,128]{3,2,1,0:T(2,128)(2,1)S(1)}, u32[]{:S(2)}, u32[]{:S(2)}) async-start(bf16[128,5,2,128]{3,2,1,0:T(2,128)(2,1)} %bitcast.16), calls=%async_computation.1 | async-start | bytes 655360 | tf_op jit(solution)/shard_map/all_to_all | solution.py:437
  54.2 0.0 collective-permute-done.4
  54.2 0.0 collective-permute-done.5
  54.2 0.1 convert_add_fusion
  54.3 0.7 collective-permute-start.7
  55.0 3.9 %collective-permute-start.6 = (bf16[64,640]{1,0:T(8,128)(2,1)S(1)}, bf16[64,640]{1,0:T(8,128)(2,1)S(1)}, u32[]{:S(2)}, u32[]{:S(2)}) collective-permute-start(bf16[64,640]{1,0:T(8,128)(2,1)S(1)} %get-tuple-element.51), channel_id=1, source_target_pairs={{0,8},{16,24},{32,40},{48,56},{64,72},{80,88},{96,104},{112,120},{... | collective-permute-start | bytes 245768 | tf_op jit(solution)/shard_map/ppermute | solution.py:409
  58.9 4.5 %local_scatter_blocks.1.gfeat_i = bf16[64,2048]{1,0:T(8,128)(2,1)} custom-call(s32[1,1]{1,0:T(1,128)S(6)} %copy.16.counts, s32[27,1,2048]{2,1,0:T(1,128)S(1)} %bitcast.26, s32[27,1,2048]{2,1,0:T(1,128)S(1)} %bitcast.30, bf16[64,2048]{1,0:T(8,128)(2,1)S(1)} %get-tuple-element.39.gpre, bf16[64,1728]{1,0:T(8,128)(2,1)S(1)} %get-tuple-element.37.w_t), custom_call_target="tpu_custom_call" | custom-call | tf_op jit(solution)/shard_map/local_scatter_blocks/pallas_call | solution.py:229
  63.4 0.0 collective-permute-done.7.right
  63.4 0.0 collective-permute-done.6.left
  63.4 0.7 add_incoming.1
  64.1 1.9 %all-to-all-done.1 = bf16[128,5,2,128]{3,2,1,0:T(2,128)(2,1)S(1)} async-done(((bf16[128,5,2,128]{3,2,1,0:T(2,128)(2,1)}), bf16[128,5,2,128]{3,2,1,0:T(2,128)(2,1)S(1)}, u32[]{:S(2)}, u32[]{:S(2)}) %all-to-all-start.1) | async-done | bytes 327712 | tf_op jit(solution)/shard_map/all_to_all | solution.py:437
  66.0 1.2 %unpack_weights.1 = (f32[27,64,64]{2,1,0:T(8,128)}, f32[8,64,64]{2,1,0:T(8,128)}) custom-call(bf16[1280,128]{1,0:T(8,128)(2,1)S(1)} %bitcast.34), custom_call_target="tpu_custom_call" | custom-call | tf_op jit(solution)/shard_map/unpack_weights/pallas_call | solution.py:395
  (13 shorter events, 0.1 us)
Async XLA Ops:
  0.6 11.0 %copy-start.4 = (bf16[27,64,64]{2,1,0:T(8,128)(2,1)S(1)}, bf16[27,64,64]{2,1,0:T(8,128)(2,1)}, u32[]{:S(2)}) copy-start(bf16[27,64,64]{2,1,0:T(8,128)(2,1)} %w_sub.1) | copy-start | bytes 663556
  1.6 4.0 %collective-permute-start.1 = (bf16[64,640]{1,0:T(8,128)(2,1)S(1)}, bf16[64,640]{1,0:T(8,128)(2,1)S(1)}, u32[]{:S(2)}, u32[]{:S(2)}) collective-permute-start(bf16[64,640]{1,0:T(8,128)(2,1)S(1)} %pack_border.1), channel_id=1, source_target_pairs={{0,8},{16,24},{32,40},{48,56},{64,72},{80,88},{96,104},{112,120},{... | collective-permute-start | bytes 245768 | tf_op jit(solution)/shard_map/ppermute | solution.py:409
  3.8 1.8 %collective-permute-start = (bf16[64,640]{1,0:T(8,128)(2,1)S(1)}, bf16[64,640]{1,0:T(8,128)(2,1)S(1)}, u32[]{:S(2)}, u32[]{:S(2)}) collective-permute-start(bf16[64,640]{1,0:T(8,128)(2,1)S(1)} %pack_border.1), channel_id=1, source_target_pairs={{8,16},{24,32},{40,48},{56,64},{72,80},{88,96},{104,112},{16,8},{3... | collective-permute-start | bytes 245768 | tf_op jit(solution)/shard_map/ppermute | solution.py:409
  5.6 6.0 %copy-start.2 = (bf16[1,1,64,2048]{3,2,1,0:T(8,128)(2,1)S(1)}, bf16[1,1,64,2048]{3,2,1,0:T(8,128)(2,1)}, u32[]{:S(2)}) copy-start(bf16[1,1,64,2048]{3,2,1,0:T(8,128)(2,1)} %param.8) | copy-start | bytes 786436
  5.6 6.0 %copy-start = (s32[1,1,27,2048]{3,1,2,0:T(1,128)S(1)}, s32[1,1,27,2048]{3,1,2,0:T(1,128)}, u32[]{:S(2)}) copy-start(s32[1,1,27,2048]{3,1,2,0:T(1,128)} %param.10) | copy-start | bytes 663556
  5.6 6.0 %copy-start.1 = (s32[1,1,27,2048]{3,1,2,0:T(1,128)S(1)}, s32[1,1,27,2048]{3,1,2,0:T(1,128)}, u32[]{:S(2)}) copy-start(s32[1,1,27,2048]{3,1,2,0:T(1,128)} %param.11) | copy-start | bytes 663556
  5.7 6.0 %copy-start.3 = (bf16[1,1,64,512]{3,2,1,0:T(8,128)(2,1)S(1)}, bf16[1,1,64,512]{3,2,1,0:T(8,128)(2,1)}, u32[]{:S(2)}) copy-start(bf16[1,1,64,512]{3,2,1,0:T(8,128)(2,1)} %param.15) | copy-start | bytes 196612
  5.7 12.8 %collective-permute-start.3 = (bf16[3,64,640]{2,1,0:T(8,128)(2,1)S(1)}, bf16[3,64,640]{2,1,0:T(8,128)(2,1)S(1)}, u32[]{:S(2)}, u32[]{:S(2)}) collective-permute-start(bf16[3,64,640]{2,1,0:T(8,128)(2,1)S(1)} %pad_maximum_fusion.column), channel_id=1, source_target_pairs={{1,2},{3,4},{5,6},{2,1},{4,3},{6,5},{9,10},{11,12},{13,14},{10,9},... | collective-permute-start | bytes 737288 | tf_op jit(solution)/shard_map/ppermute | solution.py:409
  10.8 7.7 %collective-permute-start.2 = (bf16[3,64,640]{2,1,0:T(8,128)(2,1)S(1)}, bf16[3,64,640]{2,1,0:T(8,128)(2,1)S(1)}, u32[]{:S(2)}, u32[]{:S(2)}) collective-permute-start(bf16[3,64,640]{2,1,0:T(8,128)(2,1)S(1)} %pad_maximum_fusion.column), channel_id=1, source_target_pairs={{0,1},{2,3},{4,5},{6,7},{1,0},{3,2},{5,4},{7,6},{8,9},{10,11},{12,... | collective-permute-start | bytes 737288 | tf_op jit(solution)/shard_map/ppermute | solution.py:409
  10.9 0.7 %copy-start.5 = (s32[1,1,2,2048]{3,2,1,0:T(2,128)S(1)}, s32[1,1,2,2048]{3,2,1,0:T(2,128)}, u32[]{:S(2)}) copy-start(s32[1,1,2,2048]{3,2,1,0:T(2,128)} %param.12) | copy-start | bytes 49156
  22.6 26.3 %all-to-all-start = ((bf16[128,5,2,128]{3,2,1,0:T(2,128)(2,1)}), bf16[128,5,2,128]{3,2,1,0:T(2,128)(2,1)S(1)}, u32[]{:S(2)}, u32[]{:S(2)}) async-start(bf16[128,5,2,128]{3,2,1,0:T(2,128)(2,1)} %bitcast.9), calls=%async_computation | async-start | bytes 655360 | tf_op jit(solution)/shard_map/all_to_all | solution.py:428
  40.2 14.0 %collective-permute-start.4 = (bf16[3,64,640]{2,1,0:T(8,128)(2,1)S(1)}, bf16[3,64,640]{2,1,0:T(8,128)(2,1)S(1)}, u32[]{:S(2)}, u32[]{:S(2)}) collective-permute-start(bf16[3,64,640]{2,1,0:T(8,128)(2,1)S(1)} %get-tuple-element.43), channel_id=1, source_target_pairs={{0,1},{2,3},{4,5},{6,7},{1,0},{3,2},{5,4},{7,6},{8,9},{10,11},{12,... | collective-permute-start | bytes 737288 | tf_op jit(solution)/shard_map/ppermute | solution.py:409
  41.4 12.9 %collective-permute-start.5 = (bf16[3,64,640]{2,1,0:T(8,128)(2,1)S(1)}, bf16[3,64,640]{2,1,0:T(8,128)(2,1)S(1)}, u32[]{:S(2)}, u32[]{:S(2)}) collective-permute-start(bf16[3,64,640]{2,1,0:T(8,128)(2,1)S(1)} %get-tuple-element.44), channel_id=1, source_target_pairs={{1,2},{3,4},{5,6},{2,1},{4,3},{6,5},{9,10},{11,12},{13,14},{10,9},... | collective-permute-start | bytes 737288 | tf_op jit(solution)/shard_map/ppermute | solution.py:409
  49.8 16.2 %all-to-all-start.1 = ((bf16[128,5,2,128]{3,2,1,0:T(2,128)(2,1)}), bf16[128,5,2,128]{3,2,1,0:T(2,128)(2,1)S(1)}, u32[]{:S(2)}, u32[]{:S(2)}) async-start(bf16[128,5,2,128]{3,2,1,0:T(2,128)(2,1)} %bitcast.16), calls=%async_computation.1 | async-start | bytes 655360 | tf_op jit(solution)/shard_map/all_to_all | solution.py:437
  54.3 9.1 %collective-permute-start.7 = (bf16[64,640]{1,0:T(8,128)(2,1)S(1)}, bf16[64,640]{1,0:T(8,128)(2,1)S(1)}, u32[]{:S(2)}, u32[]{:S(2)}) collective-permute-start(bf16[64,640]{1,0:T(8,128)(2,1)S(1)} %get-tuple-element.50), channel_id=1, source_target_pairs={{8,16},{24,32},{40,48},{56,64},{72,80},{88,96},{104,112},{16,8},{3... | collective-permute-start | bytes 245768 | tf_op jit(solution)/shard_map/ppermute | solution.py:409
  55.0 8.4 %collective-permute-start.6 = (bf16[64,640]{1,0:T(8,128)(2,1)S(1)}, bf16[64,640]{1,0:T(8,128)(2,1)S(1)}, u32[]{:S(2)}, u32[]{:S(2)}) collective-permute-start(bf16[64,640]{1,0:T(8,128)(2,1)S(1)} %get-tuple-element.51), channel_id=1, source_target_pairs={{0,8},{16,24},{32,40},{48,56},{64,72},{80,88},{96,104},{112,120},{... | collective-permute-start | bytes 245768 | tf_op jit(solution)/shard_map/ppermute | solution.py:409

commit v8 on v6

--- a/solution.py
+++ b/solution.py
@@ -10,6 +10,7 @@
 ROWS = 2048
 CROWS = 512
 CB = 64
+NOWHERE = CROWS + 9 * CB
 C = 64
 K = 27
 KC = K * C
@@ -118,17 +119,25 @@
     return mm(w_t[...], spread[:, 0:VB])
 
 
-def prepare_weights(w_sub, w_down, w_cat, w_t, wd_cat, wd_t):
+def prepare_sub(w_sub, w_cat, w_t):
     w_cat[...] = jnp.concatenate([w_sub[k] for k in range(K)], axis=1)
     w_t[...] = w_sub[...].reshape(KC, C).T
+
+
+def prepare_down(w_down, wd_cat, wd_t):
     wd_cat[...] = jnp.concatenate([w_down[k] for k in range(8)], axis=1)
     wd_t[...] = w_down[...].reshape(8 * C, C).T
 
 
-def one_local(block, counts, feat, rows, frm, dmap, grad, w_cat, wd_cat, wd_t, outs, source):
+def live_rows(dmap):
+    return jnp.sum((dmap[0:1, :] < NOWHERE).astype(F32)).astype(jnp.int32)
+
+
+def one_local(block, live_count, feat, rows, frm, dmap, grad, w_cat, wd_cat, wd_t, outs, source):
     coarse_o, gpre_o, gsub_o, gdown_o = outs
-
-    @pl.when(block < counts[0, 0])
+    live = block * VB < live_count
+
+    @pl.when(live)
     def _():
         coarse, gpre, gsub, gdown, _ = forward_work(
             False, block * VB, feat, rows, frm, dmap, grad, None, w_cat, wd_cat, wd_t, source)
@@ -137,46 +146,61 @@
         gsub_o[...] += gsub
         gdown_o[...] += gdown
 
-    @pl.when(block >= counts[0, 0])
+    @pl.when(jnp.logical_not(live))
     def _():
         coarse_o[...] = jnp.zeros_like(coarse_o)
 
 
-def first_kernel(counts, feat, rows, frm, dmap, grad, w_sub, w_down,
-                 coarse_o, gpre_o, gsub_o, gdown_o, w_cat, w_t, wd_cat, wd_t, source):
-    prepare_weights(w_sub, w_down, w_cat, w_t, wd_cat, wd_t)
+def views(block, feat, rows, frm, dmap, grad):
+    a, b = block * VB, (block + 1) * VB
+    return feat.at[:, a:b], rows.at[:, :, a:b], frm.at[:, :, a:b], dmap.at[:, a:b], grad.at[:, a // 4:b // 4]
+
+
+def first_kernel(feat_h, rows_h, frm_h, dmap_h, grad_h, w_sub_h, w_down_h,
+                 coarse_o, gpre_o, gsub_o, gdown_o, w_cat, w_t, wd_cat, wd_t, feat, rows, frm, dmap, grad,
+                 source, w_sub, w_down, sems):
+    pairs = [(w_sub_h, w_sub), (w_down_h, w_down), (dmap_h, dmap), (rows_h, rows), (frm_h, frm), (feat_h, feat),
+             (grad_h, grad)]
+    copies = [pltpu.make_async_copy(a, b, sems.at[i]) for i, (a, b) in enumerate(pairs)]
+    for copy in copies:
+        copy.start()
     gsub_o[...] = jnp.zeros_like(gsub_o)
     gdown_o[...] = jnp.zeros_like(gdown_o)
-    one_local(1, counts, feat, rows, frm, dmap, grad, w_cat, wd_cat, wd_t,
-              (coarse_o, gpre_o, gsub_o, gdown_o), source)
-
-
-def rest_kernel(counts, feat, rows, frm, dmap, grad, w_cat, wd_cat, wd_t, gsub, gdown, coarse_a, gpre_a,
+    copies[0].wait()
+    prepare_sub(w_sub, w_cat, w_t)
+    copies[1].wait()
+    prepare_down(w_down, wd_cat, wd_t)
+    for copy in copies[2:]:
+        copy.wait()
+    one_local(1, live_rows(dmap), *views(1, feat, rows, frm, dmap, grad), w_cat, wd_cat, wd_t,
+              (coarse_o.at[:, CQ:2 * CQ], gpre_o.at[:, VB:2 * VB], gsub_o, gdown_o), source)
+
+
+def rest_kernel(feat, rows, frm, dmap, grad, w_cat, wd_cat, wd_t, gsub, gdown, coarse, gpre,
                 coarse_o, gpre_o, gsub_o, gdown_o, source):
-    i = pl.program_id(0)
-
-    @pl.when(i == 0)
+    live_count = live_rows(dmap)
+    for i in (2, 3):
+        one_local(i, live_count, *views(i, feat, rows, frm, dmap, grad), w_cat, wd_cat, wd_t,
+                  (coarse_o.at[:, i * CQ:(i + 1) * CQ], gpre_o.at[:, i * VB:(i + 1) * VB], gsub_o, gdown_o), source)
+
+
+def local_scatter_kernel(rows, frm, dmap, gpre, w_t, gfeat_o, spread):
+    block = pl.program_id(0) + 1
+    live = block * VB < live_rows(dmap)
+
+    @pl.when(live)
     def _():
-        gsub_o[...] = gsub[...]
-        gdown_o[...] = gdown[...]
-
-    one_local(i + 2, counts, feat, rows, frm, dmap, grad, w_cat, wd_cat, wd_t,
-              (coarse_o, gpre_o, gsub_o, gdown_o), source)
-
-
-def local_scatter_kernel(counts, rows, frm, gpre, w_t, gfeat_o, spread):
-    block = pl.program_id(0) + 1
-
-    @pl.when(block < counts[0, 0])
-    def _():
-        gfeat_o[...] = scatter_work(False, block * VB, rows, frm, gpre[...], w_t, spread).astype(BF)
-
-    @pl.when(block >= counts[0, 0])
+        here = pl.ds(pl.multiple_of(block * VB, VB), VB)
+        gfeat_o[...] = scatter_work(
+            False, block * VB, rows.at[:, :, here], frm.at[:, :, here], gpre[:, here], w_t, spread).astype(BF)
+
+    @pl.when(jnp.logical_not(live))
     def _():
         gfeat_o[...] = jnp.zeros_like(gfeat_o)
 
 
 WHOLE = pl.BlockSpec(memory_space=pltpu.VMEM)
+SCALAR = pl.BlockSpec(memory_space=pltpu.SMEM)
 
 
 def full(shape):
@@ -209,50 +233,45 @@
     return jax.ShapeDtypeStruct(shape, dtype)
 
 
-def first_call(counts, feat, rows, frm, dmap, grad, w_sub, w_down):
+def first_call(feat, rows, frm, dmap, grad, w_sub, w_down):
     weights = [(C, KC), (C, KC), (C, 8 * C), (C, 8 * C)]
+    arrays = [feat, rows, frm, dmap, grad]
     return pl.pallas_call(
         first_kernel,
-        grid=(1,),
-        in_specs=[pl.BlockSpec(memory_space=pltpu.SMEM)] + table_specs(1) + [piped((K, C, C)), piped((8, C, C))],
-        out_specs=[columns((C, CQ), 1), columns((C, VB), 1), full((C, KC)), full((8 * C, C))]
-        + [full(w) for w in weights],
+        in_specs=[pl.BlockSpec(memory_space=pltpu.HBM)] * 7,
+        out_specs=[WHOLE] * 13,
         out_shape=[sd((C, CROWS), BF), sd((C, ROWS), BF), sd((C, KC), F32), sd((8 * C, C), F32)]
-        + [sd(w, BF) for w in weights],
-        scratch_shapes=[SOURCE],
+        + [sd(w, BF) for w in weights] + [sd(a.shape, a.dtype) for a in arrays],
+        scratch_shapes=[SOURCE, pltpu.VMEM((K, C, C), BF), pltpu.VMEM((8, C, C), BF), pltpu.SemaphoreType.DMA((7,))],
         compiler_params=LIMIT,
         name="first_local_block",
-    )(counts, feat, rows, frm, dmap, grad, w_sub, w_down)
-
-
-def rest_call(counts, feat, rows, frm, dmap, grad, w_cat, wd_cat, wd_t, gsub, gdown, coarse_all, gpre_all):
+    )(*[in_hbm(a) for a in arrays + [w_sub, w_down]])
+
+
+def rest_call(feat, rows, frm, dmap, grad, w_cat, wd_cat, wd_t, gsub, gdown, coarse_all, gpre_all):
     return pl.pallas_call(
         rest_kernel,
-        grid=(2,),
-        in_specs=[pl.BlockSpec(memory_space=pltpu.SMEM)] + table_specs(2)
-        + [full((C, KC)), full((C, 8 * C)), full((C, 8 * C)), full((C, KC)), full((8 * C, C)),
-           pl.BlockSpec(memory_space=pl.ANY), pl.BlockSpec(memory_space=pl.ANY)],
-        out_specs=[columns((C, CQ), 2), columns((C, VB), 2), full((C, KC)), full((8 * C, C))],
+        in_specs=[WHOLE] * 12,
+        out_specs=[WHOLE] * 4,
         out_shape=[sd((C, CROWS), BF), sd((C, ROWS), BF), sd((C, KC), F32), sd((8 * C, C), F32)],
         scratch_shapes=[SOURCE],
-        input_output_aliases={11: 0, 12: 1},
+        input_output_aliases={10: 0, 11: 1, 8: 2, 9: 3},
         compiler_params=LIMIT,
         name="other_local_blocks",
-    )(counts, feat, rows, frm, dmap, grad, w_cat, wd_cat, wd_t, gsub, gdown, coarse_all, gpre_all)
-
-
-def local_scatter_call(counts, rows, frm, gpre_all, w_t):
+    )(feat, rows, frm, dmap, grad, w_cat, wd_cat, wd_t, gsub, gdown, coarse_all, gpre_all)
+
+
+def local_scatter_call(rows, frm, dmap, gpre_all, w_t):
     return pl.pallas_call(
         local_scatter_kernel,
         grid=(3,),
-        in_specs=[pl.BlockSpec(memory_space=pltpu.SMEM), index_columns(1), index_columns(1),
-                  columns((C, VB), 1), full((C, KC))],
+        in_specs=[WHOLE] * 5,
         out_specs=columns((C, VB), 1),
         out_shape=sd((C, ROWS), BF),
         scratch_shapes=[SOURCE],
         compiler_params=LIMIT,
         name="local_scatter_blocks",
-    )(counts, rows, frm, gpre_all, w_t)
+    )(rows, frm, dmap, gpre_all, w_t)
 
 
 def in_hbm(array):
@@ -306,6 +325,7 @@
 
 def border_kernel(side, feat, rows, frm, dmap, grad, near, column, far, w_cat, wd_cat, wd_t, gsub, gdown,
                   coarse_o, packed_o, gpre_o, split_o, source, below, above):
+    feat, rows, frm, dmap, grad = views(0, feat, rows, frm, dmap, grad)
     even = side[0] == 1
     below[...] = jnp.where(even, far[...], near[...])
     above[...] = jnp.where(even, near[...], far[...])
@@ -329,7 +349,7 @@
     return pl.pallas_call(
         border_kernel,
         grid=(1,),
-        in_specs=[pl.BlockSpec(memory_space=pltpu.SMEM)] + table_specs(0) + [slab, slab, slab, full((C, KC)), full((C, 8 * C)), full((C, 8 * C)),
+        in_specs=[SCALAR] + [WHOLE] * 5 + [slab, slab, slab, full((C, KC)), full((C, 8 * C)), full((C, 8 * C)),
                                    full((C, KC)), full((8 * C, C))],
         out_specs=[full((C, CQ)), piped((count * PIECE, 2 * C)), full((C, VB)), full((2 * C, VB))],
         out_shape=[sd((C, CQ), F32), sd((count * PIECE, 2 * C), BF), sd((C, VB), BF), sd((2 * C, VB), BF)],
@@ -340,8 +360,8 @@
 
 
 def border_scatter_kernel(side, rows, frm, dmap, gpre, split, w_t, gfeat_o, mid_o, near_o, far_o, spread):
-    gfeat_o[...] = scatter_work(True, 0, rows, frm, gpre[...], w_t, spread)
-    both = mm_nt(split[...], pick_edges(dmap[0:1, :]))
+    gfeat_o[...] = scatter_work(True, 0, rows.at[:, :, 0:VB], frm.at[:, :, 0:VB], gpre[...], w_t, spread)
+    both = mm_nt(split[...], pick_edges(dmap[0:1, 0:VB]))
     edge = both[:C] + both[C:]
     even = side[0] == 1
 
@@ -363,8 +383,7 @@
     return pl.pallas_call(
         border_scatter_kernel,
         grid=(1,),
-        in_specs=[pl.BlockSpec(memory_space=pltpu.SMEM), index_columns(0), index_columns(0), columns((2, VB), 0),
-                  full((C, VB)), full((2 * C, VB)),
+        in_specs=[SCALAR, WHOLE, WHOLE, WHOLE, full((C, VB)), full((2 * C, VB)),
                   full((C, KC))],
         out_specs=[full((C, VB)), full(slab), full(slab), full(slab)],
         out_shape=[sd((C, VB), F32), sd(slab, F32), sd(slab, BF), sd(slab, BF)],
@@ -378,7 +397,8 @@
     inc = total[...] + left[...].astype(F32) + right[...].astype(F32)
     gfeat_o[...] = (gfeat[...] + inc[:, 0:VB]).astype(BF)
     coarse_o[:, 0:CB] = (coarse[:, 0:CB] + inc[:, VB:VB + CB]).astype(BF)
-    coarse_o[:, CB:] = coarse[:, CB:].astype(BF)
+    coarse_o[:, CB:CQ] = coarse[:, CB:].astype(BF)
+    coarse_o[:, CQ:] = coarse_i[:, CQ:]
 
 
 def finish_call(coarse_all, gfeat_all, coarse, gfeat, total, left, right):
@@ -386,13 +406,12 @@
         finish_kernel,
         grid=(1,),
         in_specs=[
-            pl.BlockSpec(memory_space=pl.ANY),
-            pl.BlockSpec(memory_space=pl.ANY),
+            WHOLE, pl.BlockSpec(memory_space=pl.ANY),
             full((C, CQ)), full((C, VB)), full((C, WIDE)), full((C, WIDE)), full((C, WIDE)),
         ],
-        out_specs=[pl.BlockSpec((C, CQ), lambda i: (0, 0)), pl.BlockSpec((C, VB), lambda i: (0, 0))],
+        out_specs=[piped((C, CROWS)), pl.BlockSpec((C, VB), lambda i: (0, 0))],
         out_shape=[sd((C, CROWS), BF), sd((C, ROWS), BF)],
-        input_output_aliases={0: 0, 1: 1},
+        input_output_aliases={1: 1},
         compiler_params=SMALL,
         name="add_incoming",
     )(coarse_all, gfeat_all, coarse, gfeat, total, left, right)
@@ -435,13 +454,13 @@
     even_x, even_y = lax.axis_index("gx") % 2 == 0, lax.axis_index("gy") % 2 == 0
     side = even_y.astype(jnp.int32).reshape(1)
     near, far = swapped(border, "gx", True), swapped(border, "gx", False)
-    coarse_all, gpre_all, gsub, gdown, w_cat, w_t, wd_cat, wd_t = first_call(
-        counts, *[in_hbm(a) for a in (feat, rows, frm)], dmap, *[in_hbm(a) for a in (grad, w_sub, w_down)])
+    (coarse_all, gpre_all, gsub, gdown, w_cat, w_t, wd_cat, wd_t, feat, rows, frm, dmap, grad) = first_call(
+        feat, rows, frm, dmap, grad, w_sub, w_down)
     near, far, gsub = lax.optimization_barrier((near, far, gsub))
     column = jnp.stack([jnp.where(even_x, far, near), border, jnp.where(even_x, near, far)])
     near, far = swapped(column, "gy", True), swapped(column, "gy", False)
     coarse_all, gpre_all, gsub, gdown = rest_call(
-        counts, feat, rows, frm, dmap, grad, w_cat, wd_cat, wd_t, gsub, gdown, coarse_all, gpre_all)
+        feat, rows, frm, dmap, grad, w_cat, wd_cat, wd_t, gsub, gdown, coarse_all, gpre_all)
     coarse, packed, gpre, split = border_call(
         count, side, feat, rows, frm, dmap, grad, near, column, far, w_cat, wd_cat, wd_t, gsub, gdown)
     pieces = lax.all_to_all(packed.reshape(count, PAIRS, 2, 2 * C), ("gx", "gy"), 0, 0, tiled=True)
@@ -454,7 +473,7 @@
     near = swapped(jnp.where(even_x, total[2], total[0]).astype(BF), "gx", True)
     far = swapped(jnp.where(even_x, total[0], total[2]).astype(BF), "gx", False)
     gathered = lax.all_to_all(spread.reshape(shape), ("gx", "gy"), 0, 0, tiled=True).reshape(-1, 2 * C)
-    gfeat_all = local_scatter_call(counts, rows, frm, gpre_all, w_t)
+    gfeat_all = local_scatter_call(rows, frm, dmap, gpre_all, w_t)
     coarse_out, grad_features = finish_call(coarse_all, gfeat_all, coarse, gfeat, total[1], near, far)
     grad_w_sub, grad_w_down = weights_call(float(ROWS * count) ** -0.5, gathered)
     return coarse_out[None, None], grad_features[None, None], grad_w_sub, grad_w_down

time: 64 us -> 63.2 us (0.988)
  Pallas kernels: 19.1 us -> 13.9 us
  starting transfers between devices: 30 us -> 34.3 us
  waiting for transfers between devices: 12.6 us -> 13.6 us
  between operations: 1.5 us -> 0.79 us
    pallas_call x6, Pallas kernels: 16.3 us -> 11.1 us  [the longest x1 4.08 us: border_call(): pl.pallas_call(border_kernel, grid=(1,), in_specs=[SCALAR] + [WHOLE] * 5...]
    ppermute x8, starting transfers between devices: 16 us -> 18.6 us  [swapped(): return lax.ppermute(block, axis, pairs + [(b, a) for a, b in pairs])]
    all_to_all x1, starting transfers between devices: 9.49 us -> 11.2 us  [shards(): lax.all_to_all(packed.reshape(count, PAIRS, 2, 2 * C), ('gx', 'gy'), 0, 0...]
    ppermute x8, waiting for transfers between devices: 5.18 us -> 6.05 us  [swapped(): return lax.ppermute(block, axis, pairs + [(b, a) for a, b in pairs])]
  transfers between devices with their start and end apart: 10 -> 10, of which waited for: 4 -> 5; matrix products, arithmetic and copies ran while one was open for 0% -> 0% of each run, Pallas kernels for 21% -> 12%
where the time goes in v8:
time: 63.2 us; the launch traced here: 62.7 us
  starting transfers between devices  34.3 us (54%)
  Pallas kernels  13.9 us (22%)
  waiting for transfers between devices  13.6 us (22%)
  between operations  0.79 us (1%)
    ppermute x8, starting transfers between devices, swapped(): return lax.ppermute(block, axis, pairs + [(b, a) for a, b in pairs])  18.6 us
    all_to_all x1, starting transfers between devices, shards(): lax.all_to_all(packed.reshape(count, PAIRS, 2, 2 * C), ('gx', 'gy'), 0, 0...  11.2 us
    ppermute x8, waiting for transfers between devices, swapped(): return lax.ppermute(block, axis, pairs + [(b, a) for a, b in pairs])  6.05 us
    all_to_all x1, waiting for transfers between devices, shards(): lax.all_to_all(packed.reshape(count, PAIRS, 2, 2 * C), ('gx', 'gy'), 0, 0...  5 us
    all_to_all x1, starting transfers between devices, shards(): lax.all_to_all(spread.reshape(shape), ('gx', 'gy'), 0, 0, tiled=True)  4.44 us
    pallas_call x1, Pallas kernels, border_call(): pl.pallas_call(border_kernel, grid=(1,), in_specs=[SCALAR] + [WHOLE] * 5...  4.08 us
    pallas_call x1, Pallas kernels, border_scatter_call(): pl.pallas_call(border_scatter_kernel, grid=(1,), in_specs=[SCALAR, WHOLE,...  2.97 us
    all_to_all x1, waiting for transfers between devices, shards(): lax.all_to_all(spread.reshape(shape), ('gx', 'gy'), 0, 0, tiled=True)  2.55 us
  transfers between devices with their start and end apart: 10, of which 5 were waited for; matrix products, arithmetic and copies ran while one was open for 0% of the time, Pallas kernels for 12%

profile of v8, /device:TPU:1, one launch (start us, length us, event | category | flops | bytes accessed | tf_op | source)
XLA Modules:
  0.0 62.7 jit_solution(8109548326773775963)
XLA Ops:
  0.6 0.9 %pack_border.1 = bf16[64,640]{1,0:T(8,128)(2,1)S(1)} custom-call(bf16[64,2048]{1,0:T(8,128)(2,1)} %bitcast.27, bf16[64,512]{1,0:T(8,128)(2,1)} %bitcast.29), custom_call_target="tpu_custom_call" | custom-call | tf_op jit(solution)/shard_map/pack_border/pallas_call | solution.py:291
  1.5 0.7 %collective-permute-start.1 = (bf16[64,640]{1,0:T(8,128)(2,1)S(1)}, bf16[64,640]{1,0:T(8,128)(2,1)S(1)}, u32[]{:S(2)}, u32[]{:S(2)}) collective-permute-start(bf16[64,640]{1,0:T(8,128)(2,1)S(1)} %pack_border.1), channel_id=1, source_target_pairs={{8,16},{24,32},{40,48},{56,64},{72,80},{88,96},{104,112},{16,8},{3... | collective-permute-start | bytes 245768 | tf_op jit(solution)/shard_map/ppermute | solution.py:444
  2.2 4.7 %collective-permute-start = (bf16[64,640]{1,0:T(8,128)(2,1)S(1)}, bf16[64,640]{1,0:T(8,128)(2,1)S(1)}, u32[]{:S(2)}, u32[]{:S(2)}) collective-permute-start(bf16[64,640]{1,0:T(8,128)(2,1)S(1)} %pack_border.1), channel_id=1, source_target_pairs={{0,8},{16,24},{32,40},{48,56},{64,72},{80,88},{96,104},{112,120},{... | collective-permute-start | bytes 245768 | tf_op jit(solution)/shard_map/ppermute | solution.py:444
  6.9 1.6 %first_local_block.1 = (bf16[64,512]{1,0:T(8,128)(2,1)S(1)}, bf16[64,2048]{1,0:T(8,128)(2,1)S(1)}, f32[64,1728]{1,0:T(8,128)S(1)}, f32[512,64]{1,0:T(8,128)S(1)}...) custom-call(bf16[64,2048]{1,0:T(8,128)(2,1)} %bitcast.28, ...), custom_call_target="tpu_custom_call" | custom-call | tf_op jit(solution)/shard_map/first_local_block/pallas_call | solution.py:239
  8.5 0.0 collective-permute-done.1
  8.5 0.2 collective-permute-done
  8.8 4.8 %collective-permute-start.3 = (bf16[3,64,640]{2,1,0:T(8,128)(2,1)S(1)}, bf16[3,64,640]{2,1,0:T(8,128)(2,1)S(1)}, u32[]{:S(2)}, u32[]{:S(2)}) collective-permute-start(bf16[3,64,640]{2,1,0:T(8,128)(2,1)S(1)} %pad_maximum_fusion.column), channel_id=1, source_target_pairs={{1,2},{3,4},{5,6},{2,1},{4,3},{6,5},{9,10},{11,12},{13,14},{10,9},... | collective-permute-start | bytes 737288 | tf_op jit(solution)/shard_map/ppermute | solution.py:444
  13.7 0.1 collective-permute-start.2
  13.8 0.2 other_local_blocks.1
  13.9 3.6 %collective-permute-done.3.far = bf16[3,64,640]{2,1,0:T(8,128)(2,1)S(1)} collective-permute-done((bf16[3,64,640]{2,1,0:T(8,128)(2,1)S(1)}, bf16[3,64,640]{2,1,0:T(8,128)(2,1)S(1)}, u32[]{:S(2)}, u32[]{:S(2)}) %collective-permute-start.3) | collective-permute-done | bytes 245792 | tf_op jit(solution)/shard_map/ppermute | solution.py:444
  17.5 0.0 collective-permute-done.2.near
  17.5 4.1 %border_block.1 = (f32[64,128]{1,0:T(8,128)S(1)}, bf16[1280,128]{1,0:T(8,128)(2,1)}, bf16[64,512]{1,0:T(8,128)(2,1)S(1)}, bf16[128,512]{1,0:T(8,128)(2,1)S(1)}) custom-call(s32[1]{0:T(128)} %bitcast.5.side, bf16[64,2048]{1,0:T(8,128)(2,1)S(1)} %get-tuple-element.39.feat, s32[27,1,2048]{2,1,0:T(1,128)S(1)} %get-tuple-element.40.rows, ...), custom_call_target="tpu_custom_call" | custom-call | tf_op jit(solution)/shard_map/border_block/pallas_call | solution.py:349
  21.6 11.2 %all-to-all-start = ((bf16[128,5,2,128]{3,2,1,0:T(2,128)(2,1)}), bf16[128,5,2,128]{3,2,1,0:T(2,128)(2,1)S(1)}, u32[]{:S(2)}, u32[]{:S(2)}) async-start(bf16[128,5,2,128]{3,2,1,0:T(2,128)(2,1)} %bitcast.9), calls=%async_computation | async-start | bytes 655360 | tf_op jit(solution)/shard_map/all_to_all | solution.py:466
  32.8 3.0 %border_scatter_block.1 = (f32[64,512]{1,0:T(8,128)S(1)}, f32[3,64,640]{2,1,0:T(8,128)S(1)}, bf16[3,64,640]{2,1,0:T(8,128)(2,1)S(1)}, bf16[3,64,640]{2,1,0:T(8,128)(2,1)S(1)}) custom-call(s32[1]{0:T(128)} %bitcast.5.side, s32[27,1,2048]{2,1,0:T(1,128)S(1)} %get-tuple-element.40.rows, s32[27,1,2048]{2,1,0:T(1,128)S(1)} %get-tuple-element.41.frm, ...), custom_call_target="tpu_custom_call" | custom-call | tf_op jit(solution)/shard_map/border_scatter_block/pallas_call | solution.py:383
  35.8 1.3 %collective-permute-start.4 = (bf16[3,64,640]{2,1,0:T(8,128)(2,1)S(1)}, bf16[3,64,640]{2,1,0:T(8,128)(2,1)S(1)}, u32[]{:S(2)}, u32[]{:S(2)}) collective-permute-start(bf16[3,64,640]{2,1,0:T(8,128)(2,1)S(1)} %get-tuple-element.67), channel_id=1, source_target_pairs={{0,1},{2,3},{4,5},{6,7},{1,0},{3,2},{5,4},{7,6},{8,9},{10,11},{12,... | collective-permute-start | bytes 737288 | tf_op jit(solution)/shard_map/ppermute | solution.py:444
  37.1 2.4 %collective-permute-start.5 = (bf16[3,64,640]{2,1,0:T(8,128)(2,1)S(1)}, bf16[3,64,640]{2,1,0:T(8,128)(2,1)S(1)}, u32[]{:S(2)}, u32[]{:S(2)}) collective-permute-start(bf16[3,64,640]{2,1,0:T(8,128)(2,1)S(1)} %get-tuple-element.68), channel_id=1, source_target_pairs={{1,2},{3,4},{5,6},{2,1},{4,3},{6,5},{9,10},{11,12},{13,14},{10,9},... | collective-permute-start | bytes 737288 | tf_op jit(solution)/shard_map/ppermute | solution.py:444
  39.5 5.0 %all-to-all-done = bf16[128,5,2,128]{3,2,1,0:T(2,128)(2,1)S(1)} async-done(((bf16[128,5,2,128]{3,2,1,0:T(2,128)(2,1)}), bf16[128,5,2,128]{3,2,1,0:T(2,128)(2,1)S(1)}, u32[]{:S(2)}, u32[]{:S(2)}) %all-to-all-start) | async-done | bytes 327712 | tf_op jit(solution)/shard_map/all_to_all | solution.py:466
  44.5 0.8 %sum_pieces.1 = bf16[1280,128]{1,0:T(8,128)(2,1)} custom-call(bf16[1280,128]{1,0:T(8,128)(2,1)S(1)} %bitcast.24), custom_call_target="tpu_custom_call" | custom-call | tf_op jit(solution)/shard_map/sum_pieces/pallas_call | solution.py:315
  45.3 4.4 %all-to-all-start.1 = ((bf16[128,5,2,128]{3,2,1,0:T(2,128)(2,1)}), bf16[128,5,2,128]{3,2,1,0:T(2,128)(2,1)S(1)}, u32[]{:S(2)}, u32[]{:S(2)}) async-start(bf16[128,5,2,128]{3,2,1,0:T(2,128)(2,1)} %bitcast.16), calls=%async_computation.1 | async-start | bytes 655360 | tf_op jit(solution)/shard_map/all_to_all | solution.py:475
  49.8 0.0 collective-permute-done.4
  49.8 0.0 collective-permute-done.5
  49.8 0.1 convert_add_fusion
  49.9 0.7 %collective-permute-start.7 = (bf16[64,640]{1,0:T(8,128)(2,1)S(1)}, bf16[64,640]{1,0:T(8,128)(2,1)S(1)}, u32[]{:S(2)}, u32[]{:S(2)}) collective-permute-start(bf16[64,640]{1,0:T(8,128)(2,1)S(1)} %get-tuple-element.74), channel_id=1, source_target_pairs={{8,16},{24,32},{40,48},{56,64},{72,80},{88,96},{104,112},{16,8},{3... | collective-permute-start | bytes 245768 | tf_op jit(solution)/shard_map/ppermute | solution.py:444
  50.6 3.9 %collective-permute-start.6 = (bf16[64,640]{1,0:T(8,128)(2,1)S(1)}, bf16[64,640]{1,0:T(8,128)(2,1)S(1)}, u32[]{:S(2)}, u32[]{:S(2)}) collective-permute-start(bf16[64,640]{1,0:T(8,128)(2,1)S(1)} %get-tuple-element.75), channel_id=1, source_target_pairs={{0,8},{16,24},{32,40},{48,56},{64,72},{80,88},{96,104},{112,120},{... | collective-permute-start | bytes 245768 | tf_op jit(solution)/shard_map/ppermute | solution.py:444
  54.5 1.6 %local_scatter_blocks.1.gfeat_i = bf16[64,2048]{1,0:T(8,128)(2,1)} custom-call(s32[27,1,2048]{2,1,0:T(1,128)S(1)} %get-tuple-element.40.rows, s32[27,1,2048]{2,1,0:T(1,128)S(1)} %get-tuple-element.41.frm, s32[2,2048]{1,0:T(2,128)S(1)} %get-tuple-element.42.dmap, bf16[64,2048]{1,0:T(8,128)(2,1)S(1)} %get-tuple-element.63.gpre, ...), custom_call_target="tpu_custom_call" | custom-call | tf_op jit(solution)/shard_map/local_scatter_blocks/pallas_call | solution.py:265
  56.1 0.0 collective-permute-done.7.right
  56.1 2.2 %collective-permute-done.6.left = bf16[64,640]{1,0:T(8,128)(2,1)S(1)} collective-permute-done((bf16[64,640]{1,0:T(8,128)(2,1)S(1)}, bf16[64,640]{1,0:T(8,128)(2,1)S(1)}, u32[]{:S(2)}, u32[]{:S(2)}) %collective-permute-start.6) | collective-permute-done | bytes 81952 | tf_op jit(solution)/shard_map/ppermute | solution.py:444
  58.3 0.7 %add_incoming.1 = (bf16[64,512]{1,0:T(8,128)(2,1)}, bf16[64,2048]{1,0:T(8,128)(2,1)}) custom-call(bf16[64,512]{1,0:T(8,128)(2,1)S(1)} %get-tuple-element.52.coarse_i, bf16[64,2048]{1,0:T(8,128)(2,1)} %local_scatter_blocks.1.gfeat_i, f32[64,128]{1,0:T(8,128)S(1)} %get-tuple-element.64.coarse, ...), custom_call_target="tpu_custom_call", output_to_operand_aliasing={{1}: (1, {})} | custom-call | tf_op jit(solution)/shard_map/add_incoming/pallas_call | solution.py:405
  59.0 2.6 %all-to-all-done.1 = bf16[128,5,2,128]{3,2,1,0:T(2,128)(2,1)S(1)} async-done(((bf16[128,5,2,128]{3,2,1,0:T(2,128)(2,1)}), bf16[128,5,2,128]{3,2,1,0:T(2,128)(2,1)S(1)}, u32[]{:S(2)}, u32[]{:S(2)}) %all-to-all-start.1) | async-done | bytes 327712 | tf_op jit(solution)/shard_map/all_to_all | solution.py:475
  61.5 1.2 %unpack_weights.1 = (f32[27,64,64]{2,1,0:T(8,128)}, f32[8,64,64]{2,1,0:T(8,128)}) custom-call(bf16[1280,128]{1,0:T(8,128)(2,1)S(1)} %bitcast.23), custom_call_target="tpu_custom_call" | custom-call | tf_op jit(solution)/shard_map/unpack_weights/pallas_call | solution.py:430
  (4 shorter events, 0.1 us)
Async XLA Ops:
  1.5 7.0 %collective-permute-start.1 = (bf16[64,640]{1,0:T(8,128)(2,1)S(1)}, bf16[64,640]{1,0:T(8,128)(2,1)S(1)}, u32[]{:S(2)}, u32[]{:S(2)}) collective-permute-start(bf16[64,640]{1,0:T(8,128)(2,1)S(1)} %pack_border.1), channel_id=1, source_target_pairs={{8,16},{24,32},{40,48},{56,64},{72,80},{88,96},{104,112},{16,8},{3... | collective-permute-start | bytes 245768 | tf_op jit(solution)/shard_map/ppermute | solution.py:444
  2.2 6.6 %collective-permute-start = (bf16[64,640]{1,0:T(8,128)(2,1)S(1)}, bf16[64,640]{1,0:T(8,128)(2,1)S(1)}, u32[]{:S(2)}, u32[]{:S(2)}) collective-permute-start(bf16[64,640]{1,0:T(8,128)(2,1)S(1)} %pack_border.1), channel_id=1, source_target_pairs={{0,8},{16,24},{32,40},{48,56},{64,72},{80,88},{96,104},{112,120},{... | collective-permute-start | bytes 245768 | tf_op jit(solution)/shard_map/ppermute | solution.py:444
  8.8 8.7 %collective-permute-start.3 = (bf16[3,64,640]{2,1,0:T(8,128)(2,1)S(1)}, bf16[3,64,640]{2,1,0:T(8,128)(2,1)S(1)}, u32[]{:S(2)}, u32[]{:S(2)}) collective-permute-start(bf16[3,64,640]{2,1,0:T(8,128)(2,1)S(1)} %pad_maximum_fusion.column), channel_id=1, source_target_pairs={{1,2},{3,4},{5,6},{2,1},{4,3},{6,5},{9,10},{11,12},{13,14},{10,9},... | collective-permute-start | bytes 737288 | tf_op jit(solution)/shard_map/ppermute | solution.py:444
  13.7 3.9 %collective-permute-start.2 = (bf16[3,64,640]{2,1,0:T(8,128)(2,1)S(1)}, bf16[3,64,640]{2,1,0:T(8,128)(2,1)S(1)}, u32[]{:S(2)}, u32[]{:S(2)}) collective-permute-start(bf16[3,64,640]{2,1,0:T(8,128)(2,1)S(1)} %pad_maximum_fusion.column), channel_id=1, source_target_pairs={{0,1},{2,3},{4,5},{6,7},{1,0},{3,2},{5,4},{7,6},{8,9},{10,11},{12,... | collective-permute-start | bytes 737288 | tf_op jit(solution)/shard_map/ppermute | solution.py:444
  21.6 22.9 %all-to-all-start = ((bf16[128,5,2,128]{3,2,1,0:T(2,128)(2,1)}), bf16[128,5,2,128]{3,2,1,0:T(2,128)(2,1)S(1)}, u32[]{:S(2)}, u32[]{:S(2)}) async-start(bf16[128,5,2,128]{3,2,1,0:T(2,128)(2,1)} %bitcast.9), calls=%async_computation | async-start | bytes 655360 | tf_op jit(solution)/shard_map/all_to_all | solution.py:466
  35.8 14.0 %collective-permute-start.4 = (bf16[3,64,640]{2,1,0:T(8,128)(2,1)S(1)}, bf16[3,64,640]{2,1,0:T(8,128)(2,1)S(1)}, u32[]{:S(2)}, u32[]{:S(2)}) collective-permute-start(bf16[3,64,640]{2,1,0:T(8,128)(2,1)S(1)} %get-tuple-element.67), channel_id=1, source_target_pairs={{0,1},{2,3},{4,5},{6,7},{1,0},{3,2},{5,4},{7,6},{8,9},{10,11},{12,... | collective-permute-start | bytes 737288 | tf_op jit(solution)/shard_map/ppermute | solution.py:444
  37.1 12.7 %collective-permute-start.5 = (bf16[3,64,640]{2,1,0:T(8,128)(2,1)S(1)}, bf16[3,64,640]{2,1,0:T(8,128)(2,1)S(1)}, u32[]{:S(2)}, u32[]{:S(2)}) collective-permute-start(bf16[3,64,640]{2,1,0:T(8,128)(2,1)S(1)} %get-tuple-element.68), channel_id=1, source_target_pairs={{1,2},{3,4},{5,6},{2,1},{4,3},{6,5},{9,10},{11,12},{13,14},{10,9},... | collective-permute-start | bytes 737288 | tf_op jit(solution)/shard_map/ppermute | solution.py:444
  45.3 16.2 %all-to-all-start.1 = ((bf16[128,5,2,128]{3,2,1,0:T(2,128)(2,1)}), bf16[128,5,2,128]{3,2,1,0:T(2,128)(2,1)S(1)}, u32[]{:S(2)}, u32[]{:S(2)}) async-start(bf16[128,5,2,128]{3,2,1,0:T(2,128)(2,1)} %bitcast.16), calls=%async_computation.1 | async-start | bytes 655360 | tf_op jit(solution)/shard_map/all_to_all | solution.py:475
  49.9 6.2 %collective-permute-start.7 = (bf16[64,640]{1,0:T(8,128)(2,1)S(1)}, bf16[64,640]{1,0:T(8,128)(2,1)S(1)}, u32[]{:S(2)}, u32[]{:S(2)}) collective-permute-start(bf16[64,640]{1,0:T(8,128)(2,1)S(1)} %get-tuple-element.74), channel_id=1, source_target_pairs={{8,16},{24,32},{40,48},{56,64},{72,80},{88,96},{104,112},{16,8},{3... | collective-permute-start | bytes 245768 | tf_op jit(solution)/shard_map/ppermute | solution.py:444
  50.6 7.7 %collective-permute-start.6 = (bf16[64,640]{1,0:T(8,128)(2,1)S(1)}, bf16[64,640]{1,0:T(8,128)(2,1)S(1)}, u32[]{:S(2)}, u32[]{:S(2)}) collective-permute-start(bf16[64,640]{1,0:T(8,128)(2,1)S(1)} %get-tuple-element.75), channel_id=1, source_target_pairs={{0,8},{16,24},{32,40},{48,56},{64,72},{80,88},{96,104},{112,120},{... | collective-permute-start | bytes 245768 | tf_op jit(solution)/shard_map/ppermute | solution.py:444

commit v9 on v8

--- a/solution.py
+++ b/solution.py
@@ -178,6 +178,10 @@
 
 def rest_kernel(feat, rows, frm, dmap, grad, w_cat, wd_cat, wd_t, gsub, gdown, coarse, gpre,
                 coarse_o, gpre_o, gsub_o, gdown_o, source):
+    gsub_o[...] = gsub[...]
+    gdown_o[...] = gdown[...]
+    coarse_o[:, CQ:2 * CQ] = coarse[:, CQ:2 * CQ]
+    gpre_o[:, VB:2 * VB] = gpre[:, VB:2 * VB]
     live_count = live_rows(dmap)
     for i in (2, 3):
         one_local(i, live_count, *views(i, feat, rows, frm, dmap, grad), w_cat, wd_cat, wd_t,

time: 63.2 us -> 63.3 us (level)
  no operation moved by 1% of the time
where the time goes in v9:
time: 63.3 us; the launch traced here: 62.8 us
  starting transfers between devices  34.4 us (54%)
  Pallas kernels  14 us (22%)
  waiting for transfers between devices  13.5 us (21%)
  between operations  0.79 us (1%)
    ppermute x8, starting transfers between devices, swapped(): return lax.ppermute(block, axis, pairs + [(b, a) for a, b in pairs])  18.6 us
    all_to_all x1, starting transfers between devices, shards(): lax.all_to_all(packed.reshape(count, PAIRS, 2, 2 * C), ('gx', 'gy'), 0, 0...  11.3 us
    ppermute x8, waiting for transfers between devices, swapped(): return lax.ppermute(block, axis, pairs + [(b, a) for a, b in pairs])  5.97 us
    all_to_all x1, waiting for transfers between devices, shards(): lax.all_to_all(packed.reshape(count, PAIRS, 2, 2 * C), ('gx', 'gy'), 0, 0...  5.01 us
    all_to_all x1, starting transfers between devices, shards(): lax.all_to_all(spread.reshape(shape), ('gx', 'gy'), 0, 0, tiled=True)  4.44 us
    pallas_call x1, Pallas kernels, border_call(): pl.pallas_call(border_kernel, grid=(1,), in_specs=[SCALAR] + [WHOLE] * 5...  4.08 us
    pallas_call x1, Pallas kernels, border_scatter_call(): pl.pallas_call(border_scatter_kernel, grid=(1,), in_specs=[SCALAR, WHOLE,...  2.97 us
    all_to_all x1, waiting for transfers between devices, shards(): lax.all_to_all(spread.reshape(shape), ('gx', 'gy'), 0, 0, tiled=True)  2.55 us
  transfers between devices with their start and end apart: 10, of which 5 were waited for; matrix products, arithmetic and copies ran while one was open for 0% of the time, Pallas kernels for 12%

profile of v9, /device:TPU:1, one launch (start us, length us, event | category | flops | bytes accessed | tf_op | source)
XLA Modules:
  0.0 62.8 jit_solution(5065601554268215890)
XLA Ops:
  0.6 0.9 %pack_border.1 = bf16[64,640]{1,0:T(8,128)(2,1)S(1)} custom-call(bf16[64,2048]{1,0:T(8,128)(2,1)} %bitcast.27, bf16[64,512]{1,0:T(8,128)(2,1)} %bitcast.29), custom_call_target="tpu_custom_call" | custom-call | tf_op jit(solution)/shard_map/pack_border/pallas_call | solution.py:295
  1.5 0.7 %collective-permute-start.1 = (bf16[64,640]{1,0:T(8,128)(2,1)S(1)}, bf16[64,640]{1,0:T(8,128)(2,1)S(1)}, u32[]{:S(2)}, u32[]{:S(2)}) collective-permute-start(bf16[64,640]{1,0:T(8,128)(2,1)S(1)} %pack_border.1), channel_id=1, source_target_pairs={{8,16},{24,32},{40,48},{56,64},{72,80},{88,96},{104,112},{16,8},{3... | collective-permute-start | bytes 245768 | tf_op jit(solution)/shard_map/ppermute | solution.py:448
  2.2 4.7 %collective-permute-start = (bf16[64,640]{1,0:T(8,128)(2,1)S(1)}, bf16[64,640]{1,0:T(8,128)(2,1)S(1)}, u32[]{:S(2)}, u32[]{:S(2)}) collective-permute-start(bf16[64,640]{1,0:T(8,128)(2,1)S(1)} %pack_border.1), channel_id=1, source_target_pairs={{0,8},{16,24},{32,40},{48,56},{64,72},{80,88},{96,104},{112,120},{... | collective-permute-start | bytes 245768 | tf_op jit(solution)/shard_map/ppermute | solution.py:448
  6.9 1.6 %first_local_block.1 = (bf16[64,512]{1,0:T(8,128)(2,1)S(1)}, bf16[64,2048]{1,0:T(8,128)(2,1)S(1)}, f32[64,1728]{1,0:T(8,128)S(1)}, f32[512,64]{1,0:T(8,128)S(1)}...) custom-call(bf16[64,2048]{1,0:T(8,128)(2,1)} %bitcast.28, ...), custom_call_target="tpu_custom_call" | custom-call | tf_op jit(solution)/shard_map/first_local_block/pallas_call | solution.py:243
  8.5 0.0 collective-permute-done.1
  8.5 0.2 collective-permute-done
  8.8 4.8 %collective-permute-start.3 = (bf16[3,64,640]{2,1,0:T(8,128)(2,1)S(1)}, bf16[3,64,640]{2,1,0:T(8,128)(2,1)S(1)}, u32[]{:S(2)}, u32[]{:S(2)}) collective-permute-start(bf16[3,64,640]{2,1,0:T(8,128)(2,1)S(1)} %pad_maximum_fusion.column), channel_id=1, source_target_pairs={{1,2},{3,4},{5,6},{2,1},{4,3},{6,5},{9,10},{11,12},{13,14},{10,9},... | collective-permute-start | bytes 737288 | tf_op jit(solution)/shard_map/ppermute | solution.py:448
  13.7 0.1 collective-permute-start.2
  13.8 0.2 other_local_blocks.1
  14.0 3.5 %collective-permute-done.3.far = bf16[3,64,640]{2,1,0:T(8,128)(2,1)S(1)} collective-permute-done((bf16[3,64,640]{2,1,0:T(8,128)(2,1)S(1)}, bf16[3,64,640]{2,1,0:T(8,128)(2,1)S(1)}, u32[]{:S(2)}, u32[]{:S(2)}) %collective-permute-start.3) | collective-permute-done | bytes 245792 | tf_op jit(solution)/shard_map/ppermute | solution.py:448
  17.5 0.0 collective-permute-done.2.near
  17.5 4.1 %border_block.1 = (f32[64,128]{1,0:T(8,128)S(1)}, bf16[1280,128]{1,0:T(8,128)(2,1)}, bf16[64,512]{1,0:T(8,128)(2,1)S(1)}, bf16[128,512]{1,0:T(8,128)(2,1)S(1)}) custom-call(s32[1]{0:T(128)} %bitcast.5.side, bf16[64,2048]{1,0:T(8,128)(2,1)S(1)} %get-tuple-element.39.feat, s32[27,1,2048]{2,1,0:T(1,128)S(1)} %get-tuple-element.40.rows, ...), custom_call_target="tpu_custom_call" | custom-call | tf_op jit(solution)/shard_map/border_block/pallas_call | solution.py:353
  21.6 11.3 %all-to-all-start = ((bf16[128,5,2,128]{3,2,1,0:T(2,128)(2,1)}), bf16[128,5,2,128]{3,2,1,0:T(2,128)(2,1)S(1)}, u32[]{:S(2)}, u32[]{:S(2)}) async-start(bf16[128,5,2,128]{3,2,1,0:T(2,128)(2,1)} %bitcast.9), calls=%async_computation | async-start | bytes 655360 | tf_op jit(solution)/shard_map/all_to_all | solution.py:470
  32.9 3.0 %border_scatter_block.1 = (f32[64,512]{1,0:T(8,128)S(1)}, f32[3,64,640]{2,1,0:T(8,128)S(1)}, bf16[3,64,640]{2,1,0:T(8,128)(2,1)S(1)}, bf16[3,64,640]{2,1,0:T(8,128)(2,1)S(1)}) custom-call(s32[1]{0:T(128)} %bitcast.5.side, s32[27,1,2048]{2,1,0:T(1,128)S(1)} %get-tuple-element.40.rows, s32[27,1,2048]{2,1,0:T(1,128)S(1)} %get-tuple-element.41.frm, ...), custom_call_target="tpu_custom_call" | custom-call | tf_op jit(solution)/shard_map/border_scatter_block/pallas_call | solution.py:387
  35.9 1.3 %collective-permute-start.4 = (bf16[3,64,640]{2,1,0:T(8,128)(2,1)S(1)}, bf16[3,64,640]{2,1,0:T(8,128)(2,1)S(1)}, u32[]{:S(2)}, u32[]{:S(2)}) collective-permute-start(bf16[3,64,640]{2,1,0:T(8,128)(2,1)S(1)} %get-tuple-element.67), channel_id=1, source_target_pairs={{0,1},{2,3},{4,5},{6,7},{1,0},{3,2},{5,4},{7,6},{8,9},{10,11},{12,... | collective-permute-start | bytes 737288 | tf_op jit(solution)/shard_map/ppermute | solution.py:448
  37.2 2.4 %collective-permute-start.5 = (bf16[3,64,640]{2,1,0:T(8,128)(2,1)S(1)}, bf16[3,64,640]{2,1,0:T(8,128)(2,1)S(1)}, u32[]{:S(2)}, u32[]{:S(2)}) collective-permute-start(bf16[3,64,640]{2,1,0:T(8,128)(2,1)S(1)} %get-tuple-element.68), channel_id=1, source_target_pairs={{1,2},{3,4},{5,6},{2,1},{4,3},{6,5},{9,10},{11,12},{13,14},{10,9},... | collective-permute-start | bytes 737288 | tf_op jit(solution)/shard_map/ppermute | solution.py:448
  39.6 5.0 %all-to-all-done = bf16[128,5,2,128]{3,2,1,0:T(2,128)(2,1)S(1)} async-done(((bf16[128,5,2,128]{3,2,1,0:T(2,128)(2,1)}), bf16[128,5,2,128]{3,2,1,0:T(2,128)(2,1)S(1)}, u32[]{:S(2)}, u32[]{:S(2)}) %all-to-all-start) | async-done | bytes 327712 | tf_op jit(solution)/shard_map/all_to_all | solution.py:470
  44.7 0.8 %sum_pieces.1 = bf16[1280,128]{1,0:T(8,128)(2,1)} custom-call(bf16[1280,128]{1,0:T(8,128)(2,1)S(1)} %bitcast.24), custom_call_target="tpu_custom_call" | custom-call | tf_op jit(solution)/shard_map/sum_pieces/pallas_call | solution.py:319
  45.4 4.4 %all-to-all-start.1 = ((bf16[128,5,2,128]{3,2,1,0:T(2,128)(2,1)}), bf16[128,5,2,128]{3,2,1,0:T(2,128)(2,1)S(1)}, u32[]{:S(2)}, u32[]{:S(2)}) async-start(bf16[128,5,2,128]{3,2,1,0:T(2,128)(2,1)} %bitcast.16), calls=%async_computation.1 | async-start | bytes 655360 | tf_op jit(solution)/shard_map/all_to_all | solution.py:479
  49.9 0.0 collective-permute-done.4
  49.9 0.0 collective-permute-done.5
  49.9 0.1 convert_add_fusion
  50.0 0.7 %collective-permute-start.7 = (bf16[64,640]{1,0:T(8,128)(2,1)S(1)}, bf16[64,640]{1,0:T(8,128)(2,1)S(1)}, u32[]{:S(2)}, u32[]{:S(2)}) collective-permute-start(bf16[64,640]{1,0:T(8,128)(2,1)S(1)} %get-tuple-element.74), channel_id=1, source_target_pairs={{8,16},{24,32},{40,48},{56,64},{72,80},{88,96},{104,112},{16,8},{3... | collective-permute-start | bytes 245768 | tf_op jit(solution)/shard_map/ppermute | solution.py:448
  50.7 3.9 %collective-permute-start.6 = (bf16[64,640]{1,0:T(8,128)(2,1)S(1)}, bf16[64,640]{1,0:T(8,128)(2,1)S(1)}, u32[]{:S(2)}, u32[]{:S(2)}) collective-permute-start(bf16[64,640]{1,0:T(8,128)(2,1)S(1)} %get-tuple-element.75), channel_id=1, source_target_pairs={{0,8},{16,24},{32,40},{48,56},{64,72},{80,88},{96,104},{112,120},{... | collective-permute-start | bytes 245768 | tf_op jit(solution)/shard_map/ppermute | solution.py:448
  54.6 1.6 %local_scatter_blocks.1.gfeat_i = bf16[64,2048]{1,0:T(8,128)(2,1)} custom-call(s32[27,1,2048]{2,1,0:T(1,128)S(1)} %get-tuple-element.40.rows, s32[27,1,2048]{2,1,0:T(1,128)S(1)} %get-tuple-element.41.frm, s32[2,2048]{1,0:T(2,128)S(1)} %get-tuple-element.42.dmap, bf16[64,2048]{1,0:T(8,128)(2,1)S(1)} %get-tuple-element.63.gpre, ...), custom_call_target="tpu_custom_call" | custom-call | tf_op jit(solution)/shard_map/local_scatter_blocks/pallas_call | solution.py:269
  56.2 0.0 collective-permute-done.7.right
  56.2 2.2 %collective-permute-done.6.left = bf16[64,640]{1,0:T(8,128)(2,1)S(1)} collective-permute-done((bf16[64,640]{1,0:T(8,128)(2,1)S(1)}, bf16[64,640]{1,0:T(8,128)(2,1)S(1)}, u32[]{:S(2)}, u32[]{:S(2)}) %collective-permute-start.6) | collective-permute-done | bytes 81952 | tf_op jit(solution)/shard_map/ppermute | solution.py:448
  58.4 0.7 %add_incoming.1 = (bf16[64,512]{1,0:T(8,128)(2,1)}, bf16[64,2048]{1,0:T(8,128)(2,1)}) custom-call(bf16[64,512]{1,0:T(8,128)(2,1)S(1)} %get-tuple-element.52.coarse_i, bf16[64,2048]{1,0:T(8,128)(2,1)} %local_scatter_blocks.1.gfeat_i, f32[64,128]{1,0:T(8,128)S(1)} %get-tuple-element.64.coarse, ...), custom_call_target="tpu_custom_call", output_to_operand_aliasing={{1}: (1, {})} | custom-call | tf_op jit(solution)/shard_map/add_incoming/pallas_call | solution.py:409
  59.1 2.6 %all-to-all-done.1 = bf16[128,5,2,128]{3,2,1,0:T(2,128)(2,1)S(1)} async-done(((bf16[128,5,2,128]{3,2,1,0:T(2,128)(2,1)}), bf16[128,5,2,128]{3,2,1,0:T(2,128)(2,1)S(1)}, u32[]{:S(2)}, u32[]{:S(2)}) %all-to-all-start.1) | async-done | bytes 327712 | tf_op jit(solution)/shard_map/all_to_all | solution.py:479
  61.7 1.2 %unpack_weights.1 = (f32[27,64,64]{2,1,0:T(8,128)}, f32[8,64,64]{2,1,0:T(8,128)}) custom-call(bf16[1280,128]{1,0:T(8,128)(2,1)S(1)} %bitcast.23), custom_call_target="tpu_custom_call" | custom-call | tf_op jit(solution)/shard_map/unpack_weights/pallas_call | solution.py:434
  (4 shorter events, 0.1 us)
Async XLA Ops:
  1.5 7.0 %collective-permute-start.1 = (bf16[64,640]{1,0:T(8,128)(2,1)S(1)}, bf16[64,640]{1,0:T(8,128)(2,1)S(1)}, u32[]{:S(2)}, u32[]{:S(2)}) collective-permute-start(bf16[64,640]{1,0:T(8,128)(2,1)S(1)} %pack_border.1), channel_id=1, source_target_pairs={{8,16},{24,32},{40,48},{56,64},{72,80},{88,96},{104,112},{16,8},{3... | collective-permute-start | bytes 245768 | tf_op jit(solution)/shard_map/ppermute | solution.py:448
  2.2 6.6 %collective-permute-start = (bf16[64,640]{1,0:T(8,128)(2,1)S(1)}, bf16[64,640]{1,0:T(8,128)(2,1)S(1)}, u32[]{:S(2)}, u32[]{:S(2)}) collective-permute-start(bf16[64,640]{1,0:T(8,128)(2,1)S(1)} %pack_border.1), channel_id=1, source_target_pairs={{0,8},{16,24},{32,40},{48,56},{64,72},{80,88},{96,104},{112,120},{... | collective-permute-start | bytes 245768 | tf_op jit(solution)/shard_map/ppermute | solution.py:448
  8.8 8.7 %collective-permute-start.3 = (bf16[3,64,640]{2,1,0:T(8,128)(2,1)S(1)}, bf16[3,64,640]{2,1,0:T(8,128)(2,1)S(1)}, u32[]{:S(2)}, u32[]{:S(2)}) collective-permute-start(bf16[3,64,640]{2,1,0:T(8,128)(2,1)S(1)} %pad_maximum_fusion.column), channel_id=1, source_target_pairs={{1,2},{3,4},{5,6},{2,1},{4,3},{6,5},{9,10},{11,12},{13,14},{10,9},... | collective-permute-start | bytes 737288 | tf_op jit(solution)/shard_map/ppermute | solution.py:448
  13.7 3.9 %collective-permute-start.2 = (bf16[3,64,640]{2,1,0:T(8,128)(2,1)S(1)}, bf16[3,64,640]{2,1,0:T(8,128)(2,1)S(1)}, u32[]{:S(2)}, u32[]{:S(2)}) collective-permute-start(bf16[3,64,640]{2,1,0:T(8,128)(2,1)S(1)} %pad_maximum_fusion.column), channel_id=1, source_target_pairs={{0,1},{2,3},{4,5},{6,7},{1,0},{3,2},{5,4},{7,6},{8,9},{10,11},{12,... | collective-permute-start | bytes 737288 | tf_op jit(solution)/shard_map/ppermute | solution.py:448
  21.6 23.0 %all-to-all-start = ((bf16[128,5,2,128]{3,2,1,0:T(2,128)(2,1)}), bf16[128,5,2,128]{3,2,1,0:T(2,128)(2,1)S(1)}, u32[]{:S(2)}, u32[]{:S(2)}) async-start(bf16[128,5,2,128]{3,2,1,0:T(2,128)(2,1)} %bitcast.9), calls=%async_computation | async-start | bytes 655360 | tf_op jit(solution)/shard_map/all_to_all | solution.py:470
  35.9 14.0 %collective-permute-start.4 = (bf16[3,64,640]{2,1,0:T(8,128)(2,1)S(1)}, bf16[3,64,640]{2,1,0:T(8,128)(2,1)S(1)}, u32[]{:S(2)}, u32[]{:S(2)}) collective-permute-start(bf16[3,64,640]{2,1,0:T(8,128)(2,1)S(1)} %get-tuple-element.67), channel_id=1, source_target_pairs={{0,1},{2,3},{4,5},{6,7},{1,0},{3,2},{5,4},{7,6},{8,9},{10,11},{12,... | collective-permute-start | bytes 737288 | tf_op jit(solution)/shard_map/ppermute | solution.py:448
  37.2 12.7 %collective-permute-start.5 = (bf16[3,64,640]{2,1,0:T(8,128)(2,1)S(1)}, bf16[3,64,640]{2,1,0:T(8,128)(2,1)S(1)}, u32[]{:S(2)}, u32[]{:S(2)}) collective-permute-start(bf16[3,64,640]{2,1,0:T(8,128)(2,1)S(1)} %get-tuple-element.68), channel_id=1, source_target_pairs={{1,2},{3,4},{5,6},{2,1},{4,3},{6,5},{9,10},{11,12},{13,14},{10,9},... | collective-permute-start | bytes 737288 | tf_op jit(solution)/shard_map/ppermute | solution.py:448
  45.4 16.2 %all-to-all-start.1 = ((bf16[128,5,2,128]{3,2,1,0:T(2,128)(2,1)}), bf16[128,5,2,128]{3,2,1,0:T(2,128)(2,1)S(1)}, u32[]{:S(2)}, u32[]{:S(2)}) async-start(bf16[128,5,2,128]{3,2,1,0:T(2,128)(2,1)} %bitcast.16), calls=%async_computation.1 | async-start | bytes 655360 | tf_op jit(solution)/shard_map/all_to_all | solution.py:479
  50.0 6.2 %collective-permute-start.7 = (bf16[64,640]{1,0:T(8,128)(2,1)S(1)}, bf16[64,640]{1,0:T(8,128)(2,1)S(1)}, u32[]{:S(2)}, u32[]{:S(2)}) collective-permute-start(bf16[64,640]{1,0:T(8,128)(2,1)S(1)} %get-tuple-element.74), channel_id=1, source_target_pairs={{8,16},{24,32},{40,48},{56,64},{72,80},{88,96},{104,112},{16,8},{3... | collective-permute-start | bytes 245768 | tf_op jit(solution)/shard_map/ppermute | solution.py:448
  50.7 7.7 %collective-permute-start.6 = (bf16[64,640]{1,0:T(8,128)(2,1)S(1)}, bf16[64,640]{1,0:T(8,128)(2,1)S(1)}, u32[]{:S(2)}, u32[]{:S(2)}) collective-permute-start(bf16[64,640]{1,0:T(8,128)(2,1)S(1)} %get-tuple-element.75), channel_id=1, source_target_pairs={{0,8},{16,24},{32,40},{48,56},{64,72},{80,88},{96,104},{112,120},{... | collective-permute-start | bytes 245768 | tf_op jit(solution)/shard_map/ppermute | solution.py:448

commit v10 on v9

--- a/solution.py
+++ b/solution.py
@@ -91,13 +91,20 @@
     grad_pre = (grad_hidden * sig * (1.0 + pre * (1.0 - sig))).astype(BF)
     grad_sub = mm_nt(grad_pre, source[...])
     grad_down = mm_nt(picked_g, hidden)
-    picked_h = jnp.concatenate([jnp.where(m, hidden, zero) for m in kinds], axis=0)
+    if remote:
+        return hidden, grad_pre, grad_sub, grad_down
+    coarse, _ = down_convolution(hidden, kinds, pick_own, wd_cat)
+    return coarse, grad_pre, grad_sub, grad_down
+
+
+def down_convolution(hidden, kinds, pick_own, wd_cat):
+    picked_h = jnp.concatenate([jnp.where(m, hidden, jnp.zeros((), BF)) for m in kinds], axis=0)
     contrib = mm(wd_cat[...], picked_h)
     c_hi = contrib.astype(BF)
     c_lo = (contrib - c_hi.astype(F32)).astype(BF)
     split = jnp.concatenate([c_hi, c_lo], axis=0)
     own = mm_nt(split, pick_own)
-    return own[:C] + own[C:], grad_pre, grad_sub, grad_down, split
+    return own[:C] + own[C:], split
 
 
 def pick_edges(target):
@@ -139,7 +146,7 @@
 
     @pl.when(live)
     def _():
-        coarse, gpre, gsub, gdown, _ = forward_work(
+        coarse, gpre, gsub, gdown = forward_work(
             False, block * VB, feat, rows, frm, dmap, grad, None, w_cat, wd_cat, wd_t, source)
         coarse_o[...] = coarse.astype(BF)
         gpre_o[...] = gpre
@@ -328,16 +335,15 @@
 
 
 def border_kernel(side, feat, rows, frm, dmap, grad, near, column, far, w_cat, wd_cat, wd_t, gsub, gdown,
-                  coarse_o, packed_o, gpre_o, split_o, source, below, above):
+                  packed_o, gpre_o, hidden_o, source, below, above):
     feat, rows, frm, dmap, grad = views(0, feat, rows, frm, dmap, grad)
     even = side[0] == 1
     below[...] = jnp.where(even, far[...], near[...])
     above[...] = jnp.where(even, near[...], far[...])
-    coarse, gpre, dsub, ddown, split = forward_work(
+    hidden, gpre, dsub, ddown = forward_work(
         True, 0, feat, rows, frm, dmap, grad, (below, column, above), w_cat, wd_cat, wd_t, source)
-    coarse_o[...] = coarse
     gpre_o[...] = gpre
-    split_o[...] = split
+    hidden_o[...] = hidden
     total = gsub[...] + dsub
     for t in range(K // 2):
         packed_o[t * C:(t + 1) * C, :] = total[:, t * 2 * C:(t + 1) * 2 * C].astype(BF)
@@ -355,17 +361,21 @@
         grid=(1,),
         in_specs=[SCALAR] + [WHOLE] * 5 + [slab, slab, slab, full((C, KC)), full((C, 8 * C)), full((C, 8 * C)),
                                    full((C, KC)), full((8 * C, C))],
-        out_specs=[full((C, CQ)), piped((count * PIECE, 2 * C)), full((C, VB)), full((2 * C, VB))],
-        out_shape=[sd((C, CQ), F32), sd((count * PIECE, 2 * C), BF), sd((C, VB), BF), sd((2 * C, VB), BF)],
+        out_specs=[piped((count * PIECE, 2 * C)), full((C, VB)), full((C, VB))],
+        out_shape=[sd((count * PIECE, 2 * C), BF), sd((C, VB), BF), sd((C, VB), BF)],
         scratch_shapes=[SOURCE, pltpu.VMEM((3, C, WIDE), BF), pltpu.VMEM((3, C, WIDE), BF)],
         compiler_params=LIMIT,
         name="border_block",
     )(side, feat, rows, frm, dmap, grad, near, column, far, w_cat, wd_cat, wd_t, gsub, gdown)
 
 
-def border_scatter_kernel(side, rows, frm, dmap, gpre, split, w_t, gfeat_o, mid_o, near_o, far_o, spread):
+def border_scatter_kernel(side, rows, frm, dmap, gpre, hidden, w_t, wd_cat, coarse_o, gfeat_o, mid_o, near_o, far_o, spread):
     gfeat_o[...] = scatter_work(True, 0, rows.at[:, :, 0:VB], frm.at[:, :, 0:VB], gpre[...], w_t, spread)
-    both = mm_nt(split[...], pick_edges(dmap[0:1, 0:VB]))
+    target = dmap[0:1, 0:VB]
+    kinds = [dmap[1:2, 0:VB] == i for i in range(8)]
+    pick_own = pick(target == lax.broadcasted_iota(jnp.int32, (CQ, VB), 0))
+    coarse_o[...], split = down_convolution(hidden[...], kinds, pick_own, wd_cat)
+    both = mm_nt(split, pick_edges(target))
     edge = both[:C] + both[C:]
     even = side[0] == 1
 
@@ -382,19 +392,18 @@
         far_o[x] = jnp.where(even, down, up)
 
 
-def border_scatter_call(side, rows, frm, dmap, gpre, split, w_t):
+def border_scatter_call(side, rows, frm, dmap, gpre, hidden, w_t, wd_cat):
     slab = (3, C, WIDE)
     return pl.pallas_call(
         border_scatter_kernel,
         grid=(1,),
-        in_specs=[SCALAR, WHOLE, WHOLE, WHOLE, full((C, VB)), full((2 * C, VB)),
-                  full((C, KC))],
-        out_specs=[full((C, VB)), full(slab), full(slab), full(slab)],
-        out_shape=[sd((C, VB), F32), sd(slab, F32), sd(slab, BF), sd(slab, BF)],
+        in_specs=[SCALAR] + [WHOLE] * 7,
+        out_specs=[WHOLE] * 5,
+        out_shape=[sd((C, CQ), F32), sd((C, VB), F32), sd(slab, F32), sd(slab, BF), sd(slab, BF)],
         scratch_shapes=[pltpu.VMEM((KC, 2 * VB), BF)],
         compiler_params=LIMIT,
         name="border_scatter_block",
-    )(side, rows, frm, dmap, gpre, split, w_t)
+    )(side, rows, frm, dmap, gpre, hidden, w_t, wd_cat)
 
 
 def finish_kernel(coarse_i, gfeat_i, coarse, gfeat, total, left, right, coarse_o, gfeat_o):
@@ -465,10 +474,11 @@
     near, far = swapped(column, "gy", True), swapped(column, "gy", False)
     coarse_all, gpre_all, gsub, gdown = rest_call(
         feat, rows, frm, dmap, grad, w_cat, wd_cat, wd_t, gsub, gdown, coarse_all, gpre_all)
-    coarse, packed, gpre, split = border_call(
+    packed, gpre, hidden = border_call(
         count, side, feat, rows, frm, dmap, grad, near, column, far, w_cat, wd_cat, wd_t, gsub, gdown)
     pieces = lax.all_to_all(packed.reshape(count, PAIRS, 2, 2 * C), ("gx", "gy"), 0, 0, tiled=True)
-    gfeat, mid, out_near, out_far = border_scatter_call(side, rows, frm, dmap, gpre, split, w_t)
+    coarse, gfeat, mid, out_near, out_far = border_scatter_call(
+        side, rows, frm, dmap, gpre, hidden, w_t, wd_cat)
     near, far = swapped(out_near, "gy", True), swapped(out_far, "gy", False)
     shape = pieces.shape
     spread = sum_call(pieces.reshape(count * PIECE, 2 * C))

time: 63.3 us -> 64.8 us (1.024)
  Pallas kernels: 14 us -> 22.3 us
  waiting for transfers between devices: 13.5 us -> 9.22 us
  starting transfers between devices: 34.4 us -> 30.3 us
  other arithmetic: 0.16 us -> 1.1 us
    ppermute x8, starting transfers between devices: 18.6 us -> 12.6 us  [swapped(): return lax.ppermute(block, axis, pairs + [(b, a) for a, b in pairs])]
    ppermute x8, waiting for transfers between devices: 5.97 us -> 1.17 us  [swapped(): return lax.ppermute(block, axis, pairs + [(b, a) for a, b in pairs])]
    pallas_call x1, Pallas kernels: 1.58 us -> 4.77 us  [local_scatter_call(): pl.pallas_call(local_scatter_kernel, grid=(3,), in_specs=[WHOLE] * 5, out...]
    pallas_call x1, Pallas kernels: 1.58 us -> 4.05 us  [first_call(): pl.pallas_call(first_kernel, in_specs=[pl.BlockSpec(memory_space=pltpu.HB...]
    pallas_call x1, Pallas kernels: 0.24 us -> 2.68 us  [rest_call(): pl.pallas_call(rest_kernel, in_specs=[WHOLE] * 12, out_specs=[WHOLE] * 4,...]
    all_to_all x1, starting transfers between devices: 11.3 us -> 13.2 us  [shards(): lax.all_to_all(packed.reshape(count, PAIRS, 2, 2 * C), ('gx', 'gy'), 0, 0...]
    add x1, other arithmetic: 0.07 us -> 1.01 us  [shards(): total = mid + near.astype(F32) + far.astype(F32)]
  transfers between devices with their start and end apart: 10 -> 10, of which waited for: 5 -> 3; matrix products, arithmetic and copies ran while one was open for 0% -> 2% of each run, Pallas kernels for 12% -> 25%
where the time goes in v10:
time: 64.8 us; the launch traced here: 63.8 us
  starting transfers between devices  30.3 us (47%)
  Pallas kernels  22.3 us (34%)
  waiting for transfers between devices  9.22 us (14%)
  other arithmetic  1.1 us (2%)
  between operations  0.82 us (1%)
    all_to_all x1, starting transfers between devices, shards(): lax.all_to_all(packed.reshape(count, PAIRS, 2, 2 * C), ('gx', 'gy'), 0, 0...  13.2 us
    ppermute x8, starting transfers between devices, swapped(): return lax.ppermute(block, axis, pairs + [(b, a) for a, b in pairs])  12.6 us
    all_to_all x1, waiting for transfers between devices, shards(): lax.all_to_all(packed.reshape(count, PAIRS, 2, 2 * C), ('gx', 'gy'), 0, 0...  4.98 us
    pallas_call x1, Pallas kernels, local_scatter_call(): pl.pallas_call(local_scatter_kernel, grid=(3,), in_specs=[WHOLE] * 5, out...  4.77 us
    all_to_all x1, starting transfers between devices, shards(): lax.all_to_all(spread.reshape(shape), ('gx', 'gy'), 0, 0, tiled=True)  4.44 us
    pallas_call x1, Pallas kernels, border_call(): pl.pallas_call(border_kernel, grid=(1,), in_specs=[SCALAR] + [WHOLE] * 5...  4.17 us
    pallas_call x1, Pallas kernels, first_call(): pl.pallas_call(first_kernel, in_specs=[pl.BlockSpec(memory_space=pltpu.HB...  4.05 us
    pallas_call x1, Pallas kernels, border_scatter_call(): pl.pallas_call(border_scatter_kernel, grid=(1,), in_specs=[SCALAR] + [WHO...  3.13 us
  transfers between devices with their start and end apart: 10, of which 3 were waited for; matrix products, arithmetic and copies ran while one was open for 2% of the time, Pallas kernels for 25%

profile of v10, /device:TPU:1, one launch (start us, length us, event | category | flops | bytes accessed | tf_op | source)
XLA Modules:
  0.0 63.8 jit_solution(1593653517052304002)
XLA Ops:
  0.6 0.9 %pack_border.1 = bf16[64,640]{1,0:T(8,128)(2,1)S(1)} custom-call(bf16[64,2048]{1,0:T(8,128)(2,1)} %bitcast.27, bf16[64,512]{1,0:T(8,128)(2,1)} %bitcast.29), custom_call_target="tpu_custom_call" | custom-call | tf_op jit(solution)/shard_map/pack_border/pallas_call | solution.py:302
  1.5 2.2 %collective-permute-start = (bf16[64,640]{1,0:T(8,128)(2,1)S(1)}, bf16[64,640]{1,0:T(8,128)(2,1)S(1)}, u32[]{:S(2)}, u32[]{:S(2)}) collective-permute-start(bf16[64,640]{1,0:T(8,128)(2,1)S(1)} %pack_border.1), channel_id=1, source_target_pairs={{0,8},{16,24},{32,40},{48,56},{64,72},{80,88},{96,104},{112,120},{... | collective-permute-start | bytes 245768 | tf_op jit(solution)/shard_map/ppermute | solution.py:457
  3.7 0.7 %collective-permute-start.1 = (bf16[64,640]{1,0:T(8,128)(2,1)S(1)}, bf16[64,640]{1,0:T(8,128)(2,1)S(1)}, u32[]{:S(2)}, u32[]{:S(2)}) collective-permute-start(bf16[64,640]{1,0:T(8,128)(2,1)S(1)} %pack_border.1), channel_id=1, source_target_pairs={{8,16},{24,32},{40,48},{56,64},{72,80},{88,96},{104,112},{16,8},{3... | collective-permute-start | bytes 245768 | tf_op jit(solution)/shard_map/ppermute | solution.py:457
  4.4 4.1 %first_local_block.1 = (bf16[64,512]{1,0:T(8,128)(2,1)S(1)}, bf16[64,2048]{1,0:T(8,128)(2,1)S(1)}, f32[64,1728]{1,0:T(8,128)S(1)}, f32[512,64]{1,0:T(8,128)S(1)}...) custom-call(bf16[64,2048]{1,0:T(8,128)(2,1)} %bitcast.28, ...), custom_call_target="tpu_custom_call" | custom-call | tf_op jit(solution)/shard_map/first_local_block/pallas_call | solution.py:250
  8.4 0.0 collective-permute-done
  8.4 0.0 collective-permute-done.1
  8.5 0.1 collective-permute-start.2
  8.6 4.0 %collective-permute-start.3 = (bf16[3,64,640]{2,1,0:T(8,128)(2,1)S(1)}, bf16[3,64,640]{2,1,0:T(8,128)(2,1)S(1)}, u32[]{:S(2)}, u32[]{:S(2)}) collective-permute-start(bf16[3,64,640]{2,1,0:T(8,128)(2,1)S(1)} %pad_maximum_fusion.column), channel_id=1, source_target_pairs={{1,2},{3,4},{5,6},{2,1},{4,3},{6,5},{9,10},{11,12},{13,14},{10,9},... | collective-permute-start | bytes 737288 | tf_op jit(solution)/shard_map/ppermute | solution.py:457
  12.6 2.7 %other_local_blocks.1 = (bf16[64,512]{1,0:T(8,128)(2,1)S(1)}, bf16[64,2048]{1,0:T(8,128)(2,1)S(1)}, f32[64,1728]{1,0:T(8,128)S(1)}, f32[512,64]{1,0:T(8,128)S(1)}) custom-call(bf16[64,2048]{1,0:T(8,128)(2,1)S(1)} %get-tuple-element.39.feat, ...), custom_call_target="tpu_custom_call", output_to_operand_aliasing={{0}: (10, {}), {1}: (11, {}), {2}: (8, {}), {3}: (9, {})} | custom-call | tf_op jit(solution)/shard_map/other_local_blocks/pallas_call | solution.py:263
  15.3 0.0 collective-permute-done.2.near
  15.3 1.2 %collective-permute-done.3.far = bf16[3,64,640]{2,1,0:T(8,128)(2,1)S(1)} collective-permute-done((bf16[3,64,640]{2,1,0:T(8,128)(2,1)S(1)}, bf16[3,64,640]{2,1,0:T(8,128)(2,1)S(1)}, u32[]{:S(2)}, u32[]{:S(2)}) %collective-permute-start.3) | collective-permute-done | bytes 245792 | tf_op jit(solution)/shard_map/ppermute | solution.py:457
  16.5 4.2 %border_block.1 = (bf16[1280,128]{1,0:T(8,128)(2,1)}, bf16[64,512]{1,0:T(8,128)(2,1)S(1)}, bf16[64,512]{1,0:T(8,128)(2,1)S(1)}) custom-call(s32[1]{0:T(128)} %bitcast.5.side, bf16[64,2048]{1,0:T(8,128)(2,1)S(1)} %get-tuple-element.39.feat, s32[27,1,2048]{2,1,0:T(1,128)S(1)} %get-tuple-element.40.rows, s32[27,1,2048]{2,1,0:T(1,128)S(1)} %get-tuple-element.41.frm, ...), custom_call_target="tpu_custom_call" | custom-call | tf_op jit(solution)/shard_map/border_block/pallas_call | solution.py:359
  20.6 13.2 %all-to-all-start = ((bf16[128,5,2,128]{3,2,1,0:T(2,128)(2,1)}), bf16[128,5,2,128]{3,2,1,0:T(2,128)(2,1)S(1)}, u32[]{:S(2)}, u32[]{:S(2)}) async-start(bf16[128,5,2,128]{3,2,1,0:T(2,128)(2,1)} %bitcast.9), calls=%async_computation | async-start | bytes 655360 | tf_op jit(solution)/shard_map/all_to_all | solution.py:479
  33.9 3.1 %border_scatter_block.1 = (f32[64,128]{1,0:T(8,128)S(1)}, f32[64,512]{1,0:T(8,128)S(1)}, f32[3,64,640]{2,1,0:T(8,128)S(1)}, bf16[3,64,640]{2,1,0:T(8,128)(2,1)S(1)}, bf16[3,64,640]{2,1,0:T(8,128)(2,1)S(1)}) custom-call(s32[1]{0:T(128)} %bitcast.5.side, s32[27,1,2048]{2,1,0:T(1,128)S(1)} %get-tuple-element.40.rows, s32[27,1,2048]{2,1,0:T(1,128)S(1)} %get-tuple-element.41.frm, ...), custom_call_target="tpu_custom_call" | custom-call | tf_op jit(solution)/shard_map/border_scatter_block/pallas_call | solution.py:397
  37.0 3.5 %collective-permute-start.5 = (bf16[3,64,640]{2,1,0:T(8,128)(2,1)S(1)}, bf16[3,64,640]{2,1,0:T(8,128)(2,1)S(1)}, u32[]{:S(2)}, u32[]{:S(2)}) collective-permute-start(bf16[3,64,640]{2,1,0:T(8,128)(2,1)S(1)} %get-tuple-element.68), channel_id=1, source_target_pairs={{1,2},{3,4},{5,6},{2,1},{4,3},{6,5},{9,10},{11,12},{13,14},{10,9},... | collective-permute-start | bytes 737288 | tf_op jit(solution)/shard_map/ppermute | solution.py:457
  40.5 0.1 collective-permute-start.4
  40.6 5.0 %all-to-all-done = bf16[128,5,2,128]{3,2,1,0:T(2,128)(2,1)S(1)} async-done(((bf16[128,5,2,128]{3,2,1,0:T(2,128)(2,1)}), bf16[128,5,2,128]{3,2,1,0:T(2,128)(2,1)S(1)}, u32[]{:S(2)}, u32[]{:S(2)}) %all-to-all-start) | async-done | bytes 327712 | tf_op jit(solution)/shard_map/all_to_all | solution.py:479
  45.6 0.8 %sum_pieces.1 = bf16[1280,128]{1,0:T(8,128)(2,1)} custom-call(bf16[1280,128]{1,0:T(8,128)(2,1)S(1)} %bitcast.24), custom_call_target="tpu_custom_call" | custom-call | tf_op jit(solution)/shard_map/sum_pieces/pallas_call | solution.py:326
  46.4 4.4 %all-to-all-start.1 = ((bf16[128,5,2,128]{3,2,1,0:T(2,128)(2,1)}), bf16[128,5,2,128]{3,2,1,0:T(2,128)(2,1)S(1)}, u32[]{:S(2)}, u32[]{:S(2)}) async-start(bf16[128,5,2,128]{3,2,1,0:T(2,128)(2,1)} %bitcast.16), calls=%async_computation.1 | async-start | bytes 655360 | tf_op jit(solution)/shard_map/all_to_all | solution.py:489
  50.9 0.0 collective-permute-done.5
  50.9 0.0 collective-permute-done.4
  50.9 1.0 %convert_add_fusion = f32[3,64,640]{2,1,0:T(8,128)S(1)} fusion(bf16[3,64,640]{2,1,0:T(8,128)(2,1)S(1)} %collective-permute-done.5, f32[3,64,640]{2,1,0:T(8,128)S(1)} %get-tuple-element.66, bf16[3,64,640]{2,1,0:T(8,128)(2,1)} %collective-permute-done.4), kind=kLoop, calls=%fused_computation | loop fusion | flops 491520 | bytes 1474560 | tf_op jit(solution)/shard_map/add | solution.py:486
  51.9 1.5 %collective-permute-start.6 = (bf16[64,640]{1,0:T(8,128)(2,1)S(1)}, bf16[64,640]{1,0:T(8,128)(2,1)S(1)}, u32[]{:S(2)}, u32[]{:S(2)}) collective-permute-start(bf16[64,640]{1,0:T(8,128)(2,1)S(1)} %get-tuple-element.75), channel_id=1, source_target_pairs={{0,8},{16,24},{32,40},{48,56},{64,72},{80,88},{96,104},{112,120},{... | collective-permute-start | bytes 245768 | tf_op jit(solution)/shard_map/ppermute | solution.py:457
  53.4 0.7 %collective-permute-start.7 = (bf16[64,640]{1,0:T(8,128)(2,1)S(1)}, bf16[64,640]{1,0:T(8,128)(2,1)S(1)}, u32[]{:S(2)}, u32[]{:S(2)}) collective-permute-start(bf16[64,640]{1,0:T(8,128)(2,1)S(1)} %get-tuple-element.74), channel_id=1, source_target_pairs={{8,16},{24,32},{40,48},{56,64},{72,80},{88,96},{104,112},{16,8},{3... | collective-permute-start | bytes 245768 | tf_op jit(solution)/shard_map/ppermute | solution.py:457
  54.1 4.8 %local_scatter_blocks.1.gfeat_i = bf16[64,2048]{1,0:T(8,128)(2,1)} custom-call(s32[27,1,2048]{2,1,0:T(1,128)S(1)} %get-tuple-element.40.rows, s32[27,1,2048]{2,1,0:T(1,128)S(1)} %get-tuple-element.41.frm, s32[2,2048]{1,0:T(2,128)S(1)} %get-tuple-element.42.dmap, bf16[64,2048]{1,0:T(8,128)(2,1)S(1)} %get-tuple-element.63.gpre, ...), custom_call_target="tpu_custom_call" | custom-call | tf_op jit(solution)/shard_map/local_scatter_blocks/pallas_call | solution.py:276
  58.9 0.0 collective-permute-done.6.left
  58.9 0.0 collective-permute-done.7.right
  58.9 0.7 %add_incoming.1 = (bf16[64,512]{1,0:T(8,128)(2,1)}, bf16[64,2048]{1,0:T(8,128)(2,1)}) custom-call(bf16[64,512]{1,0:T(8,128)(2,1)S(1)} %get-tuple-element.52.coarse_i, bf16[64,2048]{1,0:T(8,128)(2,1)} %local_scatter_blocks.1.gfeat_i, f32[64,128]{1,0:T(8,128)S(1)} %get-tuple-element.64.coarse, ...), custom_call_target="tpu_custom_call", output_to_operand_aliasing={{1}: (1, {})} | custom-call | tf_op jit(solution)/shard_map/add_incoming/pallas_call | solution.py:418
  59.5 3.1 %all-to-all-done.1 = bf16[128,5,2,128]{3,2,1,0:T(2,128)(2,1)S(1)} async-done(((bf16[128,5,2,128]{3,2,1,0:T(2,128)(2,1)}), bf16[128,5,2,128]{3,2,1,0:T(2,128)(2,1)S(1)}, u32[]{:S(2)}, u32[]{:S(2)}) %all-to-all-start.1) | async-done | bytes 327712 | tf_op jit(solution)/shard_map/all_to_all | solution.py:489
  62.6 1.2 %unpack_weights.1 = (f32[27,64,64]{2,1,0:T(8,128)}, f32[8,64,64]{2,1,0:T(8,128)}) custom-call(bf16[1280,128]{1,0:T(8,128)(2,1)S(1)} %bitcast.23), custom_call_target="tpu_custom_call" | custom-call | tf_op jit(solution)/shard_map/unpack_weights/pallas_call | solution.py:443
  (4 shorter events, 0.1 us)
Async XLA Ops:
  1.5 6.9 %collective-permute-start = (bf16[64,640]{1,0:T(8,128)(2,1)S(1)}, bf16[64,640]{1,0:T(8,128)(2,1)S(1)}, u32[]{:S(2)}, u32[]{:S(2)}) collective-permute-start(bf16[64,640]{1,0:T(8,128)(2,1)S(1)} %pack_border.1), channel_id=1, source_target_pairs={{0,8},{16,24},{32,40},{48,56},{64,72},{80,88},{96,104},{112,120},{... | collective-permute-start | bytes 245768 | tf_op jit(solution)/shard_map/ppermute | solution.py:457
  3.7 4.7 %collective-permute-start.1 = (bf16[64,640]{1,0:T(8,128)(2,1)S(1)}, bf16[64,640]{1,0:T(8,128)(2,1)S(1)}, u32[]{:S(2)}, u32[]{:S(2)}) collective-permute-start(bf16[64,640]{1,0:T(8,128)(2,1)S(1)} %pack_border.1), channel_id=1, source_target_pairs={{8,16},{24,32},{40,48},{56,64},{72,80},{88,96},{104,112},{16,8},{3... | collective-permute-start | bytes 245768 | tf_op jit(solution)/shard_map/ppermute | solution.py:457
  8.5 6.8 %collective-permute-start.2 = (bf16[3,64,640]{2,1,0:T(8,128)(2,1)S(1)}, bf16[3,64,640]{2,1,0:T(8,128)(2,1)S(1)}, u32[]{:S(2)}, u32[]{:S(2)}) collective-permute-start(bf16[3,64,640]{2,1,0:T(8,128)(2,1)S(1)} %pad_maximum_fusion.column), channel_id=1, source_target_pairs={{0,1},{2,3},{4,5},{6,7},{1,0},{3,2},{5,4},{7,6},{8,9},{10,11},{12,... | collective-permute-start | bytes 737288 | tf_op jit(solution)/shard_map/ppermute | solution.py:457
  8.6 7.8 %collective-permute-start.3 = (bf16[3,64,640]{2,1,0:T(8,128)(2,1)S(1)}, bf16[3,64,640]{2,1,0:T(8,128)(2,1)S(1)}, u32[]{:S(2)}, u32[]{:S(2)}) collective-permute-start(bf16[3,64,640]{2,1,0:T(8,128)(2,1)S(1)} %pad_maximum_fusion.column), channel_id=1, source_target_pairs={{1,2},{3,4},{5,6},{2,1},{4,3},{6,5},{9,10},{11,12},{13,14},{10,9},... | collective-permute-start | bytes 737288 | tf_op jit(solution)/shard_map/ppermute | solution.py:457
  20.6 25.0 %all-to-all-start = ((bf16[128,5,2,128]{3,2,1,0:T(2,128)(2,1)}), bf16[128,5,2,128]{3,2,1,0:T(2,128)(2,1)S(1)}, u32[]{:S(2)}, u32[]{:S(2)}) async-start(bf16[128,5,2,128]{3,2,1,0:T(2,128)(2,1)} %bitcast.9), calls=%async_computation | async-start | bytes 655360 | tf_op jit(solution)/shard_map/all_to_all | solution.py:479
  37.0 13.9 %collective-permute-start.5 = (bf16[3,64,640]{2,1,0:T(8,128)(2,1)S(1)}, bf16[3,64,640]{2,1,0:T(8,128)(2,1)S(1)}, u32[]{:S(2)}, u32[]{:S(2)}) collective-permute-start(bf16[3,64,640]{2,1,0:T(8,128)(2,1)S(1)} %get-tuple-element.68), channel_id=1, source_target_pairs={{1,2},{3,4},{5,6},{2,1},{4,3},{6,5},{9,10},{11,12},{13,14},{10,9},... | collective-permute-start | bytes 737288 | tf_op jit(solution)/shard_map/ppermute | solution.py:457
  40.5 10.3 %collective-permute-start.4 = (bf16[3,64,640]{2,1,0:T(8,128)(2,1)S(1)}, bf16[3,64,640]{2,1,0:T(8,128)(2,1)}, u32[]{:S(2)}, u32[]{:S(2)}) collective-permute-start(bf16[3,64,640]{2,1,0:T(8,128)(2,1)S(1)} %get-tuple-element.67), channel_id=1, source_target_pairs={{0,1},{2,3},{4,5},{6,7},{1,0},{3,2},{5,4},{7,6},{8,9},{10,11},{12,... | collective-permute-start | bytes 737288 | tf_op jit(solution)/shard_map/ppermute | solution.py:457
  46.4 16.2 %all-to-all-start.1 = ((bf16[128,5,2,128]{3,2,1,0:T(2,128)(2,1)}), bf16[128,5,2,128]{3,2,1,0:T(2,128)(2,1)S(1)}, u32[]{:S(2)}, u32[]{:S(2)}) async-start(bf16[128,5,2,128]{3,2,1,0:T(2,128)(2,1)} %bitcast.16), calls=%async_computation.1 | async-start | bytes 655360 | tf_op jit(solution)/shard_map/all_to_all | solution.py:489
  51.9 6.9 %collective-permute-start.6 = (bf16[64,640]{1,0:T(8,128)(2,1)S(1)}, bf16[64,640]{1,0:T(8,128)(2,1)S(1)}, u32[]{:S(2)}, u32[]{:S(2)}) collective-permute-start(bf16[64,640]{1,0:T(8,128)(2,1)S(1)} %get-tuple-element.75), channel_id=1, source_target_pairs={{0,8},{16,24},{32,40},{48,56},{64,72},{80,88},{96,104},{112,120},{... | collective-permute-start | bytes 245768 | tf_op jit(solution)/shard_map/ppermute | solution.py:457
  53.4 5.5 %collective-permute-start.7 = (bf16[64,640]{1,0:T(8,128)(2,1)S(1)}, bf16[64,640]{1,0:T(8,128)(2,1)S(1)}, u32[]{:S(2)}, u32[]{:S(2)}) collective-permute-start(bf16[64,640]{1,0:T(8,128)(2,1)S(1)} %get-tuple-element.74), channel_id=1, source_target_pairs={{8,16},{24,32},{40,48},{56,64},{72,80},{88,96},{104,112},{16,8},{3... | collective-permute-start | bytes 245768 | tf_op jit(solution)/shard_map/ppermute | solution.py:457
